TPU v7x, 256 devices: a whole 4x4x8 slice. The times are simulated.
256 devices in a mesh: ta: 32 (over y, z), gx: 8 (over x, core).
Axes of the slice: x: 4, y: 4, z: 8, core: 2. Of those that a mesh axis runs over, the one named last changes fastest.
Arguments:
- right_side: float32 [256, 64, 64, 128], P('ta', 'gx'), may hold values from -6 to 6
- basis_x: float32 [64, 64], replicated, may hold values from -0.75 to 0.75
- basis_y: float32 [64, 64], replicated, may hold values from -0.75 to 0.75
- basis_z: float32 [128, 128], replicated, may hold values from -0.5 to 0.5
- eig_x: float32 [64], replicated, may hold values from 4 to 21.3248
- eig_y: float32 [64], replicated, may hold values from 4 to 21.3248
- eig_z: float32 [128], replicated, may hold values from 4 to 21.3248
- steps: float32 [256], replicated, may hold values from 0.25 to 1
Outputs:
- preconditioned: float32 [256, 64, 64, 128], P('ta', 'gx')
All inputs are finite; a program needn't handle non-finite values.
Results may differ from a plain program's by a relative error of at most 0.00012.
Values sent between devices are 32-bit elements; how exact they have to be, the bound alone decides.
No kernel may reach another device: no remote copies, remote signals or barrier semaphores. Data moves between devices by JAX's collectives and lax.ppermute only.
A program may use at most 192 MiB of HBM per device.

v0:
```python
from functools import partial

import jax
import jax.numpy as jnp
from jax import lax
from jax.sharding import Mesh
from jax.sharding import PartitionSpec as P

TA = ("ta_0", "ta_1")


precise = lax.Precision.HIGHEST


def neutral_like(value, identity):
    return jax.tree.map(
        lambda a, e: jnp.broadcast_to(jnp.asarray(e, a.dtype), a.shape), value, identity
    )


def carried_in(value, axes, combine, identity, reverse):
    before = start = neutral_like(value, identity)
    total = value
    for axis in reversed(axes):
        count, mine = (lax.axis_size(axis), lax.axis_index(axis))
        pieces = jax.tree.map(lambda part: lax.all_gather(part, axis), total)
        inside, total = (start, start)
        for k in reversed(range(count)) if reverse else range(count):
            passed = k > mine if reverse else k < mine
            total = combine(total, jax.tree.map(lambda part: part[k], pieces))
            inside = jax.tree.map(lambda new, old: jnp.where(passed, new, old), total, inside)
        before = combine(inside, before)
    return before


def forward_yz(volume, basis_y, basis_z):
    halfway = jnp.einsum("tabc,cl->tabl", volume, basis_z, precision=precise)
    return jnp.einsum("tabc,bj->tajc", halfway, basis_y, precision=precise)


def backward_yz(volume, basis_y, basis_z):
    halfway = jnp.einsum("tajl,cl->tajc", volume, basis_z, precision=precise)
    return jnp.einsum("tajc,bj->tabc", halfway, basis_y, precision=precise)


def compose_affine(earlier, latter):
    return (latter[0] * earlier[0], latter[0] * earlier[1] + latter[1])


def compose_matrix(earlier, latter, degree):
    entries = []
    for row_at in range(degree):
        for col_at in range(degree):
            entries.append(
                sum(
                    (
                        latter[degree * row_at + inner_at] * earlier[degree * inner_at + col_at]
                        for inner_at in range(degree)
                    )
                )
            )
    factor = 1.0 / sum((jnp.abs(element) for element in entries))
    return tuple((element * factor for element in entries))


def local(right_side, basis_x, basis_y, basis_z, eig_x, eig_y, eig_z, steps):
    local_rows = right_side.shape[0]
    member = lax.axis_index("gx")
    chain_pos = lax.axis_index(TA)
    volume = forward_yz(right_side, basis_y, basis_z)
    spectral = jnp.einsum(
        "tabc,ai->tibc",
        lax.all_to_all(volume, "gx", split_axis=2, concat_axis=1, tiled=True),
        basis_x,
        precision=precise,
    )
    span_y = spectral.shape[2]
    part_y = lax.dynamic_slice_in_dim(eig_y, member * span_y, span_y)
    eigen_sum = eig_x[:, None, None] + part_y[None, :, None] + eig_z[None, None, :]
    total_rows = steps.shape[0]
    lengths = steps / total_rows
    padded = jnp.concatenate([lengths, jnp.zeros((1,), lengths.dtype)])
    first_row = chain_pos * local_rows
    current = lax.dynamic_slice_in_dim(padded, first_row, local_rows)
    following = lax.dynamic_slice_in_dim(padded, first_row + 1, local_rows)
    closing = jnp.where(
        first_row + jnp.arange(local_rows, dtype=jnp.int32) == total_rows - 1, 0.5, 0.0
    ).astype(lengths.dtype)
    all_ones = jnp.ones_like(eigen_sum)
    all_zeros = jnp.zeros_like(eigen_sum)

    def coefficients(cur_len, next_len, close_row):
        main_diag = eigen_sum * ((cur_len + next_len) / 3.0) + close_row
        sub_diag = eigen_sum * (cur_len / 6.0) - 0.5
        coupling = jnp.square(eigen_sum * (cur_len / 6.0)) - 0.25
        return (main_diag, sub_diag, coupling)

    def pivot_product(state_in, inputs):
        main_diag, sub_diag, coupling = coefficients(inputs[0], inputs[1], inputs[2])
        top_left, top_right, low_left, low_right = state_in
        new_left = main_diag * top_left - coupling * low_left
        new_right = main_diag * top_right - coupling * low_right
        factor = 1.0 / (
            jnp.abs(new_left) + jnp.abs(new_right) + jnp.abs(top_left) + jnp.abs(top_right)
        )
        return (
            (new_left * factor, new_right * factor, top_left * factor, top_right * factor),
            None,
        )

    identity = (all_ones, all_zeros, all_zeros, all_ones)
    local_map, unused = lax.scan(pivot_product, identity, (current, following, closing))
    before = carried_in(local_map, TA, partial(compose_matrix, degree=2), identity, False)

    def eliminate(state_in, inputs):
        main_diag, sub_diag, coupling = coefficients(inputs[0], inputs[1], inputs[2])
        prev_top, prev_mid, slope_in, offset = state_in
        new_top = main_diag * prev_top - coupling * prev_mid
        pivot_now = new_top / prev_top
        new_slope = -sub_diag / pivot_now * slope_in
        new_offset = (inputs[3] - sub_diag * offset) / pivot_now
        factor = 1.0 / (jnp.abs(new_top) + jnp.abs(prev_top))
        return (
            (new_top * factor, prev_top * factor, new_slope, new_offset),
            (pivot_now, new_slope, new_offset),
        )

    final_state, (pivots, slopes, offsets) = lax.scan(
        eliminate,
        (before[0], before[2], all_ones, all_zeros),
        (current, following, closing, spectral),
    )
    carried = carried_in(
        (final_state[2], final_state[3]), TA, compose_affine, (all_ones, all_zeros), False
    )
    eliminated = offsets + slopes * carried[1][None]

    def substitute(state_in, inputs):
        next_len, pivot_now, value_now = inputs
        super_diag = eigen_sum * (next_len / 6.0) + 0.5
        ratio_now = super_diag / pivot_now
        new_slope = -ratio_now * state_in[0]
        new_offset = value_now - ratio_now * state_in[1]
        return ((new_slope, new_offset), (new_slope, new_offset))

    first_map, (slopes_back, offsets_back) = lax.scan(
        substitute, (all_ones, all_zeros), (following, pivots, eliminated), reverse=True
    )
    later_carry = carried_in(first_map, TA, compose_affine, (all_ones, all_zeros), True)
    solved = offsets_back + slopes_back * later_carry[1][None]
    cell_field = jnp.einsum("tibc,ai->tabc", solved, basis_x, precision=precise)
    return backward_yz(
        lax.all_to_all(cell_field, "gx", split_axis=1, concat_axis=2, tiled=True), basis_y, basis_z
    )


def solution(mesh):
    finer = Mesh(mesh.devices.reshape(4, 8, mesh.shape["gx"]), ("ta_0", "ta_1", "gx"))
    return jax.shard_map(
        local,
        mesh=finer,
        in_specs=(P(TA, "gx", None, None), P(), P(), P(), P(), P(), P(), P()),
        out_specs=P(TA, "gx", None, None),
        check_vma=False,
    )
```

profile of v0, /device:TPU:1, one launch (start us, length us, event | category | flops | bytes accessed | tf_op | source)
XLA Modules:
  0.0 790.7 jit_solution(15737059283731592769)
XLA Ops:
  8.9 55.6 %while.65 = (s32[]{:T(128)}, f32[64,8,128]{2,1,0:T(8,128)S(1)}, f32[64,8,128]{2,1,0:T(8,128)S(1)}, f32[64,8,128]{2,1,0:T(8,128)S(1)}, f32[64,8,128]{2,1,0:T(8,12...) while((s32[]{:T(128)}, f32[64,8,128]{2,1,0:T(8,128)S(1)}, ...), condition=%wide.region_1.2_spmd.clone, body=%wide.region_0.1_spmd.clone.sunk | while | flops 2883590 | bytes 4199664 | solution.py:112
  67.4 39.3 %all-gather.41.cloned.1.call-done = f32[512,8,128]{2,1,0:T(8,128)} async-done(((f32[64,8,128]{2,1,0:T(8,128)}), f32[512,8,128]{2,1,0:T(8,128)}) %all-gather.41.cloned.1.call-update) | async-done | bytes 2097168 | tf_op jit(solution)/shard_map/all_gather | solution.py:26
  106.6 41.5 %all-gather.43.cloned.1.call-done = f32[512,8,128]{2,1,0:T(8,128)} async-done(((f32[64,8,128]{2,1,0:T(8,128)}), f32[512,8,128]{2,1,0:T(8,128)}) %all-gather.43.cloned.1.call-update) | async-done | bytes 2097168 | tf_op jit(solution)/shard_map/all_gather | solution.py:26
  148.1 41.5 %all-gather.45.cloned.1.call-done = f32[512,8,128]{2,1,0:T(8,128)} async-done(((f32[64,8,128]{2,1,0:T(8,128)}), f32[512,8,128]{2,1,0:T(8,128)}) %all-gather.45.cloned.1.call-update) | async-done | bytes 2097168 | tf_op jit(solution)/shard_map/all_gather | solution.py:26
  189.6 41.3 %all-gather.47.cloned.1.call-done = f32[512,8,128]{2,1,0:T(8,128)} async-done(((f32[64,8,128]{2,1,0:T(8,128)}), f32[512,8,128]{2,1,0:T(8,128)}) %all-gather.47.cloned.1.call-update) | async-done | bytes 2097168 | tf_op jit(solution)/shard_map/all_gather | solution.py:26
  241.0 1.9 fusion.126
  242.9 2.0 convolution_bitcast_fusion.1
  244.9 2.5 copy.28
  247.4 8.8 %all-to-all-start = ((f32[8,8,64,128]{3,1,0,2:T(8,128)}), f32[8,8,64,128]{3,1,0,2:T(8,128)S(1)}, u32[]{:S(2)}, u32[]{:S(2)}) async-start(f32[8,8,64,128]{3,1,0,2:T(8,128)} %copy.28), calls=%async_computation | async-start | bytes 4194304 | tf_op jit(solution)/shard_map/all_to_all | solution.py:73
  257.2 25.3 %all-to-all-done = f32[8,8,64,128]{3,1,0,2:T(8,128)S(1)} async-done(((f32[8,8,64,128]{3,1,0,2:T(8,128)}), f32[8,8,64,128]{3,1,0,2:T(8,128)S(1)}, u32[]{:S(2)}, u32[]{:S(2)}) %all-to-all-start) | async-done | bytes 2097184 | tf_op jit(solution)/shard_map/all_to_all | solution.py:73
  283.9 5.0 fusion.46
  288.8 5.1 add_divide_fusion.16
  294.0 2.2 all-gather.27.cloned.1.call-done
  296.2 28.7 %all-gather.31.cloned.1.call-done = f32[4,64,8,128]{3,2,1,0:T(8,128)} async-done(((f32[1,64,8,128]{3,2,1,0:T(8,128)}), f32[4,64,8,128]{3,2,1,0:T(8,128)}) %all-gather.31.cloned.1.call-update) | async-done | bytes 1048592 | tf_op jit(solution)/shard_map/all_gather | solution.py:26
  324.9 28.7 %all-gather.29.cloned.1.call-done = f32[4,64,8,128]{3,2,1,0:T(8,128)} async-done(((f32[1,64,8,128]{3,2,1,0:T(8,128)}), f32[4,64,8,128]{3,2,1,0:T(8,128)}) %all-gather.29.cloned.1.call-update) | async-done | bytes 1048592 | tf_op jit(solution)/shard_map/all_gather | solution.py:26
  353.8 2.2 multiply_add_fusion.11
  358.2 3.4 fusion.129
  366.3 59.6 %while.66 = (s32[]{:T(128)}, f32[64,8,128]{2,1,0:T(8,128)S(1)}, f32[64,8,128]{2,1,0:T(8,128)S(1)}, f32[64,8,128]{2,1,0:T(8,128)S(1)}, f32[64,8,128]{2,1,0:T(8,12...) while((s32[]{:T(128)}, f32[64,8,128]{2,1,0:T(8,128)S(1)}, ...), condition=%wide.region_3.4_spmd.clone, body=%wide.region_2.3_spmd.clone.sunk | while | flops 2359302 | bytes 4201735 | solution.py:128
  371.1 1.8 bitcast_dynamic-update-slice_fusion.7
  378.5 1.8 bitcast_dynamic-update-slice_fusion.7
  386.0 1.8 bitcast_dynamic-update-slice_fusion.7
  393.4 1.8 bitcast_dynamic-update-slice_fusion.7
  415.8 1.8 bitcast_dynamic-update-slice_fusion.7
  427.3 38.5 %all-gather.49.cloned.1.call-done = f32[512,8,128]{2,1,0:T(8,128)} async-done(((f32[64,8,128]{2,1,0:T(8,128)}), f32[512,8,128]{2,1,0:T(8,128)}) %all-gather.49.cloned.1.call-update) | async-done | bytes 2097168 | tf_op jit(solution)/shard_map/all_gather | solution.py:26
  465.8 41.3 %all-gather.51.cloned.1.call-done = f32[512,8,128]{2,1,0:T(8,128)} async-done(((f32[64,8,128]{2,1,0:T(8,128)}), f32[512,8,128]{2,1,0:T(8,128)}) %all-gather.51.cloned.1.call-update) | async-done | bytes 2097168 | tf_op jit(solution)/shard_map/all_gather | solution.py:26
  507.1 3.1 fusion.65
  511.3 27.0 %all-gather.35.cloned.1.call-done = f32[4,64,8,128]{3,2,1,0:T(8,128)} async-done(((f32[1,64,8,128]{3,2,1,0:T(8,128)}), f32[4,64,8,128]{3,2,1,0:T(8,128)}) %all-gather.35.cloned.1.call-update) | async-done | bytes 1048592 | tf_op jit(solution)/shard_map/all_gather | solution.py:26
  538.3 28.6 %all-gather.33.cloned.1.call-done = f32[4,64,8,128]{3,2,1,0:T(8,128)} async-done(((f32[1,64,8,128]{3,2,1,0:T(8,128)}), f32[4,64,8,128]{3,2,1,0:T(8,128)}) %all-gather.33.cloned.1.call-update) | async-done | bytes 1048592 | tf_op jit(solution)/shard_map/all_gather | solution.py:26
  566.8 2.5 fusion.64
  573.3 26.1 %while.67 = (s32[]{:T(128)}, f32[64,8,128]{2,1,0:T(8,128)S(1)}, f32[64,8,128]{2,1,0:T(8,128)S(1)}, f32[8,64,8,128]{3,2,1,0:T(8,128)S(1)}, f32[8,64,8,128]{3,2,1,...) while((s32[]{:T(128)}, f32[64,8,128]{2,1,0:T(8,128)S(1)}, ...), condition=%wide.region_5.6_spmd.clone, body=%wide.region_4.5_spmd.clone.sunk | while | flops 655365 | bytes 2131127 | solution.py:146
  574.7 1.9 bitcast_dynamic-update-slice_fusion.8
  577.9 1.9 bitcast_dynamic-update-slice_fusion.8
  581.2 1.9 bitcast_dynamic-update-slice_fusion.8
  584.5 1.9 bitcast_dynamic-update-slice_fusion.8
  587.7 1.9 bitcast_dynamic-update-slice_fusion.8
  591.0 1.9 bitcast_dynamic-update-slice_fusion.8
  594.2 1.9 bitcast_dynamic-update-slice_fusion.8
  597.5 1.9 bitcast_dynamic-update-slice_fusion.8
  600.9 38.1 %all-gather.53.cloned.1.call-done = f32[512,8,128]{2,1,0:T(8,128)} async-done(((f32[64,8,128]{2,1,0:T(8,128)}), f32[512,8,128]{2,1,0:T(8,128)}) %all-gather.53.cloned.1.call-update) | async-done | bytes 2097168 | tf_op jit(solution)/shard_map/all_gather | solution.py:26
  638.9 41.3 %all-gather.55.cloned.1.call-done = f32[512,8,128]{2,1,0:T(8,128)} async-done(((f32[64,8,128]{2,1,0:T(8,128)}), f32[512,8,128]{2,1,0:T(8,128)}) %all-gather.55.cloned.1.call-update) | async-done | bytes 2097168 | tf_op jit(solution)/shard_map/all_gather | solution.py:26
  680.3 3.0 fusion.53
  684.4 26.9 %all-gather.39.cloned.1.call-done = f32[4,64,8,128]{3,2,1,0:T(8,128)} async-done(((f32[1,64,8,128]{3,2,1,0:T(8,128)}), f32[4,64,8,128]{3,2,1,0:T(8,128)}) %all-gather.39.cloned.1.call-update) | async-done | bytes 1048592 | tf_op jit(solution)/shard_map/all_gather | solution.py:26
  711.4 28.6 %all-gather.37.cloned.1.call-done = f32[4,64,8,128]{3,2,1,0:T(8,128)} async-done(((f32[1,64,8,128]{3,2,1,0:T(8,128)}), f32[4,64,8,128]{3,2,1,0:T(8,128)}) %all-gather.37.cloned.1.call-update) | async-done | bytes 1048592 | tf_op jit(solution)/shard_map/all_gather | solution.py:26
  739.9 2.4 fusion.52
  743.3 2.3 fusion.43
  746.8 32.1 %all_to_all.36 = f32[8,64,8,128]{3,2,0,1:T(8,128)S(1)} all-to-all(f32[8,64,8,128]{3,2,0,1:T(8,128)S(1)} %copy.33), channel_id=1, replica_groups=mesh['ta_0'=4,'ta_1'=8,'gx'=8] {'gx'}, dimensions={1} | all-to-all | bytes 4194304 | tf_op jit(solution)/shard_map/all_to_all | solution.py:153
  778.9 1.9 fusion.37
  780.8 3.3 convolution_bitcast_fusion
  (280 shorter events, 116.3 us)
Async XLA Ops:
  6.5 234.4 %copy-start = (f32[8,8,64,128]{3,2,1,0:T(8,128)S(1)}, f32[8,8,64,128]{3,2,1,0:T(8,128)}, u32[]{:S(2)}) copy-start(f32[8,8,64,128]{3,2,1,0:T(8,128)} %param.14) | copy-start | bytes 6291460
  6.5 100.1 %all-gather.41.cloned.1.call-start = ((), (), s32[]{:S(2)}) async-start(), calls=%async_computation.10 | async-start | bytes 2359296 | tf_op jit(solution)/shard_map/all_gather | solution.py:26
  64.6 2.2 copy-start.5
  65.2 82.8 %all-gather.43.cloned.1.call-start = ((), (), s32[]{:S(2)}) async-start(), calls=%async_computation.11 | async-start | bytes 2359296 | tf_op jit(solution)/shard_map/all_gather | solution.py:26
  66.0 123.6 %all-gather.45.cloned.1.call-start = ((), (), s32[]{:S(2)}) async-start(), calls=%async_computation.12 | async-start | bytes 2359296 | tf_op jit(solution)/shard_map/all_gather | solution.py:26
  66.7 164.2 %all-gather.47.cloned.1.call-start = ((), (), s32[]{:S(2)}) async-start(), calls=%async_computation.13 | async-start | bytes 2359296 | tf_op jit(solution)/shard_map/all_gather | solution.py:26
  67.3 226.7 %all-gather.25.cloned.1.call-start = ((), (), s32[]{:S(2)}) async-start(), calls=%async_computation.2 | async-start | bytes 1310720 | tf_op jit(solution)/shard_map/all_gather | solution.py:26
  233.0 3.3 copy-start.13
  238.7 2.3 copy-start.53
  239.6 56.6 %all-gather.27.cloned.1.call-start = ((), (), s32[]{:S(2)}) async-start(), calls=%async_computation.3 | async-start | bytes 1310720 | tf_op jit(solution)/shard_map/all_gather | solution.py:26
  240.2 84.7 %all-gather.31.cloned.1.call-start = ((), (), s32[]{:S(2)}) async-start(), calls=%async_computation.5 | async-start | bytes 1310720 | tf_op jit(solution)/shard_map/all_gather | solution.py:26
  247.4 36.4 %copy-start.54 = (f32[64,64]{1,0:T(8,128)S(1)}, f32[64,64]{1,0:T(8,128)}, u32[]{:S(2)}) copy-start(f32[64,64]{1,0:T(8,128)} %param.15) | copy-start | bytes 49156
  247.4 35.1 %all-to-all-start = ((f32[8,8,64,128]{3,1,0,2:T(8,128)}), f32[8,8,64,128]{3,1,0,2:T(8,128)S(1)}, u32[]{:S(2)}, u32[]{:S(2)}) async-start(f32[8,8,64,128]{3,1,0,2:T(8,128)} %copy.28), calls=%async_computation | async-start | bytes 4194304 | tf_op jit(solution)/shard_map/all_to_all | solution.py:73
  256.2 97.5 %all-gather.29.cloned.1.call-start = ((), (), s32[]{:S(2)}) async-start(), calls=%async_computation.4 | async-start | bytes 1310720 | tf_op jit(solution)/shard_map/all_gather | solution.py:26
  256.9 208.8 %all-gather.49.cloned.1.call-start = ((), (), s32[]{:S(2)}) async-start(), calls=%async_computation.14 | async-start | bytes 2359296 | tf_op jit(solution)/shard_map/all_gather | solution.py:26
  283.9 5.0 copy-start.9
  283.9 5.0 copy-start.11
  353.7 2.4 copy-start.26
  353.7 2.5 copy-start.27
  353.7 3.8 copy-start.40
  353.7 3.8 copy-start.41
  353.7 3.8 copy-start.42
  353.7 3.8 copy-start.43
  353.7 3.8 copy-start.44
  353.7 3.8 copy-start.45
  353.7 3.8 copy-start.46
  353.7 3.8 copy-start.47
  353.7 3.8 copy-start.48
  353.7 3.8 copy-start.49
  353.7 3.8 copy-start.50
  353.7 3.8 copy-start.51
  363.3 3.0 copy-start.52
  426.7 80.4 %all-gather.51.cloned.1.call-start = ((), (), s32[]{:S(2)}) async-start(), calls=%async_computation.15 | async-start | bytes 2359296 | tf_op jit(solution)/shard_map/all_gather | solution.py:26
  427.2 111.0 %all-gather.35.cloned.1.call-start = ((), (), s32[]{:S(2)}) async-start(), calls=%async_computation.7 | async-start | bytes 1310720 | tf_op jit(solution)/shard_map/all_gather | solution.py:26
  465.8 44.5 %copy-start.7 = (f32[512,8,128]{2,1,0:T(8,128)S(1)}, f32[512,8,128]{2,1,0:T(8,128)}, u32[]{:S(2)}) copy-start(f32[512,8,128]{2,1,0:T(8,128)} %all-gather.49.cloned.1.call-done) | copy-start | bytes 6291460
  510.2 56.6 %copy-start.25 = (f32[1,64,8,128]{3,2,1,0:T(8,128)S(1)}, f32[1,64,8,128]{3,2,1,0:T(8,128)}, u32[]{:S(2)}) copy-start(f32[1,64,8,128]{3,2,1,0:T(8,128)} %get-tuple-element.747) | copy-start | bytes 786436
  510.2 56.6 %all-gather.33.cloned.1.call-start = ((), (), s32[]{:S(2)}) async-start(), calls=%async_computation.6 | async-start | bytes 1310720 | tf_op jit(solution)/shard_map/all_gather | solution.py:26
  511.2 127.7 %all-gather.53.cloned.1.call-start = ((), (), s32[]{:S(2)}) async-start(), calls=%async_computation.16 | async-start | bytes 2359296 | tf_op jit(solution)/shard_map/all_gather | solution.py:26
  566.8 2.7 copy-start.18
  566.8 3.3 copy-start.19
  600.1 80.1 %all-gather.55.cloned.1.call-start = ((), (), s32[]{:S(2)}) async-start(), calls=%async_computation.17 | async-start | bytes 2359296 | tf_op jit(solution)/shard_map/all_gather | solution.py:26
  600.7 110.6 %all-gather.39.cloned.1.call-start = ((), (), s32[]{:S(2)}) async-start(), calls=%async_computation.9 | async-start | bytes 1310720 | tf_op jit(solution)/shard_map/all_gather | solution.py:26
  638.9 44.7 %copy-start.6 = (f32[512,8,128]{2,1,0:T(8,128)S(1)}, f32[512,8,128]{2,1,0:T(8,128)}, u32[]{:S(2)}) copy-start(f32[512,8,128]{2,1,0:T(8,128)} %all-gather.53.cloned.1.call-done) | copy-start | bytes 6291460
  683.3 56.6 %copy-start.24 = (f32[1,64,8,128]{3,2,1,0:T(8,128)S(1)}, f32[1,64,8,128]{3,2,1,0:T(8,128)}, u32[]{:S(2)}) copy-start(f32[1,64,8,128]{3,2,1,0:T(8,128)} %get-tuple-element.741) | copy-start | bytes 786436
  683.3 56.6 %all-gather.37.cloned.1.call-start = ((), (), s32[]{:S(2)}) async-start(), calls=%async_computation.8 | async-start | bytes 1310720 | tf_op jit(solution)/shard_map/all_gather | solution.py:26
  739.9 2.5 copy-start.21
  739.9 3.2 copy-start.22
  778.9 5.3 copy-start.1
  (26 other events, 39.9 us)
Sparse Core Ops, SparseCore 0:
  65.4 41.1 all-gather.40
  108.4 39.6 all-gather.42
  149.9 39.6 all-gather.44
  191.2 39.6 all-gather.46
  239.7 27.8 all-gather.24
  269.3 26.8 all-gather.26
  298.0 26.8 all-gather.30
  326.7 26.8 all-gather.28
  426.8 38.9 all-gather.48
  467.4 39.6 all-gather.50
  510.3 27.8 all-gather.34
  539.9 26.8 all-gather.32
  600.2 38.6 all-gather.52
  640.6 39.6 all-gather.54
  683.4 27.8 all-gather.38
  713.0 26.8 all-gather.36
where the time goes:
time: 792 us; the launch traced here: 791 us
  waiting for transfers between devices  524 us (66%)
  other arithmetic  99 us (12%)
  local copies, waits for them, and re-layouts  60 us (8%)
  loops' own time  35.9 us (5%)
  blocking collectives  32.1 us (4%)
  matrix products  16.3 us (2%)
  between operations  14 us (2%)
  starting transfers between devices  9.73 us (1%)
    all_gather x16, waiting for transfers between devices, carried_in(): pieces = jax.tree.map(lambda part: lax.all_gather(part, axis), total)  493 us
    dynamic_slice x56, local copies, waits for them, and re-layouts, local(): lax.scan(pivot_product, identity, (current, following, closing))  34.8 us
    all_to_all x1, blocking collectives, local(): lax.all_to_all(cell_field, 'gx', split_axis=1, concat_axis=2, tiled=True)  32.1 us
    dynamic_update_slice x16, other arithmetic, local(): lax.scan(eliminate, (before[0], before[2], all_ones, all_zeros), (current...  29.6 us
    all_to_all x1, waiting for transfers between devices, local(): lax.all_to_all(volume, 'gx', split_axis=2, concat_axis=1, tiled=True)  25.3 us
  transfers between devices with their start and end apart: 17, of which 16 were waited for; matrix products, arithmetic and copies ran while one was open for 2% of the time, Pallas kernels for 0%

commit v1 on v0

v1 whole, which is shorter than its diff:
```python
from functools import partial

import jax
import jax.numpy as jnp
from jax import lax
from jax.experimental import pallas as pl
from jax.experimental.pallas import tpu as pltpu
from jax.sharding import PartitionSpec as P

f32, bf16 = jnp.float32, jnp.bfloat16
params = partial(pltpu.CompilerParams, vmem_limit_bytes=48 * 2**20)


def split(x):
    high = x.astype(bf16)
    return high, (x - high.astype(f32)).astype(bf16)


def dot3(left, right):
    (lh, ll), (rh, rl) = left, right
    mm = partial(jnp.dot, preferred_element_type=f32)
    return mm(lh, rh) + (mm(lh, rl) + mm(ll, rh))


def cost(flops, bytes_accessed):
    return pl.CostEstimate(flops=int(flops), bytes_accessed=int(bytes_accessed), transcendentals=0)


def forward_body(x_ref, by_ref, bz_ref, out_ref):
    rows, y, z = x_ref.shape[1:]
    vol = dot3(split(x_ref[0].reshape(rows * y, z)), split(bz_ref[...]))
    by = split(by_ref[...])
    for a in range(rows):
        plane = dot3(by, split(vol[a * y : (a + 1) * y]))
        out_ref[:, 0, a] = plane.reshape(out_ref.shape[0], y // out_ref.shape[0], z)


def forward_yz(x, by_t, bz, members):
    t, a, y, z = x.shape
    span = y // members
    return pl.pallas_call(
        forward_body,
        grid=(t,),
        in_specs=[
            pl.BlockSpec((1, a, y, z), lambda k: (k, 0, 0, 0)),
            pl.BlockSpec((y, y), lambda k: (0, 0)),
            pl.BlockSpec((z, z), lambda k: (0, 0)),
        ],
        out_specs=pl.BlockSpec((members, 1, a, span, z), lambda k: (0, k, 0, 0, 0)),
        out_shape=jax.ShapeDtypeStruct((members, t, a, span, z), f32),
        compiler_params=params(),
        cost_estimate=cost(6 * t * a * y * z * (y + z), 8 * x.size),
        name="forward_yz",
    )(x, by_t, bz)


def backward_body(x_ref, by_ref, bz_ref, out_ref):
    rows, y, z = out_ref.shape[1:]
    by, bz = split(by_ref[...]), split(bz_ref[...])
    planes = [
        dot3(by, split(x_ref[:, 0, a].reshape(y, z))) for a in range(rows)
    ]
    vol = jnp.concatenate(planes, axis=0)
    out_ref[0] = dot3(split(vol), bz).reshape(rows, y, z)


def backward_yz(x, by, bz_t):
    members, t, a, span, z = x.shape
    y = members * span
    return pl.pallas_call(
        backward_body,
        grid=(t,),
        in_specs=[
            pl.BlockSpec((members, 1, a, span, z), lambda k: (0, k, 0, 0, 0)),
            pl.BlockSpec((y, y), lambda k: (0, 0)),
            pl.BlockSpec((z, z), lambda k: (0, 0)),
        ],
        out_specs=pl.BlockSpec((1, a, y, z), lambda k: (k, 0, 0, 0)),
        out_shape=jax.ShapeDtypeStruct((t, a, y, z), f32),
        compiler_params=params(),
        cost_estimate=cost(6 * t * a * y * z * (y + z), 8 * x.size),
        name="backward_yz",
    )(x, by, bz_t)


def row_terms(eigen, lens, k, closing):
    main = eigen * ((lens[k] + lens[k + 1]) / 3.0) + closing
    sub = eigen * (lens[k] / 6.0) - 0.5
    sup = eigen * (lens[k + 1] / 6.0) + 0.5
    return main, sub, sup


def reduced_body(count, rows, lens_ref, eigen_ref, cl_ref, e_ref, a_ref, k_ref, b_ref, q_ref):
    eigen = eigen_ref[...]

    def block(j, carry):
        lens = [lens_ref[j * rows + k] for k in range(rows + 1)]
        pivots, subs, ratios = [], [], []
        for k in range(rows):
            closing = jnp.where(jnp.logical_and(j == count - 1, k == rows - 1), 0.5, 0.0)
            main, sub, sup = row_terms(eigen, lens, k, closing)
            pivot = main - sub * ratios[-1] if k else main
            inverse = 1.0 / pivot
            pivots.append(inverse)
            subs.append(sub)
            ratios.append(sup * inverse)
        front = subs[0] * pivots[0]
        fronts = [front]
        for k in range(1, rows):
            front = -(subs[k] * pivots[k]) * front
            fronts.append(front)
        last = ratios[rows - 1]
        low = fronts[rows - 1]
        cl_ref[j] = low
        e_ref[j] = last
        for k in reversed(range(rows - 1)):
            low = fronts[k] - ratios[k] * low
            last = -ratios[k] * last
        a_ref[j] = low
        b_ref[j] = last
        return carry

    lax.fori_loop(0, count, block, 0, unroll=4)

    def sweep(j, q_before):
        v_last, w_last, v_first, w_first = cl_ref[j], e_ref[j], a_ref[j], b_ref[j]
        scale = 1.0 / (1.0 - v_first * q_before)
        back = w_first * scale
        q_now = w_last + v_last * q_before * back
        e_now = v_last * scale
        cl_ref[j] = e_now * q_before
        e_ref[j] = e_now
        a_ref[j] = scale
        k_ref[j] = v_first * scale
        b_ref[j] = back
        q_ref[j] = q_now
        return q_now

    lax.fori_loop(0, count, sweep, jnp.zeros_like(eigen))


def reduced_terms(lens, eigen, count, rows):
    shape = (count,) + eigen.shape
    return pl.pallas_call(
        partial(reduced_body, count, rows),
        in_specs=[
            pl.BlockSpec(memory_space=pltpu.SMEM),
            pl.BlockSpec(memory_space=pltpu.VMEM),
        ],
        out_specs=[pl.BlockSpec(memory_space=pltpu.VMEM)] * 6,
        out_shape=[jax.ShapeDtypeStruct(shape, f32)] * 6,
        compiler_params=params(),
        cost_estimate=cost(40 * rows * count * eigen.size, 24 * count * eigen.size),
        name="reduced_terms",
    )(lens, eigen)


def interface_body(count, g_ref, cl_ref, e_ref, a_ref, k_ref, b_ref, q_ref, out_ref, fh_ref):
    zero = jnp.zeros(g_ref.shape[2:], f32)

    def down(j, before):
        first, last = g_ref[j, 0], g_ref[j, 1]
        out_ref[j, 0] = before
        fh_ref[j] = a_ref[j] * first - k_ref[j] * before
        return (last + cl_ref[j] * first) - e_ref[j] * before

    top = lax.fori_loop(0, count, down, zero, unroll=8)
    fh_ref[count] = top

    def up(i, after):
        j = count - 1 - i
        out_ref[j, 1] = after

        @pl.when(j < count - 1)
        def _():
            out_ref[j + 1, 0] = out_ref[j + 1, 0] - q_ref[j] * after

        return fh_ref[j] - b_ref[j] * after

    lax.fori_loop(0, count, up, zero, unroll=8)


def interface_solve(g, terms):
    count = g.shape[0]
    return pl.pallas_call(
        partial(interface_body, count),
        in_specs=[pl.BlockSpec(memory_space=pltpu.VMEM)] * 7,
        out_specs=pl.BlockSpec(memory_space=pltpu.VMEM),
        out_shape=jax.ShapeDtypeStruct(g.shape, f32),
        scratch_shapes=[pltpu.VMEM((count + 1,) + g.shape[2:], f32)],
        compiler_params=params(),
        cost_estimate=cost(6 * g.size, 20 * g.size),
        name="interface_solve",
    )(g, *terms)


def eliminate_body(lens_ref, close_ref, x_ref, eigen_ref, wh_ref, wl_ref, g_ref, ends_ref, ratio_ref):
    t = pl.program_id(0)
    rows, modes, lanes = g_ref.shape
    spectral = dot3((wh_ref[...], wl_ref[...]), split(x_ref[:, 0].reshape(modes, lanes)))
    eigen = eigen_ref[...]
    main = eigen * ((lens_ref[t] + lens_ref[t + 1]) / 3.0) + close_ref[t]
    sub = eigen * (lens_ref[t] / 6.0) - 0.5
    sup = eigen * (lens_ref[t + 1] / 6.0) + 0.5

    @pl.when(t == 0)
    def _():
        inverse = 1.0 / main
        ratio_ref[t] = sup * inverse
        g_ref[t] = spectral * inverse

    @pl.when(t > 0)
    def _():
        inverse = 1.0 / (main - sub * ratio_ref[t - 1])
        ratio_ref[t] = sup * inverse
        g_ref[t] = (spectral - sub * g_ref[t - 1]) * inverse

    @pl.when(t == rows - 1)
    def _():
        split_shape = (ends_ref.shape[0], modes // ends_ref.shape[0], lanes)
        now = g_ref[rows - 1]
        ends_ref[:, 1] = now.reshape(split_shape)
        for k in reversed(range(rows - 1)):
            now = g_ref[k] - ratio_ref[k] * now
            g_ref[k] = now
        ends_ref[:, 0] = now.reshape(split_shape)


def eliminate(x, eigen, weights, lens, close, count):
    members, t, a, span, z = x.shape
    modes = members * a * span
    whole = lambda *shape: pl.BlockSpec(shape, lambda k: (0,) * len(shape))
    return pl.pallas_call(
        eliminate_body,
        grid=(t,),
        in_specs=[
            pl.BlockSpec(memory_space=pltpu.SMEM),
            pl.BlockSpec(memory_space=pltpu.SMEM),
            pl.BlockSpec((members, 1, a, span, z), lambda k: (0, k, 0, 0, 0)),
            whole(modes, z),
            whole(modes, modes),
            whole(modes, modes),
        ],
        out_specs=[whole(t, modes, z), whole(count, 2, modes // count, z)],
        out_shape=[
            jax.ShapeDtypeStruct((t, modes, z), f32),
            jax.ShapeDtypeStruct((count, 2, modes // count, z), f32),
        ],
        scratch_shapes=[pltpu.VMEM((t, modes, z), f32)],
        compiler_params=params(),
        cost_estimate=cost(6 * t * modes * modes * z, 8 * x.size),
        name="eliminate",
    )(lens, close, x, eigen, *weights)


def substitute_body(lens_ref, close_ref, g_ref, ends_ref, eigen_ref, wh_ref, wl_ref, out_ref, sol_ref):
    t = pl.program_id(0)
    rows, modes, lanes = g_ref.shape

    @pl.when(t == 0)
    def _():
        eigen = eigen_ref[...]
        lens = [lens_ref[k] for k in range(rows + 1)]
        before = ends_ref[:, 0].reshape(modes, lanes)
        after = ends_ref[:, 1].reshape(modes, lanes)
        ratios, values = [], []
        for k in range(rows):
            main, sub, sup = row_terms(eigen, lens, k, close_ref[k])
            inverse = 1.0 / (main - sub * ratios[-1] if k else main)
            ratios.append(sup * inverse)
            value = -(sub * inverse) * (values[-1] if k else before)
            if k == rows - 1:
                value = value - ratios[-1] * after
            values.append(value)
        now = values[rows - 1]
        sol_ref[rows - 1] = g_ref[rows - 1] + now
        for k in reversed(range(rows - 1)):
            now = values[k] - ratios[k] * now
            sol_ref[k] = g_ref[k] + now

    cell = dot3((wh_ref[...], wl_ref[...]), split(sol_ref[t]))
    out_ref[:, 0] = cell.reshape(out_ref.shape[:1] + out_ref.shape[2:])


def substitute(g, ends, eigen, weights, lens, close, members):
    t, modes, z = g.shape
    span = 8
    a = modes // (members * span)
    whole = lambda *shape: pl.BlockSpec(shape, lambda k: (0,) * len(shape))
    return pl.pallas_call(
        substitute_body,
        grid=(t,),
        in_specs=[
            pl.BlockSpec(memory_space=pltpu.SMEM),
            pl.BlockSpec(memory_space=pltpu.SMEM),
            whole(t, modes, z),
            whole(*ends.shape),
            whole(modes, z),
            whole(modes, modes),
            whole(modes, modes),
        ],
        out_specs=pl.BlockSpec((members, 1, a, span, z), lambda k: (0, k, 0, 0, 0)),
        out_shape=jax.ShapeDtypeStruct((members, t, a, span, z), f32),
        scratch_shapes=[pltpu.VMEM((t, modes, z), f32)],
        compiler_params=params(),
        cost_estimate=cost(6 * t * modes * modes * z, 8 * g.size),
        name="substitute",
    )(lens, close, g, ends, eigen, *weights)


def spread_body(bx_ref, fh_ref, fl_ref, bh_ref, bl_ref):
    x = bx_ref.shape[0]
    modes = fh_ref.shape[0]
    span = modes // x
    row = lax.broadcasted_iota(jnp.int32, (modes, x), 0) // span
    col = lax.broadcasted_iota(jnp.int32, (modes, x), 1)
    pick = jnp.where(row == col, 1.0, 0.0).astype(bf16)
    row = lax.broadcasted_iota(jnp.int32, (x, modes), 0)
    col = lax.broadcasted_iota(jnp.int32, (x, modes), 1) // span
    pick_t = jnp.where(row == col, 1.0, 0.0).astype(bf16)
    row = lax.broadcasted_iota(jnp.int32, (modes, modes), 0)
    col = lax.broadcasted_iota(jnp.int32, (modes, modes), 1)
    same = row % span == col % span
    mm = partial(jnp.dot, preferred_element_type=f32)
    for source, (h_ref, l_ref) in ((bx_ref[...].T, (fh_ref, fl_ref)), (bx_ref[...], (bh_ref, bl_ref))):
        for part, ref in zip(split(source), (h_ref, l_ref)):
            wide = mm(mm(pick, part).astype(bf16), pick_t)
            ref[...] = jnp.where(same, wide, 0.0).astype(bf16)


def spread(basis_x, span):
    modes = basis_x.shape[0] * span
    return pl.pallas_call(
        spread_body,
        in_specs=[pl.BlockSpec(memory_space=pltpu.VMEM)],
        out_specs=[pl.BlockSpec(memory_space=pltpu.VMEM)] * 4,
        out_shape=[jax.ShapeDtypeStruct((modes, modes), bf16)] * 4,
        compiler_params=params(),
        cost_estimate=cost(8 * modes * modes * 64, 8 * modes * modes),
        name="spread",
    )(basis_x)


def local(right_side, basis_x, basis_y, basis_z, eig_x, eig_y, eig_z, steps):
    rows = right_side.shape[0]
    members, count = lax.axis_size("gx"), lax.axis_size("ta")
    member, place = lax.axis_index("gx"), lax.axis_index("ta")
    span = basis_y.shape[0] // members
    total = steps.shape[0]

    lengths = steps / total
    padded = jnp.concatenate([lengths, jnp.zeros((1,), f32)])
    lens = lax.dynamic_slice_in_dim(padded, place * rows, rows + 1)
    close = jnp.where(place * rows + jnp.arange(rows) == total - 1, 0.5, 0.0).astype(f32)
    part_y = lax.dynamic_slice_in_dim(eig_y, member * span, span)
    eigen = (eig_x[:, None, None] + part_y[None, :, None] + eig_z[None, None, :]).reshape(
        -1, eig_z.shape[0]
    )
    share = eigen.shape[0] // count
    eigen_own = lax.dynamic_slice_in_dim(eigen, place * share, share)

    volume = forward_yz(right_side, basis_y.T, basis_z, members)
    weights = spread(basis_x, span)
    terms = reduced_terms(padded, eigen_own, count, rows)
    volume = lax.all_to_all(volume, "gx", 0, 0, tiled=True)
    g, ends = eliminate(volume, eigen, weights[:2], lens, close, count)
    ends = lax.all_to_all(ends, "ta", 0, 0, tiled=True)
    ends = interface_solve(ends, terms)
    ends = lax.all_to_all(ends, "ta", 0, 0, tiled=True)
    cell = substitute(g, ends, eigen, weights[2:], lens, close, members)
    cell = lax.all_to_all(cell, "gx", 0, 0, tiled=True)
    return backward_yz(cell, basis_y, basis_z.T)


def solution(mesh):
    return jax.shard_map(
        local,
        mesh=mesh,
        in_specs=(P("ta", "gx", None, None), P(), P(), P(), P(), P(), P(), P()),
        out_specs=P("ta", "gx", None, None),
        check_vma=False,
    )
```

time: 792 us -> 153 us (0.19)
  waiting for transfers between devices: 524 us -> 56.3 us
  other arithmetic: 99 us -> 0.15 us
  local copies, waits for them, and re-layouts: 60 us -> 20.1 us
  loops' own time: 35.9 us -> 0 us
  Pallas kernels: 0 us -> 29.2 us
  matrix products: 16.3 us -> 0 us
  starting transfers between devices: 9.73 us -> 25.3 us
  between operations: 14 us -> 0.17 us
  blocking collectives: 32.1 us -> 21.2 us
    all_gather x16 -> x0, waiting for transfers between devices: 493 us -> none  [carried_in(): pieces = jax.tree.map(lambda part: lax.all_gather(part, axis), total)]
    mul x32 -> x0, other arithmetic: 45.2 us -> none  [the longest x8 13.2 us: pivot_product(): top_left * factor]
    dynamic_slice x65 -> x3, local copies, waits for them, and re-layouts: 43.2 us -> 0.16 us  [the longest x1 0.08 us: local(): lens = lax.dynamic_slice_in_dim(padded, place * rows, rows + 1)]
    another operation x3 -> x0, loops' own time: 35.9 us -> none  [the longest x1 15.5 us: local(): lax.scan(eliminate, (before[0], before[2], all_ones, all_zeros), (current...]
    all_to_all x1 -> x3, waiting for transfers between devices: 25.3 us -> 56.3 us  [the longest x1 26.3 us: local(): cell = lax.all_to_all(cell, 'gx', 0, 0, tiled=True)]
    dynamic_update_slice x16 -> x0, other arithmetic: 29.6 us -> none  [local(): lax.scan(eliminate, (before[0], before[2], all_ones, all_zeros), (current...]
    pallas_call x0 -> x7, Pallas kernels: none -> 29.2 us  [the longest x1 7.51 us: substitute(): pl.pallas_call(substitute_body, grid=(t,), in_specs=[pl.BlockSpec(memory_...]
    add x13 -> x0, other arithmetic: 17.4 us -> none  [the longest x9 9.5 us: compose_matrix(): sum((latter[degree * row_at + inner_at] * earlier[degree * inner_at + col...]
  transfers between devices with their start and end apart: 17 -> 3, of which waited for: 16 -> 3; matrix products, arithmetic and copies ran while one was open for 2% -> 0% of each run, Pallas kernels for 0% -> 3%
where the time goes in v1:
time: 153 us; the launch traced here: 152 us
  waiting for transfers between devices  56.3 us (37%)
  Pallas kernels  29.2 us (19%)
  starting transfers between devices  25.3 us (17%)
  blocking collectives  21.2 us (14%)
  local copies, waits for them, and re-layouts  20.1 us (13%)
    all_to_all x1, waiting for transfers between devices, local(): cell = lax.all_to_all(cell, 'gx', 0, 0, tiled=True)  26.3 us
    all_to_all x1, waiting for transfers between devices, local(): volume = lax.all_to_all(volume, 'gx', 0, 0, tiled=True)  22.8 us
    all_to_all x1, blocking collectives, local(): ends = lax.all_to_all(ends, 'ta', 0, 0, tiled=True)  21.2 us
    unnamed x58, local copies, waits for them, and re-layouts  19.7 us
    all_to_all x1, starting transfers between devices, local(): ends = lax.all_to_all(ends, 'ta', 0, 0, tiled=True)  10.2 us
    all_to_all x1, starting transfers between devices, local(): cell = lax.all_to_all(cell, 'gx', 0, 0, tiled=True)  8.19 us
    pallas_call x1, Pallas kernels, substitute(): pl.pallas_call(substitute_body, grid=(t,), in_specs=[pl.BlockSpec(memory_...  7.51 us
    all_to_all x1, waiting for transfers between devices, local(): ends = lax.all_to_all(ends, 'ta', 0, 0, tiled=True)  7.22 us
  transfers between devices with their start and end apart: 3, of which 3 were waited for; matrix products, arithmetic and copies ran while one was open for 0% of the time, Pallas kernels for 3%

profile of v1, /device:TPU:1, one launch (start us, length us, event | category | flops | bytes accessed | tf_op | source)
XLA Modules:
  0.0 152.5 jit_solution(7166002193650600654)
XLA Ops:
  0.0 0.8 copy.11
  0.8 0.0 copy-start
  0.8 1.6 %copy-done = f32[8,8,64,128]{3,2,1,0:T(8,128)S(1)} copy-done((f32[8,8,64,128]{3,2,1,0:T(8,128)S(1)}, f32[8,8,64,128]{3,2,1,0:T(8,128)}, u32[]{:S(2)}) %copy-start) | copy-done | bytes 2097176
  2.4 0.8 copy-done.6
  3.3 5.8 %forward_yz.1 = f32[8,8,8,8,128]{4,3,2,1,0:T(8,128)} custom-call(f32[8,8,64,128]{3,2,1,0:T(8,128)S(1)} %copy-done, f32[64,64]{1,0:T(8,128)S(1)} %bitcast.5, f32[128,128]{1,0:T(8,128)S(1)} %copy-done.6), custom_call_target="tpu_custom_call" | custom-call | flops 603979776 | bytes 4194304 | tf_op jit(solution)/shard_map/forward_yz/pallas_call | solution.py:41
  9.1 0.0 copy-start.26
  9.1 6.9 %all-to-all-start = ((f32[8,8,8,8,128]{4,3,2,1,0:T(8,128)}), f32[8,8,8,8,128]{4,3,2,1,0:T(8,128)S(1)}, u32[]{:S(2)}, u32[]{:S(2)}) async-start(f32[8,8,8,8,128]{4,3,2,1,0:T(8,128)} %forward_yz.1), calls=%async_computation | async-start | bytes 4194304 | tf_op jit(solution)/shard_map/all_to_all | solution.py:365
  16.0 0.0 copy-done.27
  16.0 0.1 dynamic_slice.10
  16.1 0.1 add.58
  16.2 0.0 copy-done.25
  16.2 0.1 add.54
  16.3 0.1 add.55
  16.4 0.0 copy-done.24
  16.4 0.1 dynamic_slice.9.lens_ref
  16.5 1.3 spread.1
  17.8 0.8 copy-done.3
  18.6 0.8 copy-done.22
  19.4 0.1 broadcast_add_fusion.eigen_ref
  19.5 22.8 %all-to-all-done.x_ref = f32[8,8,8,8,128]{4,3,2,1,0:T(8,128)S(1)} async-done(((f32[8,8,8,8,128]{4,3,2,1,0:T(8,128)}), f32[8,8,8,8,128]{4,3,2,1,0:T(8,128)S(1)}, u32[]{:S(2)}, u32[]{:S(2)}) %all-to-all-start) | async-done | bytes 2097184 | tf_op jit(solution)/shard_map/all_to_all | solution.py:365
  42.4 1.3 copy-done.1
  43.7 1.6 %copy-done.2 = f32[8,8,8,8,128]{4,3,2,1,0:T(8,128)S(1)} copy-done((f32[8,8,8,8,128]{4,3,2,1,0:T(8,128)S(1)}, f32[8,8,8,8,128]{4,3,2,1,0:T(8,128)}, u32[]{:S(2)}) %copy-start.2) | copy-done | bytes 2097176
  45.3 1.0 copy-done.23
  46.3 6.6 %eliminate.1 = (f32[8,512,128]{2,1,0:T(8,128)S(1)}, f32[32,2,16,128]{3,2,1,0:T(8,128)S(1)}) custom-call(f32[9]{0:T(128)S(1)} %dynamic_slice.9.lens_ref, f32[8]{0:T(128)S(1)} %compare_select_fusion.close_ref, f32[8,8,8,8,128]{4,3,2,1,0:T(8,128)S(1)} %copy-done.2, f32[512,128]{1,0:T(8,128)S(1)} %broadcast_add_fusion.eigen_ref, ...), custom_call_target="tpu_custom_call" | custom-call | flops 1610612736 | bytes 4194304 | tf_op jit(solution)/shard_map/eliminate/pallas_call | solution.py:233
  52.9 0.0 copy-start.5
  53.0 0.8 copy-done.5
  53.7 10.2 %all-to-all-start.1 = ((f32[32,2,16,128]{3,2,1,0:T(8,128)}), f32[32,2,16,128]{3,2,1,0:T(8,128)S(1)}, u32[]{:S(2)}, u32[]{:S(2)}) async-start(f32[32,2,16,128]{3,2,1,0:T(8,128)} %copy-done.5), calls=%async_computation.1 | async-start | bytes 1048576 | tf_op jit(solution)/shard_map/all_to_all | solution.py:367
  64.0 2.6 %reduced_terms.1 = (f32[32,16,128]{2,1,0:T(8,128)S(1)}, f32[32,16,128]{2,1,0:T(8,128)S(1)}, f32[32,16,128]{2,1,0:T(8,128)S(1)}, f32[32,16,128]{2,1,0:T(8,128)S(1...) custom-call(f32[257]{0:T(512)S(1)} %pad_maximum_fusion.lens_ref, ...), custom_call_target="tpu_custom_call" | custom-call | flops 20971520 | bytes 1572864 | tf_op jit(solution)/shard_map/reduced_terms/pallas_call | solution.py:144
  66.6 0.7 copy-done.8
  67.3 0.7 copy-done.10
  68.0 0.7 copy-done.12
  68.7 0.7 copy-done.14
  69.4 0.7 copy-done.16
  70.1 0.7 copy-done.18
  70.8 7.2 %all-to-all-done.1.g_ref = f32[32,2,16,128]{3,2,1,0:T(8,128)S(1)} async-done(((f32[32,2,16,128]{3,2,1,0:T(8,128)}), f32[32,2,16,128]{3,2,1,0:T(8,128)S(1)}, u32[]{:S(2)}, u32[]{:S(2)}) %all-to-all-start.1) | async-done | bytes 524320 | tf_op jit(solution)/shard_map/all_to_all | solution.py:367
  78.0 1.0 copy-done.9
  79.0 0.9 copy-done.11
  80.0 0.9 copy-done.13
  80.9 0.9 copy-done.15
  81.9 0.9 copy-done.17
  82.8 0.9 copy-done.19
  83.8 0.3 interface_solve.1
  84.2 21.2 %all_to_all.20.ends_ref = f32[32,2,16,128]{3,2,1,0:T(8,128)S(1)} all-to-all(f32[32,2,16,128]{3,2,1,0:T(8,128)S(1)} %interface_solve.1), channel_id=1, replica_groups=mesh['ta'=32,'gx'=8] {'ta'}, dimensions={0} | all-to-all | bytes 1048576 | tf_op jit(solution)/shard_map/all_to_all | solution.py:369
  105.4 7.5 %substitute.1 = f32[8,8,8,8,128]{4,3,2,1,0:T(8,128)} custom-call(f32[9]{0:T(128)S(1)} %dynamic_slice.9.lens_ref, f32[8]{0:T(128)S(1)} %compare_select_fusion.close_ref, f32[8,512,128]{2,1,0:T(8,128)S(1)} %get-tuple-element.19.g_ref, f32[32,2,16,128]{3,2,1,0:T(8,128)S(1)} %all_to_all.20.ends_ref, f32[512,128]{1,0:T(8,128)S(1)} %broadcast_add_fusion.eigen_ref, ...), custom_call_target="tpu_custom_call" | custom-call | flops 1610612736 | bytes 4194304 | tf_op jit(solution)/shard_map/substitute/pallas_call | solution.py:290
  112.9 8.2 %all-to-all-start.3 = ((f32[8,8,8,8,128]{4,3,2,1,0:T(8,128)}), f32[8,8,8,8,128]{4,3,2,1,0:T(8,128)S(1)}, u32[]{:S(2)}, u32[]{:S(2)}) async-start(f32[8,8,8,8,128]{4,3,2,1,0:T(8,128)} %substitute.1), calls=%async_computation.3 | async-start | bytes 4194304 | tf_op jit(solution)/shard_map/all_to_all | solution.py:371
  121.1 0.1 copy.12
  121.2 26.3 %all-to-all-done.3.x_ref = f32[8,8,8,8,128]{4,3,2,1,0:T(8,128)S(1)} async-done(((f32[8,8,8,8,128]{4,3,2,1,0:T(8,128)}), f32[8,8,8,8,128]{4,3,2,1,0:T(8,128)S(1)}, u32[]{:S(2)}, u32[]{:S(2)}) %all-to-all-start.3) | async-done | bytes 2097184 | tf_op jit(solution)/shard_map/all_to_all | solution.py:371
  147.4 5.1 %backward_yz.1 = f32[8,8,64,128]{3,2,1,0:T(8,128)} custom-call(f32[8,8,8,8,128]{4,3,2,1,0:T(8,128)S(1)} %all-to-all-done.3.x_ref, f32[64,64]{1,0:T(8,128)S(1)} %copy-done.20, f32[128,128]{1,0:T(8,128)S(1)} %bitcast.4), custom_call_target="tpu_custom_call" | custom-call | flops 603979776 | bytes 4194304 | tf_op jit(solution)/shard_map/backward_yz/pallas_call | solution.py:70
  (36 shorter events, 0.1 us)
Async XLA Ops:
  0.8 1.6 %copy-start = (f32[8,8,64,128]{3,2,1,0:T(8,128)S(1)}, f32[8,8,64,128]{3,2,1,0:T(8,128)}, u32[]{:S(2)}) copy-start(f32[8,8,64,128]{3,2,1,0:T(8,128)} %x_ref.1) | copy-start | bytes 6291460
  2.4 0.8 copy-start.6
  9.1 6.9 %copy-start.27 = (f32[64]{0:T(128)S(1)}, f32[64]{0:T(128)}, u32[]{:S(2)}) copy-start(f32[64]{0:T(128)} %param.13) | copy-start | bytes 772
  9.1 7.1 %copy-start.25 = (f32[64]{0:T(128)S(1)}, f32[64]{0:T(128)}, u32[]{:S(2)}) copy-start(f32[64]{0:T(128)} %param.12) | copy-start | bytes 772
  9.1 7.3 %copy-start.24 = (f32[256]{0:T(256)S(1)}, f32[256]{0:T(256)}, u32[]{:S(2)}) copy-start(f32[256]{0:T(256)} %param.15) | copy-start | bytes 3076
  9.1 7.4 %copy-start.21 = (f32[64,64]{1,0:T(8,128)S(1)}, f32[64,64]{1,0:T(8,128)}, u32[]{:S(2)}) copy-start(f32[64,64]{1,0:T(8,128)} %bx_ref.1) | copy-start | bytes 49156
  9.1 10.3 %copy-start.26 = (f32[128]{0:T(128)S(1)}, f32[128]{0:T(128)}, u32[]{:S(2)}) copy-start(f32[128]{0:T(128)} %param.14) | copy-start | bytes 1540
  9.1 33.2 %all-to-all-start = ((f32[8,8,8,8,128]{4,3,2,1,0:T(8,128)}), f32[8,8,8,8,128]{4,3,2,1,0:T(8,128)S(1)}, u32[]{:S(2)}, u32[]{:S(2)}) async-start(f32[8,8,8,8,128]{4,3,2,1,0:T(8,128)} %forward_yz.1), calls=%async_computation | async-start | bytes 4194304 | tf_op jit(solution)/shard_map/all_to_all | solution.py:365
  17.8 0.8 copy-start.3
  18.6 0.8 copy-start.22
  42.4 1.3 copy-start.1
  43.7 1.6 %copy-start.2 = (f32[8,8,8,8,128]{4,3,2,1,0:T(8,128)S(1)}, f32[8,8,8,8,128]{4,3,2,1,0:T(8,128)}, u32[]{:S(2)}) copy-start(f32[8,8,8,8,128]{4,3,2,1,0:T(8,128)} %copy-done.1) | copy-start | bytes 6291460
  45.3 1.0 copy-start.23
  52.9 0.8 copy-start.5
  53.7 24.3 %all-to-all-start.1 = ((f32[32,2,16,128]{3,2,1,0:T(8,128)}), f32[32,2,16,128]{3,2,1,0:T(8,128)S(1)}, u32[]{:S(2)}, u32[]{:S(2)}) async-start(f32[32,2,16,128]{3,2,1,0:T(8,128)} %copy-done.5), calls=%async_computation.1 | async-start | bytes 1048576 | tf_op jit(solution)/shard_map/all_to_all | solution.py:367
  66.6 0.7 copy-start.8
  67.3 0.7 copy-start.10
  68.0 0.7 copy-start.12
  68.7 0.7 copy-start.14
  69.4 0.7 copy-start.16
  70.1 0.7 copy-start.18
  78.0 27.3 %copy-start.4 = (bf16[512,512]{1,0:T(8,128)(2,1)S(1)}, bf16[512,512]{1,0:T(8,128)(2,1)}, u32[]{:S(2)}) copy-start(bf16[512,512]{1,0:T(8,128)(2,1)} %copy-done.3) | copy-start | bytes 1572868
  78.0 1.0 copy-start.9
  79.0 0.9 copy-start.11
  80.0 0.9 copy-start.13
  80.9 0.9 copy-start.15
  81.9 0.9 copy-start.17
  82.8 0.9 copy-start.19
  112.9 8.2 %copy-start.7 = (f32[128,128]{1,0:T(8,128)S(1)}, f32[128,128]{1,0:T(8,128)}, u32[]{:S(2)}) copy-start(f32[128,128]{1,0:T(8,128)} %bz_ref.1) | copy-start | bytes 196612
  112.9 34.5 %copy-start.20 = (f32[64,64]{1,0:T(8,128)S(1)}, f32[64,64]{1,0:T(8,128)}, u32[]{:S(2)}) copy-start(f32[64,64]{1,0:T(8,128)} %by_ref.1) | copy-start | bytes 49156
  112.9 34.5 %all-to-all-start.3 = ((f32[8,8,8,8,128]{4,3,2,1,0:T(8,128)}), f32[8,8,8,8,128]{4,3,2,1,0:T(8,128)S(1)}, u32[]{:S(2)}, u32[]{:S(2)}) async-start(f32[8,8,8,8,128]{4,3,2,1,0:T(8,128)} %substitute.1), calls=%async_computation.3 | async-start | bytes 4194304 | tf_op jit(solution)/shard_map/all_to_all | solution.py:371

commit v2 on v1

v2 whole, which is shorter than its diff:
```python
from functools import partial

import jax
import jax.numpy as jnp
from jax import lax
from jax.experimental import pallas as pl
from jax.experimental.pallas import tpu as pltpu
from jax.sharding import PartitionSpec as P

f32, bf16 = jnp.float32, jnp.bfloat16
params = partial(pltpu.CompilerParams, vmem_limit_bytes=24 * 2**20)
VMEM = pl.BlockSpec(memory_space=pltpu.VMEM)
SMEM = pl.BlockSpec(memory_space=pltpu.SMEM)

PEERS = ((0, 0), (2, 0), (2, 1), (1, 0), (3, 0), (1, 1), (3, 1), (0, 1))


def peer(member, members, k, sign):
    chips, core = PEERS[k]
    ring = members // 2
    far = lax.rem(member // 2 + (sign * chips) % ring, ring)
    own = lax.rem(member, 2)
    return far * 2 + (1 - own if core else own)


def exchange(pieces):
    members = len(pieces)
    moved = [pieces[0]]
    for k in range(1, members):
        chips, core = PEERS[k]
        pairs = [(i, ((i // 2 + chips) * 2 + (i % 2 + core) % 2) % members) for i in range(members)]
        moved.append(lax.ppermute(pieces[k], "gx", pairs))
    return moved


def split(x):
    high = x.astype(bf16)
    return high, (x - high.astype(f32)).astype(bf16)


def left3(x):
    high, low = split(x)
    return jnp.concatenate([high, high, low], axis=1)


def right3(x):
    high, low = split(x)
    return jnp.concatenate([high, low, high], axis=0)


mm = partial(jnp.dot, preferred_element_type=f32)


def cost(flops, bytes_accessed):
    return pl.CostEstimate(flops=int(flops), bytes_accessed=int(bytes_accessed), transcendentals=0)


def whole(*shape):
    return pl.BlockSpec(shape, lambda k: (0,) * len(shape))


def array(*shape):
    return jax.ShapeDtypeStruct(shape, f32)


def gather_rows(source_ref, target_ref, sign):
    members = len(PEERS)
    span = target_ref.shape[0] // members
    member = lax.axis_index("gx")
    for k in range(members):
        start = pl.multiple_of(peer(member, members, k, sign) * span, span)
        target_ref[k * span : (k + 1) * span] = source_ref[pl.ds(start, span), :]


def forward_body(x_ref, by_ref, bz_ref, *refs):
    outs, (turn_ref, rows_ref, by3_ref, bz3_ref) = refs[:-4], refs[-4:]
    times, rows, y, z = x_ref.shape
    span = y // len(outs)

    @pl.when(pl.program_id(0) == 0)
    def _():
        turn_ref[...] = by_ref[...].T
        gather_rows(turn_ref, rows_ref, 1)
        by3_ref[...] = left3(rows_ref[...])
        bz3_ref[...] = right3(bz_ref[...])

    vol = [mm(left3(x_ref[t].reshape(rows * y, z)), bz3_ref[...]) for t in range(times)]
    for a in range(rows):
        plane = jnp.concatenate([v[a * y : (a + 1) * y] for v in vol], axis=1)
        plane = mm(by3_ref[...], right3(plane))
        for k, out in enumerate(outs):
            for t in range(times):
                out[t, pl.ds(a, span, stride=rows), :] = plane[
                    k * span : (k + 1) * span, t * z : (t + 1) * z
                ]


def forward_yz(x, by, bz, first, steps):
    _, a, y, z = x.shape
    members = len(PEERS)
    rows = a * y // members
    return pl.pallas_call(
        forward_body,
        grid=(steps // 2,),
        in_specs=[
            pl.BlockSpec((2, a, y, z), lambda k: (k + first // 2, 0, 0, 0)),
            whole(y, y),
            whole(z, z),
        ],
        out_specs=[pl.BlockSpec((2, rows, z), lambda k: (k, 0, 0))] * members,
        out_shape=[array(steps, rows, z)] * members,
        scratch_shapes=[
            pltpu.VMEM((y, y), f32),
            pltpu.VMEM((y, y), f32),
            pltpu.VMEM((y, 3 * y), bf16),
            pltpu.VMEM((3 * z, z), bf16),
        ],
        compiler_params=params(),
        cost_estimate=cost(6 * steps * a * y * z * (y + z), 8 * steps * a * y * z),
        name="forward_yz",
    )(x, by, bz)


def backward_body(by_ref, bz_ref, *refs):
    pieces, (out_ref, turn_ref, rows_ref, by3_ref, bz3_ref) = refs[: len(PEERS)], refs[-5:]
    times, rows, y, z = out_ref.shape
    span = y // len(pieces)

    @pl.when(pl.program_id(0) == 0)
    def _():
        turn_ref[...] = by_ref[...].T
        gather_rows(turn_ref, rows_ref, -1)
        by3_ref[...] = left3(rows_ref[...].T)
        bz3_ref[...] = right3(bz_ref[...].T)

    vol = [[] for t in range(times)]
    for a in range(rows):
        plane = jnp.concatenate(
            [
                jnp.concatenate(
                    [piece[t, pl.ds(a, span, stride=rows), :] for piece in pieces], axis=0
                )
                for t in range(times)
            ],
            axis=1,
        )
        plane = mm(by3_ref[...], right3(plane))
        for t in range(times):
            vol[t].append(plane[:, t * z : (t + 1) * z])
    for t in range(times):
        flat = jnp.concatenate(vol[t], axis=0)
        out_ref[t] = mm(left3(flat), bz3_ref[...]).reshape(rows, y, z)


def backward_yz(pieces, by, bz, first, total, earlier):
    members = len(pieces)
    y, z = by.shape[0], bz.shape[0]
    steps, rows = pieces[0].shape[:2]
    a = rows * members // y
    more = [] if earlier is None else [earlier]
    return pl.pallas_call(
        backward_body,
        grid=(steps // 2,),
        in_specs=[whole(y, y), whole(z, z)]
        + [pl.BlockSpec((2, rows, z), lambda k: (k, 0, 0))] * members
        + [pl.BlockSpec(memory_space=pl.ANY)] * len(more),
        out_specs=pl.BlockSpec((2, a, y, z), lambda k: (k + first // 2, 0, 0, 0)),
        out_shape=array(total, a, y, z),
        input_output_aliases={2 + members: 0} if more else {},
        scratch_shapes=[
            pltpu.VMEM((y, y), f32),
            pltpu.VMEM((y, y), f32),
            pltpu.VMEM((y, 3 * y), bf16),
            pltpu.VMEM((3 * z, z), bf16),
        ],
        compiler_params=params(),
        cost_estimate=cost(6 * steps * a * y * z * (y + z), 8 * steps * a * y * z),
        name="backward_yz",
    )(by, bz, *pieces, *more)


def length(steps_ref, at):
    total = steps_ref.shape[0]
    here = steps_ref[jnp.minimum(at, total - 1)] / total
    return jnp.where(at < total, here, 0.0)


def row_terms(eigen, steps_ref, at):
    now, then = length(steps_ref, at), length(steps_ref, at + 1)
    closing = jnp.where(at == steps_ref.shape[0] - 1, 0.5, 0.0)
    main = eigen * ((now + then) / 3.0) + closing
    sub = eigen * (now / 6.0) - 0.5
    sup = eigen * (then / 6.0) + 0.5
    return main, sub, sup


def mode_sums(ex_ref, ey_ref, ez_ref, j):
    x, z = ex_ref.shape[1], ez_ref.shape[1]
    along_x = jnp.broadcast_to(ex_ref[...], (z, x)).T
    return (along_x + ey_ref[j]) + ez_ref[...]


def fill_sums(ex_ref, ey_ref, ez_ref, sums_ref):
    x, members = ex_ref.shape[1], len(PEERS)
    span = ey_ref.shape[0] // members
    member = lax.axis_index("gx")
    for j in range(span):
        sums_ref[j * x : (j + 1) * x] = mode_sums(ex_ref, ey_ref, ez_ref, member * span + j)


def reduced_body(rows, steps_ref, ex_ref, ey_ref, ez_ref, cl_ref, e_ref, a_ref, k_ref, b_ref, q_ref, sums_ref):
    count, share = cl_ref.shape[:2]
    x, span = ex_ref.shape[1], ey_ref.shape[0] // len(PEERS)
    first = lax.axis_index("ta") * share
    sums_ref[...] = mode_sums(ex_ref, ey_ref, ez_ref, lax.axis_index("gx") * span + first // x)
    eigen = sums_ref[pl.ds(pl.multiple_of(lax.rem(first, x), share), share), :]

    def block(j, carry):
        inverses, subs, ratios = [], [], []
        for k in range(rows):
            main, sub, sup = row_terms(eigen, steps_ref, j * rows + k)
            inverse = 1.0 / (main - sub * ratios[-1] if k else main)
            inverses.append(inverse)
            subs.append(sub)
            ratios.append(sup * inverse)
        front = subs[0] * inverses[0]
        fronts = [front]
        for k in range(1, rows):
            front = -(subs[k] * inverses[k]) * front
            fronts.append(front)
        last = ratios[rows - 1]
        low = fronts[rows - 1]
        cl_ref[j] = low
        e_ref[j] = last
        for k in reversed(range(rows - 1)):
            low = fronts[k] - ratios[k] * low
            last = -ratios[k] * last
        a_ref[j] = low
        b_ref[j] = last
        return carry

    lax.fori_loop(0, count, block, 0, unroll=4)

    def sweep(j, q_before):
        v_last, w_last, v_first, w_first = cl_ref[j], e_ref[j], a_ref[j], b_ref[j]
        scale = 1.0 / (1.0 - v_first * q_before)
        back = w_first * scale
        q_now = w_last + v_last * q_before * back
        e_now = v_last * scale
        cl_ref[j] = e_now * q_before
        e_ref[j] = e_now
        a_ref[j] = scale
        k_ref[j] = v_first * scale
        b_ref[j] = back
        q_ref[j] = q_now
        return q_now

    lax.fori_loop(0, count, sweep, jnp.zeros_like(eigen))


def reduced_terms(steps, sums, count, rows, share):
    x, z = sums[0].shape[1], sums[2].shape[1]
    return pl.pallas_call(
        partial(reduced_body, rows),
        in_specs=[SMEM, VMEM, SMEM, VMEM],
        out_specs=[VMEM] * 6,
        out_shape=[array(count, share, z)] * 6,
        scratch_shapes=[pltpu.VMEM((x, z), f32)],
        compiler_params=params(),
        cost_estimate=cost(40 * rows * count * share * z, 24 * count * share * z),
        name="reduced_terms",
    )(steps, *sums)


def interface_body(g_ref, cl_ref, e_ref, a_ref, k_ref, b_ref, q_ref, out_ref, fh_ref):
    count = g_ref.shape[0]
    zero = jnp.zeros(g_ref.shape[2:], f32)

    def down(j, before):
        first, last = g_ref[j, 0], g_ref[j, 1]
        out_ref[j, 0] = before
        fh_ref[j] = a_ref[j] * first - k_ref[j] * before
        return (last + cl_ref[j] * first) - e_ref[j] * before

    lax.fori_loop(0, count, down, zero, unroll=8)

    def up(i, after):
        j = count - 1 - i
        out_ref[j, 1] = after

        @pl.when(j < count - 1)
        def _():
            out_ref[j + 1, 0] = out_ref[j + 1, 0] - q_ref[j] * after

        return fh_ref[j] - b_ref[j] * after

    lax.fori_loop(0, count, up, zero, unroll=8)


def interface_solve(g, terms):
    return pl.pallas_call(
        interface_body,
        in_specs=[VMEM] * 7,
        out_specs=VMEM,
        out_shape=array(*g.shape),
        scratch_shapes=[pltpu.VMEM(g.shape[:1] + g.shape[2:], f32)],
        compiler_params=params(),
        cost_estimate=cost(6 * g.size, 20 * g.size),
        name="interface_solve",
    )(g, *terms)


def eliminate_body(first, total, steps_ref, ex_ref, ey_ref, ez_ref, bx_ref, *refs):
    pieces, refs = refs[: len(PEERS)], refs[len(PEERS) :]
    earlier, refs = (refs[:2], refs[2:]) if first else ((), refs)
    closes = first + pl.num_programs(0) == total
    g_ref, ratio_ref, refs = refs[0], refs[1], refs[2:]
    ends_ref, refs = (refs[0], refs[1:]) if len(refs) == 4 else (None, refs)
    sums_ref, rows_ref, bx3_ref = refs
    step = pl.program_id(0)
    modes, lanes = g_ref.shape[1:]
    x = bx_ref.shape[0]
    span = x // len(pieces)
    t = step + first

    @pl.when(step == 0)
    def _():
        gather_rows(bx_ref, rows_ref, -1)
        bx3_ref[...] = left3(rows_ref[...].T)
        fill_sums(ex_ref, ey_ref, ez_ref, sums_ref)
        if first:
            g_ref[:first] = earlier[0][...]
            ratio_ref[:first] = earlier[1][...]

    spectral = []
    for j in range(0, modes // x, 2):
        plane = jnp.concatenate(
            [
                jnp.concatenate([piece[0, i * span : (i + 1) * span, :] for piece in pieces], axis=0)
                for i in (j, j + 1)
            ],
            axis=1,
        )
        plane = mm(bx3_ref[...], right3(plane))
        spectral += [plane[:, :lanes], plane[:, lanes:]]
    spectral = jnp.concatenate(spectral, axis=0)
    main, sub, sup = row_terms(sums_ref[...], steps_ref, lax.axis_index("ta") * total + t)

    def begin():
        inverse = 1.0 / main
        ratio_ref[t] = sup * inverse
        g_ref[t] = spectral * inverse

    def follow():
        inverse = 1.0 / (main - sub * ratio_ref[t - 1])
        ratio_ref[t] = sup * inverse
        g_ref[t] = (spectral - sub * g_ref[t - 1]) * inverse

    if first:
        follow()
    else:
        pl.when(step == 0)(begin)
        pl.when(step > 0)(follow)

    if ends_ref is not None:

        @pl.when(t == total - 1)
        def _():
            split_shape = (ends_ref.shape[0], modes // ends_ref.shape[0], lanes)
            now = g_ref[total - 1]
            ends_ref[:, 1] = now.reshape(split_shape)
            for k in reversed(range(total - 1)):
                now = g_ref[k] - ratio_ref[k] * now
                g_ref[k] = now
            ends_ref[:, 0] = now.reshape(split_shape)


def eliminate(pieces, sums, bx, steps, count, first, total, earlier):
    n, rows, z = pieces[0].shape
    x = bx.shape[0]
    modes = rows * len(pieces)
    last = first + n == total
    out = array(first + n, modes, z)
    outs = [out] + ([array(count, 2, modes // count, z)] if last else [out])
    scratch = [
        pltpu.VMEM((modes, z), f32),
        pltpu.VMEM((x, x), f32),
        pltpu.VMEM((x, 3 * x), bf16),
    ]

    def kernel(*refs):
        if last:
            at = len(refs) - 4
            refs = refs[: at - 1] + (refs[at], refs[at - 1]) + refs[at + 1 :]
        eliminate_body(first, total, *refs)

    return pl.pallas_call(
        kernel,
        grid=(n,),
        in_specs=[SMEM, whole(1, x), SMEM, whole(1, z), whole(x, x)]
        + [pl.BlockSpec((1, rows, z), lambda k: (k, 0, 0))] * len(pieces)
        + [whole(*e.shape) for e in earlier],
        out_specs=[whole(*o.shape) for o in outs],
        out_shape=outs,
        scratch_shapes=([pltpu.VMEM(out.shape, f32)] if last else []) + scratch,
        compiler_params=params(),
        cost_estimate=cost(6 * n * modes * x * z, 8 * n * modes * z),
        name="eliminate",
    )(steps, *sums, bx, *pieces, *earlier)


def return_body(first, total, steps_ref, ex_ref, ey_ref, ez_ref, bx_ref, *refs):
    members = len(PEERS)
    given, refs = (refs[:1], refs[1:]) if first else (refs[:2], refs[2:])
    outs, refs = refs[:members], refs[members:]
    sol_ref, refs = (given[0], refs) if first else (refs[0], refs[1:])
    step = pl.program_id(0)
    x, lanes = bx_ref.shape[0], ez_ref.shape[1]
    span = x // members
    rows_ref, bx3_ref = refs[-2:]

    @pl.when(step == 0)
    def _():
        gather_rows(bx_ref, rows_ref, 1)
        bx3_ref[...] = left3(rows_ref[...])

    if not first:
        g_ref, ends_ref = given
        sums_ref = refs[0]
        modes = g_ref.shape[1]

        @pl.when(step == 0)
        def _():
            fill_sums(ex_ref, ey_ref, ez_ref, sums_ref)
            eigen = sums_ref[...]
            begin = lax.axis_index("ta") * total
            before = ends_ref[:, 0].reshape(modes, lanes)
            after = ends_ref[:, 1].reshape(modes, lanes)
            ratios, values = [], []
            for k in range(total):
                main, sub, sup = row_terms(eigen, steps_ref, begin + k)
                inverse = 1.0 / (main - sub * ratios[-1] if k else main)
                ratios.append(sup * inverse)
                value = -(sub * inverse) * (values[-1] if k else before)
                if k == total - 1:
                    value = value - ratios[-1] * after
                values.append(value)
            now = values[total - 1]
            sol_ref[total - 1] = g_ref[total - 1] + now
            for k in reversed(range(total - 1)):
                now = values[k] - ratios[k] * now
                sol_ref[k] = g_ref[k] + now

    for j in range(0, sol_ref.shape[1] // x, 2):
        plane = jnp.concatenate(
            [sol_ref[step + first, i * x : (i + 1) * x, :] for i in (j, j + 1)], axis=1
        )
        plane = mm(bx3_ref[...], right3(plane))
        for k, out in enumerate(outs):
            for i in (0, 1):
                out[0, (j + i) * span : (j + i + 1) * span, :] = plane[
                    k * span : (k + 1) * span, i * lanes : (i + 1) * lanes
                ]


def return_x(given, sums, bx, steps, first, n):
    total, modes, z = given[0].shape
    x, members = bx.shape[0], len(PEERS)
    rows = modes // members
    whole_sol = n == total
    outs = [array(n, rows, z)] * members
    out_specs = [pl.BlockSpec((1, rows, z), lambda k: (k, 0, 0))] * members
    scratch = [pltpu.VMEM((x, x), f32), pltpu.VMEM((x, 3 * x), bf16)]
    if not first:
        scratch = [pltpu.VMEM((modes, z), f32)] + scratch
        if whole_sol:
            scratch = [pltpu.VMEM((total, modes, z), f32)] + scratch
        else:
            outs, out_specs = outs + [array(total, modes, z)], out_specs + [whole(total, modes, z)]
    return pl.pallas_call(
        partial(return_body, first, total),
        grid=(n,),
        in_specs=[SMEM, whole(1, x), SMEM, whole(1, z), whole(x, x)]
        + [whole(*g.shape) for g in given],
        out_specs=out_specs,
        out_shape=outs,
        scratch_shapes=scratch,
        compiler_params=params(),
        cost_estimate=cost(6 * n * modes * x * z, 8 * n * modes * z),
        name="return_x",
    )(steps, *sums, bx, *given)


CHUNKS = 1


def local(right_side, basis_x, basis_y, basis_z, eig_x, eig_y, eig_z, steps):
    rows = right_side.shape[0]
    count = lax.axis_size("ta")
    sums = (eig_x[None, :], eig_y, eig_z[None, :])
    n = rows // CHUNKS
    share = basis_x.shape[0] * basis_y.shape[0] // (lax.axis_size("gx") * count)
    right_side = pltpu.with_memory_space_constraint(right_side, pltpu.HBM)

    sent = [forward_yz(right_side, basis_y, basis_z, first, n) for first in range(0, rows, n)]
    state = ()
    for c, pieces in enumerate(sent):
        state = eliminate(exchange(pieces), sums, basis_x, steps, count, c * n, rows, state)
    g, ends = state
    terms = reduced_terms(steps, sums, count, rows, share)
    ends = lax.all_to_all(ends, "ta", 0, 0, tiled=True)
    ends = interface_solve(ends, terms)
    ends = lax.all_to_all(ends, "ta", 0, 0, tiled=True)
    given, sent = (g, ends), []
    for c in range(CHUNKS):
        pieces = return_x(given, sums, basis_x, steps, c * n, n)
        given = given if c else pieces[len(PEERS) :]
        sent.append(pieces[: len(PEERS)])
    result = None
    for c, pieces in enumerate(sent):
        result = backward_yz(exchange(pieces), basis_y, basis_z, c * n, rows, result)
    return result


def solution(mesh):
    return jax.shard_map(
        local,
        mesh=mesh,
        in_specs=(P("ta", "gx", None, None), P(), P(), P(), P(), P(), P(), P()),
        out_specs=P("ta", "gx", None, None),
        check_vma=False,
    )
```

time: 153 us -> 127 us (0.83)
  waiting for transfers between devices: 56.3 us -> 36.4 us
  starting transfers between devices: 25.3 us -> 42.9 us
  local copies, waits for them, and re-layouts: 20.1 us -> 6.57 us
  Pallas kernels: 29.2 us -> 18.8 us
    all_to_all x2 -> x0, waiting for transfers between devices: 49.1 us -> none  [the longest x1 26.3 us: local(): cell = lax.all_to_all(cell, 'gx', 0, 0, tiled=True)]
    ppermute x0 -> x14, starting transfers between devices: none -> 31.8 us  [exchange(): moved.append(lax.ppermute(pieces[k], 'gx', pairs))]
    ppermute x0 -> x14, waiting for transfers between devices: none -> 27.1 us  [exchange(): moved.append(lax.ppermute(pieces[k], 'gx', pairs))]
    all_to_all x2 -> x0, starting transfers between devices: 15.1 us -> none  [the longest x1 8.19 us: local(): cell = lax.all_to_all(cell, 'gx', 0, 0, tiled=True)]
    unnamed x58 -> x30, local copies, waits for them, and re-layouts: 19.7 us -> 6.57 us
    pallas_call x7 -> x6, Pallas kernels: 29.2 us -> 18.8 us  [the longest x1 4.43 us: eliminate(): pl.pallas_call(kernel, grid=(n,), in_specs=[SMEM, whole(1, x), SMEM, whol...]
    all_to_all x1, waiting for transfers between devices: 7.22 us -> 9.29 us  [local(): ends = lax.all_to_all(ends, 'ta', 0, 0, tiled=True)]
  transfers between devices with their start and end apart: 3 -> 15, of which waited for: 3 -> 8; matrix products, arithmetic and copies ran while one was open for 0% -> 0% of each run, Pallas kernels for 3% -> 2%
where the time goes in v2:
time: 127 us
  starting transfers between devices  42.9 us (34%)
  waiting for transfers between devices  36.4 us (29%)
  blocking collectives  22.1 us (17%)
  Pallas kernels  18.8 us (15%)
  local copies, waits for them, and re-layouts  6.57 us (5%)
    ppermute x14, starting transfers between devices, exchange(): moved.append(lax.ppermute(pieces[k], 'gx', pairs))  31.8 us
    ppermute x14, waiting for transfers between devices, exchange(): moved.append(lax.ppermute(pieces[k], 'gx', pairs))  27.1 us
    all_to_all x1, blocking collectives, local(): ends = lax.all_to_all(ends, 'ta', 0, 0, tiled=True)  22.1 us
    all_to_all x1, starting transfers between devices, local(): ends = lax.all_to_all(ends, 'ta', 0, 0, tiled=True)  11.1 us
    all_to_all x1, waiting for transfers between devices, local(): ends = lax.all_to_all(ends, 'ta', 0, 0, tiled=True)  9.29 us
    unnamed x30, local copies, waits for them, and re-layouts  6.57 us
    pallas_call x1, Pallas kernels, eliminate(): pl.pallas_call(kernel, grid=(n,), in_specs=[SMEM, whole(1, x), SMEM, whol...  4.43 us
    pallas_call x1, Pallas kernels, forward_yz(): pl.pallas_call(forward_body, grid=(steps // 2,), in_specs=[pl.BlockSpec((...  4.11 us
  transfers between devices with their start and end apart: 15, of which 8 were waited for; matrix products, arithmetic and copies ran while one was open for 0% of the time, Pallas kernels for 2%

profile of v2, /device:TPU:1, one launch (start us, length us, event | category | flops | bytes accessed | tf_op | source)
XLA Modules:
  0.0 127.0 jit_solution(1190038396958794593)
XLA Ops:
  0.0 0.8 copy-done.7
  0.8 0.8 copy-done.9
  1.6 0.0 copy-start.14
  1.6 4.1 %forward_yz.1 = (f32[8,64,128]{2,1,0:T(8,128)S(1)}, f32[8,64,128]{2,1,0:T(8,128)S(1)}, f32[8,64,128]{2,1,0:T(8,128)S(1)}, f32[8,64,128]{2,1,0:T(8,128)S(1)}, f32...) custom-call(f32[8,8,64,128]{3,2,1,0:T(8,128)} %x_ref.1, ...), custom_call_target="tpu_custom_call" | custom-call | flops 603979776 | bytes 4194304 | tf_op jit(solution)/shard_map/forward_yz/pallas_call | solution.py:102
  5.7 3.7 %collective-permute-start = (f32[8,64,128]{2,1,0:T(8,128)S(1)}, f32[8,64,128]{2,1,0:T(8,128)S(1)}, u32[]{:S(2)}, u32[]{:S(2)}) collective-permute-start(f32[8,64,128]{2,1,0:T(8,128)S(1)} %get-tuple-element.30), channel_id=1, source_target_pairs={{0,4},{1,5},{2,6},{3,7},{4,0},{5,1},{6,2},{7,3},{8,12},{9,13},{10,... | collective-permute-start | bytes 786440 | tf_op jit(solution)/shard_map/ppermute | solution.py:32
  9.4 2.8 %collective-permute-start.1 = (f32[8,64,128]{2,1,0:T(8,128)S(1)}, f32[8,64,128]{2,1,0:T(8,128)S(1)}, u32[]{:S(2)}, u32[]{:S(2)}) collective-permute-start(f32[8,64,128]{2,1,0:T(8,128)S(1)} %get-tuple-element.31), channel_id=1, source_target_pairs={{0,5},{1,4},{2,7},{3,6},{4,1},{5,0},{6,3},{7,2},{8,13},{9,12},{10,... | collective-permute-start | bytes 786440 | tf_op jit(solution)/shard_map/ppermute | solution.py:32
  12.2 0.0 collective-permute-start.2
  12.2 2.7 %collective-permute-start.3 = (f32[8,64,128]{2,1,0:T(8,128)S(1)}, f32[8,64,128]{2,1,0:T(8,128)S(1)}, u32[]{:S(2)}, u32[]{:S(2)}) collective-permute-start(f32[8,64,128]{2,1,0:T(8,128)S(1)} %get-tuple-element.33), channel_id=1, source_target_pairs={{0,6},{1,7},{2,0},{3,1},{4,2},{5,3},{6,4},{7,5},{8,14},{9,15},{10,... | collective-permute-start | bytes 786440 | tf_op jit(solution)/shard_map/ppermute | solution.py:32
  14.9 0.0 collective-permute-start.4
  14.9 0.0 collective-permute-done.refs_6_
  14.9 5.6 %collective-permute-start.5 = (f32[8,64,128]{2,1,0:T(8,128)S(1)}, f32[8,64,128]{2,1,0:T(8,128)S(1)}, u32[]{:S(2)}, u32[]{:S(2)}) collective-permute-start(f32[8,64,128]{2,1,0:T(8,128)S(1)} %get-tuple-element.35), channel_id=1, source_target_pairs={{0,7},{1,6},{2,1},{3,0},{4,3},{5,2},{6,5},{7,4},{8,15},{9,14},{10,... | collective-permute-start | bytes 786440 | tf_op jit(solution)/shard_map/ppermute | solution.py:32
  20.5 3.6 %collective-permute-done.1.refs_7_ = f32[8,64,128]{2,1,0:T(8,128)S(1)} collective-permute-done((f32[8,64,128]{2,1,0:T(8,128)S(1)}, f32[8,64,128]{2,1,0:T(8,128)S(1)}, u32[]{:S(2)}, u32[]{:S(2)}) %collective-permute-start.1) | collective-permute-done | bytes 262176 | tf_op jit(solution)/shard_map/ppermute | solution.py:32
  24.0 0.0 collective-permute-start.6
  24.0 3.6 %collective-permute-done.2.refs_8_ = f32[8,64,128]{2,1,0:T(8,128)S(1)} collective-permute-done((f32[8,64,128]{2,1,0:T(8,128)S(1)}, f32[8,64,128]{2,1,0:T(8,128)S(1)}, u32[]{:S(2)}, u32[]{:S(2)}) %collective-permute-start.2) | collective-permute-done | bytes 262176 | tf_op jit(solution)/shard_map/ppermute | solution.py:32
  27.7 0.0 collective-permute-done.3.refs_9_
  27.7 5.6 %collective-permute-done.4.refs_10_ = f32[8,64,128]{2,1,0:T(8,128)S(1)} collective-permute-done((f32[8,64,128]{2,1,0:T(8,128)S(1)}, f32[8,64,128]{2,1,0:T(8,128)S(1)}, u32[]{:S(2)}, u32[]{:S(2)}) %collective-permute-start.4) | collective-permute-done | bytes 262176 | tf_op jit(solution)/shard_map/ppermute | solution.py:32
  33.3 0.1 collective-permute-done.5.refs_11_
  33.4 0.0 collective-permute-done.6.refs_12_
  33.4 4.4 %eliminate.1 = (f32[8,512,128]{2,1,0:T(8,128)S(1)}, f32[32,2,16,128]{3,2,1,0:T(8,128)}) custom-call(f32[256]{0:T(256)S(1)} %copy-done.11, f32[1,64]{1,0:T(1,128)S(1)} %bitcast.2, f32[64]{0:T(128)S(1)} %copy-done.13, f32[1,128]{1,0:T(1,128)S(1)} %bitcast.5, f32[64,64]{1,0:T(8,128)S(1)} %copy-done.6, f32[8,64,128]{2,1,0:T(8,128)S(1)} %get-tuple-element.29.refs_5_, ...), custom_call_target="tpu_custom_call" | custom-call | flops 201326592 | bytes 4194304 | tf_op jit(solution)/shard_map/eliminate/pallas_call | solution.py:397
  37.9 11.1 %all-to-all-start = ((f32[32,2,16,128]{3,2,1,0:T(8,128)}), f32[32,2,16,128]{3,2,1,0:T(8,128)S(1)}, u32[]{:S(2)}, u32[]{:S(2)}) async-start(f32[32,2,16,128]{3,2,1,0:T(8,128)} %get-tuple-element.38), calls=%async_computation | async-start | bytes 1048576 | tf_op jit(solution)/shard_map/all_to_all | solution.py:511
  49.0 2.7 %reduced_terms.1 = (f32[32,16,128]{2,1,0:T(8,128)S(1)}, f32[32,16,128]{2,1,0:T(8,128)S(1)}, f32[32,16,128]{2,1,0:T(8,128)S(1)}, f32[32,16,128]{2,1,0:T(8,128)S(1...) custom-call(f32[256]{0:T(256)S(1)} %copy-done.11, f32[1,64]{1,0:T(1,128)S(1)} %bitcast.3, f32[64]{0:T(128)S(1)} %copy-done.13, ...), custom_call_target="tpu_custom_call" | custom-call | flops 20971520 | bytes 1572864 | tf_op jit(solution)/shard_map/reduced_terms/pallas_call | solution.py:263
  51.8 0.7 copy-done
  52.4 0.7 copy-done.2
  53.1 0.7 copy-done.4
  53.9 9.3 %all-to-all-done.g_ref = f32[32,2,16,128]{3,2,1,0:T(8,128)S(1)} async-done(((f32[32,2,16,128]{3,2,1,0:T(8,128)}), f32[32,2,16,128]{3,2,1,0:T(8,128)S(1)}, u32[]{:S(2)}, u32[]{:S(2)}) %all-to-all-start) | async-done | bytes 524320 | tf_op jit(solution)/shard_map/all_to_all | solution.py:511
  63.1 0.9 copy-done.1
  64.1 0.9 copy-done.3
  65.0 0.9 copy-done.5
  66.0 0.3 interface_solve.1
  66.3 0.0 copy-start.8
  66.4 0.0 copy-start.10
  66.4 22.1 %all_to_all.10.refs_1_ = f32[32,2,16,128]{3,2,1,0:T(8,128)S(1)} all-to-all(f32[32,2,16,128]{3,2,1,0:T(8,128)S(1)} %interface_solve.1), channel_id=1, replica_groups=mesh['ta'=32,'gx'=8] {'ta'}, dimensions={0} | all-to-all | bytes 1048576 | tf_op jit(solution)/shard_map/all_to_all | solution.py:513
  88.5 3.6 %return_x.1 = (f32[8,64,128]{2,1,0:T(8,128)S(1)}, f32[8,64,128]{2,1,0:T(8,128)S(1)}, f32[8,64,128]{2,1,0:T(8,128)S(1)}, f32[8,64,128]{2,1,0:T(8,128)S(1)}, f32[8...) custom-call(f32[256]{0:T(256)S(1)} %copy-done.11, ...), custom_call_target="tpu_custom_call" | custom-call | flops 201326592 | bytes 4194304 | tf_op jit(solution)/shard_map/return_x/pallas_call | solution.py:480
  92.1 2.5 %collective-permute-start.10 = (f32[8,64,128]{2,1,0:T(8,128)S(1)}, f32[8,64,128]{2,1,0:T(8,128)S(1)}, u32[]{:S(2)}, u32[]{:S(2)}) collective-permute-start(f32[8,64,128]{2,1,0:T(8,128)S(1)} %get-tuple-element.49), channel_id=1, source_target_pairs={{0,6},{1,7},{2,0},{3,1},{4,2},{5,3},{6,4},{7,5},{8,14},{9,15},{10,... | collective-permute-start | bytes 786440 | tf_op jit(solution)/shard_map/ppermute | solution.py:32
  94.6 3.2 %collective-permute-start.11 = (f32[8,64,128]{2,1,0:T(8,128)S(1)}, f32[8,64,128]{2,1,0:T(8,128)S(1)}, u32[]{:S(2)}, u32[]{:S(2)}) collective-permute-start(f32[8,64,128]{2,1,0:T(8,128)S(1)} %get-tuple-element.50), channel_id=1, source_target_pairs={{0,3},{1,2},{2,5},{3,4},{4,7},{5,6},{6,1},{7,0},{8,11},{9,10},{10,... | collective-permute-start | bytes 786440 | tf_op jit(solution)/shard_map/ppermute | solution.py:32
  97.8 1.6 %collective-permute-start.12 = (f32[8,64,128]{2,1,0:T(8,128)S(1)}, f32[8,64,128]{2,1,0:T(8,128)S(1)}, u32[]{:S(2)}, u32[]{:S(2)}) collective-permute-start(f32[8,64,128]{2,1,0:T(8,128)S(1)} %get-tuple-element.51), channel_id=1, source_target_pairs={{0,7},{1,6},{2,1},{3,0},{4,3},{5,2},{6,5},{7,4},{8,15},{9,14},{10,... | collective-permute-start | bytes 786440 | tf_op jit(solution)/shard_map/ppermute | solution.py:32
  99.4 2.4 %collective-permute-start.13 = (f32[8,64,128]{2,1,0:T(8,128)S(1)}, f32[8,64,128]{2,1,0:T(8,128)S(1)}, u32[]{:S(2)}, u32[]{:S(2)}) collective-permute-start(f32[8,64,128]{2,1,0:T(8,128)S(1)} %get-tuple-element.52), channel_id=1, source_target_pairs={{0,1},{1,0},{2,3},{3,2},{4,5},{5,4},{6,7},{7,6},{8,9},{9,8},{10,11... | collective-permute-start | bytes 786440 | tf_op jit(solution)/shard_map/ppermute | solution.py:32
  101.9 0.0 collective-permute-start.7
  101.9 0.0 collective-permute-done.10.refs_4_
  101.9 4.3 %collective-permute-start.8 = (f32[8,64,128]{2,1,0:T(8,128)S(1)}, f32[8,64,128]{2,1,0:T(8,128)S(1)}, u32[]{:S(2)}, u32[]{:S(2)}) collective-permute-start(f32[8,64,128]{2,1,0:T(8,128)S(1)} %get-tuple-element.47), channel_id=1, source_target_pairs={{0,5},{1,4},{2,7},{3,6},{4,1},{5,0},{6,3},{7,2},{8,13},{9,12},{10,... | collective-permute-start | bytes 786440 | tf_op jit(solution)/shard_map/ppermute | solution.py:32
  106.2 0.0 collective-permute-done.11.refs_5_
  106.2 2.9 %collective-permute-start.9 = (f32[8,64,128]{2,1,0:T(8,128)S(1)}, f32[8,64,128]{2,1,0:T(8,128)S(1)}, u32[]{:S(2)}, u32[]{:S(2)}) collective-permute-start(f32[8,64,128]{2,1,0:T(8,128)S(1)} %get-tuple-element.48), channel_id=1, source_target_pairs={{0,2},{1,3},{2,4},{3,5},{4,6},{5,7},{6,0},{7,1},{8,10},{9,11},{10,... | collective-permute-start | bytes 786440 | tf_op jit(solution)/shard_map/ppermute | solution.py:32
  109.2 0.0 collective-permute-done.12.refs_6_
  109.2 0.0 collective-permute-done.13.refs_7_
  109.2 2.9 %collective-permute-done.7.refs_1_ = f32[8,64,128]{2,1,0:T(8,128)S(1)} collective-permute-done((f32[8,64,128]{2,1,0:T(8,128)S(1)}, f32[8,64,128]{2,1,0:T(8,128)S(1)}, u32[]{:S(2)}, u32[]{:S(2)}) %collective-permute-start.7) | collective-permute-done | bytes 262176 | tf_op jit(solution)/shard_map/ppermute | solution.py:32
  112.1 5.6 %collective-permute-done.8.refs_2_ = f32[8,64,128]{2,1,0:T(8,128)S(1)} collective-permute-done((f32[8,64,128]{2,1,0:T(8,128)S(1)}, f32[8,64,128]{2,1,0:T(8,128)S(1)}, u32[]{:S(2)}, u32[]{:S(2)}) %collective-permute-start.8) | collective-permute-done | bytes 262176 | tf_op jit(solution)/shard_map/ppermute | solution.py:32
  117.7 5.7 %collective-permute-done.9.refs_3_ = f32[8,64,128]{2,1,0:T(8,128)S(1)} collective-permute-done((f32[8,64,128]{2,1,0:T(8,128)S(1)}, f32[8,64,128]{2,1,0:T(8,128)S(1)}, u32[]{:S(2)}, u32[]{:S(2)}) %collective-permute-start.9) | collective-permute-done | bytes 262176 | tf_op jit(solution)/shard_map/ppermute | solution.py:32
  123.4 3.5 %backward_yz.1 = f32[8,8,64,128]{3,2,1,0:T(8,128)} custom-call(f32[64,64]{1,0:T(8,128)S(1)} %copy-done.10, f32[128,128]{1,0:T(8,128)S(1)} %copy-done.8, f32[8,64,128]{2,1,0:T(8,128)S(1)} %get-tuple-element.45.refs_0_, f32[8,64,128]{2,1,0:T(8,128)S(1)} %collective-permute-done.7.refs_1_, f32[8,64,128]{2,1,0:T(8,128)S(1)} %collective-permute-done.8.refs_2_, ...), custom_call_target="tpu_custom_call" | custom-call | flops 603979776 | bytes 4194304 | tf_op jit(solution)/shard_map/backward_yz/pallas_call | solution.py:161
  (19 shorter events, 0.0 us)
Async XLA Ops:
  0.0 0.8 copy-start.7
  0.8 0.8 copy-start.9
  1.6 31.8 %copy-start.6 = (f32[64,64]{1,0:T(8,128)S(1)}, f32[64,64]{1,0:T(8,128)}, u32[]{:S(2)}) copy-start(f32[64,64]{1,0:T(8,128)} %bx_ref.1) | copy-start | bytes 49156
  1.6 31.8 %copy-start.11 = (f32[256]{0:T(256)S(1)}, f32[256]{0:T(256)}, u32[]{:S(2)}) copy-start(f32[256]{0:T(256)} %steps_ref.3) | copy-start | bytes 3076
  1.6 31.8 %copy-start.12 = (f32[64]{0:T(128)S(1)}, f32[64]{0:T(128)}, u32[]{:S(2)}) copy-start(f32[64]{0:T(128)} %param.12) | copy-start | bytes 772
  1.6 31.8 %copy-start.13 = (f32[64]{0:T(128)S(1)}, f32[64]{0:T(128)}, u32[]{:S(2)}) copy-start(f32[64]{0:T(128)} %ey_ref.3) | copy-start | bytes 772
  1.6 31.8 %copy-start.14 = (f32[128]{0:T(128)S(1)}, f32[128]{0:T(128)}, u32[]{:S(2)}) copy-start(f32[128]{0:T(128)} %param.14) | copy-start | bytes 1540
  5.7 9.1 %collective-permute-start = (f32[8,64,128]{2,1,0:T(8,128)S(1)}, f32[8,64,128]{2,1,0:T(8,128)S(1)}, u32[]{:S(2)}, u32[]{:S(2)}) collective-permute-start(f32[8,64,128]{2,1,0:T(8,128)S(1)} %get-tuple-element.30), channel_id=1, source_target_pairs={{0,4},{1,5},{2,6},{3,7},{4,0},{5,1},{6,2},{7,3},{8,12},{9,13},{10,... | collective-permute-start | bytes 786440 | tf_op jit(solution)/shard_map/ppermute | solution.py:32
  9.4 14.6 %collective-permute-start.1 = (f32[8,64,128]{2,1,0:T(8,128)S(1)}, f32[8,64,128]{2,1,0:T(8,128)S(1)}, u32[]{:S(2)}, u32[]{:S(2)}) collective-permute-start(f32[8,64,128]{2,1,0:T(8,128)S(1)} %get-tuple-element.31), channel_id=1, source_target_pairs={{0,5},{1,4},{2,7},{3,6},{4,1},{5,0},{6,3},{7,2},{8,13},{9,12},{10,... | collective-permute-start | bytes 786440 | tf_op jit(solution)/shard_map/ppermute | solution.py:32
  12.2 15.5 %collective-permute-start.2 = (f32[8,64,128]{2,1,0:T(8,128)S(1)}, f32[8,64,128]{2,1,0:T(8,128)S(1)}, u32[]{:S(2)}, u32[]{:S(2)}) collective-permute-start(f32[8,64,128]{2,1,0:T(8,128)S(1)} %get-tuple-element.32), channel_id=1, source_target_pairs={{0,2},{1,3},{2,4},{3,5},{4,6},{5,7},{6,0},{7,1},{8,10},{9,11},{10,... | collective-permute-start | bytes 786440 | tf_op jit(solution)/shard_map/ppermute | solution.py:32
  12.2 15.5 %collective-permute-start.3 = (f32[8,64,128]{2,1,0:T(8,128)S(1)}, f32[8,64,128]{2,1,0:T(8,128)S(1)}, u32[]{:S(2)}, u32[]{:S(2)}) collective-permute-start(f32[8,64,128]{2,1,0:T(8,128)S(1)} %get-tuple-element.33), channel_id=1, source_target_pairs={{0,6},{1,7},{2,0},{3,1},{4,2},{5,3},{6,4},{7,5},{8,14},{9,15},{10,... | collective-permute-start | bytes 786440 | tf_op jit(solution)/shard_map/ppermute | solution.py:32
  14.9 18.4 %collective-permute-start.4 = (f32[8,64,128]{2,1,0:T(8,128)S(1)}, f32[8,64,128]{2,1,0:T(8,128)S(1)}, u32[]{:S(2)}, u32[]{:S(2)}) collective-permute-start(f32[8,64,128]{2,1,0:T(8,128)S(1)} %get-tuple-element.34), channel_id=1, source_target_pairs={{0,3},{1,2},{2,5},{3,4},{4,7},{5,6},{6,1},{7,0},{8,11},{9,10},{10,... | collective-permute-start | bytes 786440 | tf_op jit(solution)/shard_map/ppermute | solution.py:32
  14.9 18.5 %collective-permute-start.5 = (f32[8,64,128]{2,1,0:T(8,128)S(1)}, f32[8,64,128]{2,1,0:T(8,128)S(1)}, u32[]{:S(2)}, u32[]{:S(2)}) collective-permute-start(f32[8,64,128]{2,1,0:T(8,128)S(1)} %get-tuple-element.35), channel_id=1, source_target_pairs={{0,7},{1,6},{2,1},{3,0},{4,3},{5,2},{6,5},{7,4},{8,15},{9,14},{10,... | collective-permute-start | bytes 786440 | tf_op jit(solution)/shard_map/ppermute | solution.py:32
  24.0 9.4 %collective-permute-start.6 = (f32[8,64,128]{2,1,0:T(8,128)S(1)}, f32[8,64,128]{2,1,0:T(8,128)S(1)}, u32[]{:S(2)}, u32[]{:S(2)}) collective-permute-start(f32[8,64,128]{2,1,0:T(8,128)S(1)} %get-tuple-element.36), channel_id=1, source_target_pairs={{0,1},{1,0},{2,3},{3,2},{4,5},{5,4},{6,7},{7,6},{8,9},{9,8},{10,11... | collective-permute-start | bytes 786440 | tf_op jit(solution)/shard_map/ppermute | solution.py:32
  37.9 25.3 %all-to-all-start = ((f32[32,2,16,128]{3,2,1,0:T(8,128)}), f32[32,2,16,128]{3,2,1,0:T(8,128)S(1)}, u32[]{:S(2)}, u32[]{:S(2)}) async-start(f32[32,2,16,128]{3,2,1,0:T(8,128)} %get-tuple-element.38), calls=%async_computation | async-start | bytes 1048576 | tf_op jit(solution)/shard_map/all_to_all | solution.py:511
  51.8 0.7 copy-start
  52.4 0.7 copy-start.2
  53.1 0.7 copy-start.4
  63.1 1.0 copy-start.1
  64.1 0.9 copy-start.3
  65.0 0.9 copy-start.5
  66.3 57.0 %copy-start.8 = (f32[128,128]{1,0:T(8,128)S(1)}, f32[128,128]{1,0:T(8,128)}, u32[]{:S(2)}) copy-start(f32[128,128]{1,0:T(8,128)} %bz_ref.3) | copy-start | bytes 196612
  66.4 57.0 %copy-start.10 = (f32[64,64]{1,0:T(8,128)S(1)}, f32[64,64]{1,0:T(8,128)}, u32[]{:S(2)}) copy-start(f32[64,64]{1,0:T(8,128)} %by_ref.3) | copy-start | bytes 49156
  92.1 9.8 %collective-permute-start.10 = (f32[8,64,128]{2,1,0:T(8,128)S(1)}, f32[8,64,128]{2,1,0:T(8,128)S(1)}, u32[]{:S(2)}, u32[]{:S(2)}) collective-permute-start(f32[8,64,128]{2,1,0:T(8,128)S(1)} %get-tuple-element.49), channel_id=1, source_target_pairs={{0,6},{1,7},{2,0},{3,1},{4,2},{5,3},{6,4},{7,5},{8,14},{9,15},{10,... | collective-permute-start | bytes 786440 | tf_op jit(solution)/shard_map/ppermute | solution.py:32
  94.6 11.6 %collective-permute-start.11 = (f32[8,64,128]{2,1,0:T(8,128)S(1)}, f32[8,64,128]{2,1,0:T(8,128)S(1)}, u32[]{:S(2)}, u32[]{:S(2)}) collective-permute-start(f32[8,64,128]{2,1,0:T(8,128)S(1)} %get-tuple-element.50), channel_id=1, source_target_pairs={{0,3},{1,2},{2,5},{3,4},{4,7},{5,6},{6,1},{7,0},{8,11},{9,10},{10,... | collective-permute-start | bytes 786440 | tf_op jit(solution)/shard_map/ppermute | solution.py:32
  97.8 11.3 %collective-permute-start.12 = (f32[8,64,128]{2,1,0:T(8,128)S(1)}, f32[8,64,128]{2,1,0:T(8,128)S(1)}, u32[]{:S(2)}, u32[]{:S(2)}) collective-permute-start(f32[8,64,128]{2,1,0:T(8,128)S(1)} %get-tuple-element.51), channel_id=1, source_target_pairs={{0,7},{1,6},{2,1},{3,0},{4,3},{5,2},{6,5},{7,4},{8,15},{9,14},{10,... | collective-permute-start | bytes 786440 | tf_op jit(solution)/shard_map/ppermute | solution.py:32
  99.4 9.7 %collective-permute-start.13 = (f32[8,64,128]{2,1,0:T(8,128)S(1)}, f32[8,64,128]{2,1,0:T(8,128)S(1)}, u32[]{:S(2)}, u32[]{:S(2)}) collective-permute-start(f32[8,64,128]{2,1,0:T(8,128)S(1)} %get-tuple-element.52), channel_id=1, source_target_pairs={{0,1},{1,0},{2,3},{3,2},{4,5},{5,4},{6,7},{7,6},{8,9},{9,8},{10,11... | collective-permute-start | bytes 786440 | tf_op jit(solution)/shard_map/ppermute | solution.py:32
  101.9 10.2 %collective-permute-start.7 = (f32[8,64,128]{2,1,0:T(8,128)S(1)}, f32[8,64,128]{2,1,0:T(8,128)S(1)}, u32[]{:S(2)}, u32[]{:S(2)}) collective-permute-start(f32[8,64,128]{2,1,0:T(8,128)S(1)} %get-tuple-element.46), channel_id=1, source_target_pairs={{0,4},{1,5},{2,6},{3,7},{4,0},{5,1},{6,2},{7,3},{8,12},{9,13},{10,... | collective-permute-start | bytes 786440 | tf_op jit(solution)/shard_map/ppermute | solution.py:32
  101.9 15.8 %collective-permute-start.8 = (f32[8,64,128]{2,1,0:T(8,128)S(1)}, f32[8,64,128]{2,1,0:T(8,128)S(1)}, u32[]{:S(2)}, u32[]{:S(2)}) collective-permute-start(f32[8,64,128]{2,1,0:T(8,128)S(1)} %get-tuple-element.47), channel_id=1, source_target_pairs={{0,5},{1,4},{2,7},{3,6},{4,1},{5,0},{6,3},{7,2},{8,13},{9,12},{10,... | collective-permute-start | bytes 786440 | tf_op jit(solution)/shard_map/ppermute | solution.py:32
  106.2 17.2 %collective-permute-start.9 = (f32[8,64,128]{2,1,0:T(8,128)S(1)}, f32[8,64,128]{2,1,0:T(8,128)S(1)}, u32[]{:S(2)}, u32[]{:S(2)}) collective-permute-start(f32[8,64,128]{2,1,0:T(8,128)S(1)} %get-tuple-element.48), channel_id=1, source_target_pairs={{0,2},{1,3},{2,4},{3,5},{4,6},{5,7},{6,0},{7,1},{8,10},{9,11},{10,... | collective-permute-start | bytes 786440 | tf_op jit(solution)/shard_map/ppermute | solution.py:32

commit v3 on v2

v3 whole, which is shorter than its diff:
```python
from functools import partial

import jax
import jax.numpy as jnp
from jax import lax
from jax.experimental import pallas as pl
from jax.experimental.pallas import tpu as pltpu
from jax.sharding import PartitionSpec as P

f32, bf16 = jnp.float32, jnp.bfloat16
params = partial(pltpu.CompilerParams, vmem_limit_bytes=24 * 2**20)
VMEM = pl.BlockSpec(memory_space=pltpu.VMEM)
SMEM = pl.BlockSpec(memory_space=pltpu.SMEM)

PEERS = ((0, 0), (2, 0), (2, 1), (1, 0), (3, 0), (1, 1), (3, 1), (0, 1))


def peer(member, members, place, sign):
    chips, core = place
    ring = members // 2
    far = lax.rem(member // 2 + (sign * chips) % ring, ring)
    own = lax.rem(member, 2)
    return far * 2 + (1 - own if core else own)


def exchange(pieces, peers):
    members = len(pieces)
    moved = [pieces[0]]
    for k in range(1, members):
        chips, core = peers[k]
        pairs = [(i, ((i // 2 + chips) * 2 + (i % 2 + core) % 2) % members) for i in range(members)]
        moved.append(lax.ppermute(pieces[k], "gx", pairs))
    return moved


def split(x):
    high = x.astype(bf16)
    return high, (x - high.astype(f32)).astype(bf16)


def left3(x):
    high, low = split(x)
    return jnp.concatenate([high, high, low], axis=1)


def right3(x):
    high, low = split(x)
    return jnp.concatenate([high, low, high], axis=0)


mm = partial(jnp.dot, preferred_element_type=f32)


def cost(flops, bytes_accessed):
    return pl.CostEstimate(flops=int(flops), bytes_accessed=int(bytes_accessed), transcendentals=0)


def whole(*shape):
    return pl.BlockSpec(shape, lambda k: (0,) * len(shape))


def array(*shape):
    return jax.ShapeDtypeStruct(shape, f32)


def gather_rows(source_ref, target_ref, peers, sign):
    members = len(peers)
    span = target_ref.shape[0] // members
    member = lax.axis_index("gx")
    for k, place in enumerate(peers):
        start = pl.multiple_of(peer(member, members, place, sign) * span, span)
        target_ref[k * span : (k + 1) * span] = source_ref[pl.ds(start, span), :]


def forward_body(x_ref, by_ref, bz_ref, *refs):
    outs, (turn_ref, rows_ref, by3_ref, bz3_ref) = refs[:-4], refs[-4:]
    times, rows, y, z = x_ref.shape
    span = y // len(outs)

    @pl.when(pl.program_id(0) == 0)
    def _():
        turn_ref[...] = by_ref[...].T
        gather_rows(turn_ref, rows_ref, PEERS, 1)
        by3_ref[...] = left3(rows_ref[...])
        bz3_ref[...] = right3(bz_ref[...])

    vol = [mm(left3(x_ref[t].reshape(rows * y, z)), bz3_ref[...]) for t in range(times)]
    for a in range(rows):
        plane = jnp.concatenate([v[a * y : (a + 1) * y] for v in vol], axis=1)
        plane = mm(by3_ref[...], right3(plane))
        for k, out in enumerate(outs):
            for t in range(times):
                out[t, pl.ds(a, span, stride=rows), :] = plane[
                    k * span : (k + 1) * span, t * z : (t + 1) * z
                ]


def forward_yz(x, by, bz):
    t, a, y, z = x.shape
    members = len(PEERS)
    rows = a * y // members
    return pl.pallas_call(
        forward_body,
        grid=(t // 2,),
        in_specs=[
            pl.BlockSpec((2, a, y, z), lambda k: (k, 0, 0, 0)),
            whole(y, y),
            whole(z, z),
        ],
        out_specs=[pl.BlockSpec((2, rows, z), lambda k: (k, 0, 0))] * members,
        out_shape=[array(t, rows, z)] * members,
        scratch_shapes=[
            pltpu.VMEM((y, y), f32),
            pltpu.VMEM((y, y), f32),
            pltpu.VMEM((y, 3 * y), bf16),
            pltpu.VMEM((3 * z, z), bf16),
        ],
        compiler_params=params(),
        cost_estimate=cost(6 * t * a * y * z * (y + z), 8 * t * a * y * z),
        name="forward_yz",
    )(x, by, bz)


def backward_body(by_ref, bz_ref, *refs):
    pieces, (out_ref, turn_ref, rows_ref, by3_ref, bz3_ref) = refs[:-5], refs[-5:]
    times, rows, y, z = out_ref.shape
    span = y // len(pieces)

    @pl.when(pl.program_id(0) == 0)
    def _():
        turn_ref[...] = by_ref[...].T
        gather_rows(turn_ref, rows_ref, PEERS, -1)
        by3_ref[...] = left3(rows_ref[...].T)
        bz3_ref[...] = right3(bz_ref[...].T)

    vol = [[] for t in range(times)]
    for a in range(rows):
        plane = jnp.concatenate(
            [
                jnp.concatenate(
                    [piece[t, pl.ds(a, span, stride=rows), :] for piece in pieces], axis=0
                )
                for t in range(times)
            ],
            axis=1,
        )
        plane = mm(by3_ref[...], right3(plane))
        for t in range(times):
            vol[t].append(plane[:, t * z : (t + 1) * z])
    for t in range(times):
        flat = jnp.concatenate(vol[t], axis=0)
        out_ref[t] = mm(left3(flat), bz3_ref[...]).reshape(rows, y, z)


def backward_yz(pieces, by, bz):
    members = len(pieces)
    y, z = by.shape[0], bz.shape[0]
    t, rows = pieces[0].shape[:2]
    a = rows * members // y
    return pl.pallas_call(
        backward_body,
        grid=(t // 2,),
        in_specs=[whole(y, y), whole(z, z)]
        + [pl.BlockSpec((2, rows, z), lambda k: (k, 0, 0))] * members,
        out_specs=pl.BlockSpec((2, a, y, z), lambda k: (k, 0, 0, 0)),
        out_shape=array(t, a, y, z),
        scratch_shapes=[
            pltpu.VMEM((y, y), f32),
            pltpu.VMEM((y, y), f32),
            pltpu.VMEM((y, 3 * y), bf16),
            pltpu.VMEM((3 * z, z), bf16),
        ],
        compiler_params=params(),
        cost_estimate=cost(6 * t * a * y * z * (y + z), 8 * t * a * y * z),
        name="backward_yz",
    )(by, bz, *pieces)


def length(steps_ref, at):
    total = steps_ref.shape[0]
    here = steps_ref[jnp.minimum(at, total - 1)] / total
    return jnp.where(at < total, here, 0.0)


def row_terms(eigen, steps_ref, at):
    now, then = length(steps_ref, at), length(steps_ref, at + 1)
    closing = jnp.where(at == steps_ref.shape[0] - 1, 0.5, 0.0)
    main = eigen * ((now + then) / 3.0) + closing
    sub = eigen * (now / 6.0) - 0.5
    sup = eigen * (then / 6.0) + 0.5
    return main, sub, sup


def mode_sums(ex_ref, ey_ref, ez_ref, j):
    x, z = ex_ref.shape[1], ez_ref.shape[1]
    along_x = jnp.broadcast_to(ex_ref[...], (z, x)).T
    return (along_x + ey_ref[j]) + ez_ref[...]


def fill_sums(ex_ref, ey_ref, ez_ref, sums_ref):
    x, members = ex_ref.shape[1], len(PEERS)
    span = ey_ref.shape[0] // members
    member = lax.axis_index("gx")
    for j in range(span):
        sums_ref[j * x : (j + 1) * x] = mode_sums(ex_ref, ey_ref, ez_ref, member * span + j)


def reduced_body(rows, steps_ref, ex_ref, ey_ref, ez_ref, cl_ref, e_ref, a_ref, k_ref, b_ref, q_ref, sums_ref):
    count, share = cl_ref.shape[:2]
    x, span = ex_ref.shape[1], ey_ref.shape[0] // len(PEERS)
    first = lax.axis_index("ta") * share
    sums_ref[...] = mode_sums(ex_ref, ey_ref, ez_ref, lax.axis_index("gx") * span + first // x)
    eigen = sums_ref[pl.ds(pl.multiple_of(lax.rem(first, x), share), share), :]

    def block(j, carry):
        inverses, subs, ratios = [], [], []
        for k in range(rows):
            main, sub, sup = row_terms(eigen, steps_ref, j * rows + k)
            inverse = 1.0 / (main - sub * ratios[-1] if k else main)
            inverses.append(inverse)
            subs.append(sub)
            ratios.append(sup * inverse)
        front = subs[0] * inverses[0]
        fronts = [front]
        for k in range(1, rows):
            front = -(subs[k] * inverses[k]) * front
            fronts.append(front)
        last = ratios[rows - 1]
        low = fronts[rows - 1]
        cl_ref[j] = low
        e_ref[j] = last
        for k in reversed(range(rows - 1)):
            low = fronts[k] - ratios[k] * low
            last = -ratios[k] * last
        a_ref[j] = low
        b_ref[j] = last
        return carry

    lax.fori_loop(0, count, block, 0, unroll=4)

    def sweep(j, q_before):
        v_last, w_last, v_first, w_first = cl_ref[j], e_ref[j], a_ref[j], b_ref[j]
        scale = 1.0 / (1.0 - v_first * q_before)
        back = w_first * scale
        q_now = w_last + v_last * q_before * back
        e_now = v_last * scale
        cl_ref[j] = e_now * q_before
        e_ref[j] = e_now
        a_ref[j] = scale
        k_ref[j] = v_first * scale
        b_ref[j] = back
        q_ref[j] = q_now
        return q_now

    lax.fori_loop(0, count, sweep, jnp.zeros_like(eigen))


def reduced_terms(steps, sums, count, rows, share):
    x, z = sums[0].shape[1], sums[2].shape[1]
    return pl.pallas_call(
        partial(reduced_body, rows),
        in_specs=[SMEM, VMEM, SMEM, VMEM],
        out_specs=[VMEM] * 6,
        out_shape=[array(count, share, z)] * 6,
        scratch_shapes=[pltpu.VMEM((x, z), f32)],
        compiler_params=params(),
        cost_estimate=cost(40 * rows * count * share * z, 24 * count * share * z),
        name="reduced_terms",
    )(steps, *sums)


def interface_body(g_ref, cl_ref, e_ref, a_ref, k_ref, b_ref, q_ref, out_ref, fh_ref):
    count = g_ref.shape[0]
    zero = jnp.zeros(g_ref.shape[2:], f32)

    def down(j, before):
        first, last = g_ref[j, 0], g_ref[j, 1]
        out_ref[j, 0] = before
        fh_ref[j] = a_ref[j] * first - k_ref[j] * before
        return (last + cl_ref[j] * first) - e_ref[j] * before

    lax.fori_loop(0, count, down, zero, unroll=8)

    def up(i, after):
        j = count - 1 - i
        out_ref[j, 1] = after

        @pl.when(j < count - 1)
        def _():
            out_ref[j + 1, 0] = out_ref[j + 1, 0] - q_ref[j] * after

        return fh_ref[j] - b_ref[j] * after

    lax.fori_loop(0, count, up, zero, unroll=8)


def interface_solve(g, terms):
    return pl.pallas_call(
        interface_body,
        in_specs=[VMEM] * 7,
        out_specs=VMEM,
        out_shape=array(*g.shape),
        scratch_shapes=[pltpu.VMEM(g.shape[:1] + g.shape[2:], f32)],
        compiler_params=params(),
        cost_estimate=cost(6 * g.size, 20 * g.size),
        name="interface_solve",
    )(g, *terms)


def eliminate_body(steps_ref, ex_ref, ey_ref, ez_ref, bx_ref, *refs):
    pieces, (g_ref, ends_ref, ratio_ref, sums_ref, rows_ref, bx3_ref) = refs[:-6], refs[-6:]
    step = pl.program_id(0)
    total, modes, lanes = g_ref.shape
    times = pieces[0].shape[0]
    x = bx_ref.shape[0]
    span = x // len(pieces)

    @pl.when(step == 0)
    def _():
        gather_rows(bx_ref, rows_ref, PEERS, -1)
        bx3_ref[...] = left3(rows_ref[...].T)
        fill_sums(ex_ref, ey_ref, ez_ref, sums_ref)

    spectral = [[] for k in range(times)]
    for j in range(modes // x):
        plane = jnp.concatenate(
            [
                jnp.concatenate([piece[k, j * span : (j + 1) * span, :] for piece in pieces], axis=0)
                for k in range(times)
            ],
            axis=1,
        )
        plane = mm(bx3_ref[...], right3(plane))
        for k in range(times):
            spectral[k].append(plane[:, k * lanes : (k + 1) * lanes])
    for k in range(times):
        t = step * times + k
        values = jnp.concatenate(spectral[k], axis=0)
        main, sub, sup = row_terms(sums_ref[...], steps_ref, lax.axis_index("ta") * total + t)

        def begin():
            inverse = 1.0 / main
            ratio_ref[t] = sup * inverse
            g_ref[t] = values * inverse

        def follow():
            inverse = 1.0 / (main - sub * ratio_ref[t - 1])
            ratio_ref[t] = sup * inverse
            g_ref[t] = (values - sub * g_ref[t - 1]) * inverse

        if k:
            follow()
        else:
            pl.when(step == 0)(begin)
            pl.when(step > 0)(follow)

    @pl.when(step == pl.num_programs(0) - 1)
    def _():
        split_shape = (ends_ref.shape[0], modes // ends_ref.shape[0], lanes)
        now = g_ref[total - 1]
        ends_ref[:, 1] = now.reshape(split_shape)
        for k in reversed(range(total - 1)):
            now = g_ref[k] - ratio_ref[k] * now
            g_ref[k] = now
        ends_ref[:, 0] = now.reshape(split_shape)


def eliminate(pieces, sums, bx, steps, count):
    t, rows, z = pieces[0].shape
    x = bx.shape[0]
    modes = rows * len(pieces)
    outs = [array(t, modes, z), array(count, 2, modes // count, z)]
    return pl.pallas_call(
        eliminate_body,
        grid=(t // 2,),
        in_specs=[SMEM, whole(1, x), SMEM, whole(1, z), whole(x, x)]
        + [pl.BlockSpec((2, rows, z), lambda k: (k, 0, 0))] * len(pieces),
        out_specs=[whole(*o.shape) for o in outs],
        out_shape=outs,
        scratch_shapes=[
            pltpu.VMEM((t, modes, z), f32),
            pltpu.VMEM((modes, z), f32),
            pltpu.VMEM((x, x), f32),
            pltpu.VMEM((x, 3 * x), bf16),
        ],
        compiler_params=params(),
        cost_estimate=cost(6 * t * modes * x * z, 8 * t * modes * z),
        name="eliminate",
    )(steps, *sums, bx, *pieces)


def return_body(steps_ref, ex_ref, ey_ref, ez_ref, bx_ref, g_ref, ends_ref, *refs):
    outs, (sol_ref, sums_ref, rows_ref, bx3_ref) = refs[:-4], refs[-4:]
    step = pl.program_id(0)
    total, modes, lanes = g_ref.shape
    times = outs[0].shape[0]
    x = bx_ref.shape[0]
    span = x // len(outs)

    @pl.when(step == 0)
    def _():
        gather_rows(bx_ref, rows_ref, PEERS, 1)
        bx3_ref[...] = left3(rows_ref[...])
        fill_sums(ex_ref, ey_ref, ez_ref, sums_ref)
        eigen = sums_ref[...]
        begin = lax.axis_index("ta") * total
        before = ends_ref[:, 0].reshape(modes, lanes)
        after = ends_ref[:, 1].reshape(modes, lanes)
        ratios, values = [], []
        for k in range(total):
            main, sub, sup = row_terms(eigen, steps_ref, begin + k)
            inverse = 1.0 / (main - sub * ratios[-1] if k else main)
            ratios.append(sup * inverse)
            value = -(sub * inverse) * (values[-1] if k else before)
            if k == total - 1:
                value = value - ratios[-1] * after
            values.append(value)
        now = values[total - 1]
        sol_ref[total - 1] = g_ref[total - 1] + now
        for k in reversed(range(total - 1)):
            now = values[k] - ratios[k] * now
            sol_ref[k] = g_ref[k] + now

    for j in range(modes // x):
        plane = jnp.concatenate(
            [sol_ref[step * times + k, j * x : (j + 1) * x, :] for k in range(times)], axis=1
        )
        plane = mm(bx3_ref[...], right3(plane))
        for i, out in enumerate(outs):
            for k in range(times):
                out[k, j * span : (j + 1) * span, :] = plane[
                    i * span : (i + 1) * span, k * lanes : (k + 1) * lanes
                ]


def return_x(g, ends, sums, bx, steps):
    t, modes, z = g.shape
    x, members = bx.shape[0], len(PEERS)
    rows = modes // members
    return pl.pallas_call(
        return_body,
        grid=(t // 2,),
        in_specs=[SMEM, whole(1, x), SMEM, whole(1, z), whole(x, x), whole(*g.shape), whole(*ends.shape)],
        out_specs=[pl.BlockSpec((2, rows, z), lambda k: (k, 0, 0))] * members,
        out_shape=[array(t, rows, z)] * members,
        scratch_shapes=[
            pltpu.VMEM((t, modes, z), f32),
            pltpu.VMEM((modes, z), f32),
            pltpu.VMEM((x, x), f32),
            pltpu.VMEM((x, 3 * x), bf16),
        ],
        compiler_params=params(),
        cost_estimate=cost(6 * t * modes * x * z, 8 * t * modes * z),
        name="return_x",
    )(steps, *sums, bx, g, ends)


def local(right_side, basis_x, basis_y, basis_z, eig_x, eig_y, eig_z, steps):
    rows = right_side.shape[0]
    count = lax.axis_size("ta")
    sums = (eig_x[None, :], eig_y, eig_z[None, :])
    share = basis_x.shape[0] * basis_y.shape[0] // (lax.axis_size("gx") * count)
    hbm = lambda value: pltpu.with_memory_space_constraint(value, pltpu.HBM)

    sent = forward_yz(hbm(right_side), hbm(basis_y), hbm(basis_z))
    moved = exchange(sent, PEERS)
    terms = list(reduced_terms(steps, sums, count, rows, share))
    moved[0], terms[0] = lax.optimization_barrier((moved[0], terms[0]))
    g, ends = eliminate(moved, sums, basis_x, steps, count)
    ends = lax.all_to_all(ends, "ta", 0, 0, tiled=True)
    ends = interface_solve(ends, terms)
    ends = lax.all_to_all(ends, "ta", 0, 0, tiled=True)
    moved = exchange(return_x(g, ends, sums, basis_x, steps), PEERS)
    return backward_yz(moved, basis_y, basis_z)


def solution(mesh):
    return jax.shard_map(
        local,
        mesh=mesh,
        in_specs=(P("ta", "gx", None, None), P(), P(), P(), P(), P(), P(), P()),
        out_specs=P("ta", "gx", None, None),
        check_vma=False,
    )
```

time: 127 us -> 118 us (0.929)
  blocking collectives: 22.1 us -> 47.2 us
  waiting for transfers between devices: 36.4 us -> 19.9 us
  starting transfers between devices: 42.9 us -> 33.4 us
  local copies, waits for them, and re-layouts: 6.57 us -> 0.03 us
  Pallas kernels: 18.8 us -> 16.9 us
    all_to_all x1 -> x2, blocking collectives: 22.1 us -> 47.2 us  [local(): ends = lax.all_to_all(ends, 'ta', 0, 0, tiled=True)]
    all_to_all x1 -> x0, starting transfers between devices: 11.1 us -> none  [local(): ends = lax.all_to_all(ends, 'ta', 0, 0, tiled=True)]
    all_to_all x1 -> x0, waiting for transfers between devices: 9.29 us -> none  [local(): ends = lax.all_to_all(ends, 'ta', 0, 0, tiled=True)]
    ppermute x14, waiting for transfers between devices: 27.1 us -> 19.9 us  [exchange(): moved.append(lax.ppermute(pieces[k], 'gx', pairs))]
    unnamed x30 -> x14, local copies, waits for them, and re-layouts: 6.57 us -> 0.03 us
    pallas_call x4, Pallas kernels: 15.7 us -> 13.8 us  [the longest x1 4.11 us: forward_yz(): pl.pallas_call(forward_body, grid=(t // 2,), in_specs=[pl.BlockSpec((2, a...]
    ppermute x14, starting transfers between devices: 31.8 us -> 33.4 us  [exchange(): moved.append(lax.ppermute(pieces[k], 'gx', pairs))]
  transfers between devices with their start and end apart: 15 -> 14, of which waited for: 8 -> 7; matrix products, arithmetic and copies ran while one was open for 0% -> 0% of each run, Pallas kernels for 2% -> 2%
where the time goes in v3:
time: 118 us
  blocking collectives  47.2 us (40%)
  starting transfers between devices  33.4 us (28%)
  waiting for transfers between devices  19.9 us (17%)
  Pallas kernels  16.9 us (14%)
    all_to_all x2, blocking collectives, local(): ends = lax.all_to_all(ends, 'ta', 0, 0, tiled=True)  47.2 us
    ppermute x14, starting transfers between devices, exchange(): moved.append(lax.ppermute(pieces[k], 'gx', pairs))  33.4 us
    ppermute x14, waiting for transfers between devices, exchange(): moved.append(lax.ppermute(pieces[k], 'gx', pairs))  19.9 us
    pallas_call x1, Pallas kernels, forward_yz(): pl.pallas_call(forward_body, grid=(t // 2,), in_specs=[pl.BlockSpec((2, a...  4.11 us
    pallas_call x1, Pallas kernels, backward_yz(): pl.pallas_call(backward_body, grid=(t // 2,), in_specs=[whole(y, y), whol...  3.6 us
    pallas_call x1, Pallas kernels, eliminate(): pl.pallas_call(eliminate_body, grid=(t // 2,), in_specs=[SMEM, whole(1, x...  3.14 us
    pallas_call x1, Pallas kernels, return_x(): pl.pallas_call(return_body, grid=(t // 2,), in_specs=[SMEM, whole(1, x),...  2.98 us
    pallas_call x1, Pallas kernels, reduced_terms(): pl.pallas_call(partial(reduced_body, rows), in_specs=[SMEM, VMEM, SMEM, V...  2.75 us
  transfers between devices with their start and end apart: 14, of which 7 were waited for; matrix products, arithmetic and copies ran while one was open for 0% of the time, Pallas kernels for 2%

profile of v3, /device:TPU:1, one launch (start us, length us, event | category | flops | bytes accessed | tf_op | source)
XLA Modules:
  0.0 117.6 jit_solution(16983006573904307992)
XLA Ops:
  0.0 0.0 copy-start.3
  0.0 0.0 copy-start.4
  0.0 0.0 copy-start
  0.0 4.1 %forward_yz.1 = (f32[8,64,128]{2,1,0:T(8,128)S(1)}, f32[8,64,128]{2,1,0:T(8,128)S(1)}, f32[8,64,128]{2,1,0:T(8,128)S(1)}, f32[8,64,128]{2,1,0:T(8,128)S(1)}, f32...) custom-call(f32[8,8,64,128]{3,2,1,0:T(8,128)} %x_ref.1, ...), custom_call_target="tpu_custom_call" | custom-call | flops 603979776 | bytes 4194304 | tf_op jit(solution)/shard_map/forward_yz/pallas_call | solution.py:102
  4.2 3.7 %collective-permute-start = (f32[8,64,128]{2,1,0:T(8,128)S(1)}, f32[8,64,128]{2,1,0:T(8,128)S(1)}, u32[]{:S(2)}, u32[]{:S(2)}) collective-permute-start(f32[8,64,128]{2,1,0:T(8,128)S(1)} %get-tuple-element.34), channel_id=1, source_target_pairs={{0,4},{1,5},{2,6},{3,7},{4,0},{5,1},{6,2},{7,3},{8,12},{9,13},{10,... | collective-permute-start | bytes 786440 | tf_op jit(solution)/shard_map/ppermute | solution.py:32
  7.8 2.8 %collective-permute-start.1 = (f32[8,64,128]{2,1,0:T(8,128)S(1)}, f32[8,64,128]{2,1,0:T(8,128)S(1)}, u32[]{:S(2)}, u32[]{:S(2)}) collective-permute-start(f32[8,64,128]{2,1,0:T(8,128)S(1)} %get-tuple-element.35), channel_id=1, source_target_pairs={{0,5},{1,4},{2,7},{3,6},{4,1},{5,0},{6,3},{7,2},{8,13},{9,12},{10,... | collective-permute-start | bytes 786440 | tf_op jit(solution)/shard_map/ppermute | solution.py:32
  10.6 0.0 collective-permute-start.2
  10.6 2.7 %collective-permute-start.3 = (f32[8,64,128]{2,1,0:T(8,128)S(1)}, f32[8,64,128]{2,1,0:T(8,128)S(1)}, u32[]{:S(2)}, u32[]{:S(2)}) collective-permute-start(f32[8,64,128]{2,1,0:T(8,128)S(1)} %get-tuple-element.37), channel_id=1, source_target_pairs={{0,6},{1,7},{2,0},{3,1},{4,2},{5,3},{6,4},{7,5},{8,14},{9,15},{10,... | collective-permute-start | bytes 786440 | tf_op jit(solution)/shard_map/ppermute | solution.py:32
  13.3 0.0 collective-permute-start.4
  13.3 0.0 collective-permute-done.refs_1_
  13.3 5.6 %collective-permute-start.5 = (f32[8,64,128]{2,1,0:T(8,128)S(1)}, f32[8,64,128]{2,1,0:T(8,128)S(1)}, u32[]{:S(2)}, u32[]{:S(2)}) collective-permute-start(f32[8,64,128]{2,1,0:T(8,128)S(1)} %get-tuple-element.39), channel_id=1, source_target_pairs={{0,7},{1,6},{2,1},{3,0},{4,3},{5,2},{6,5},{7,4},{8,15},{9,14},{10,... | collective-permute-start | bytes 786440 | tf_op jit(solution)/shard_map/ppermute | solution.py:32
  18.9 3.6 %collective-permute-done.1.refs_2_ = f32[8,64,128]{2,1,0:T(8,128)S(1)} collective-permute-done((f32[8,64,128]{2,1,0:T(8,128)S(1)}, f32[8,64,128]{2,1,0:T(8,128)S(1)}, u32[]{:S(2)}, u32[]{:S(2)}) %collective-permute-start.1) | collective-permute-done | bytes 262176 | tf_op jit(solution)/shard_map/ppermute | solution.py:32
  22.5 0.0 collective-permute-start.6
  22.5 0.0 copy-done.3
  22.5 0.0 copy-done.5
  22.5 0.0 copy-done.6
  22.5 0.0 copy-done.4
  22.5 2.7 %reduced_terms.1 = (f32[32,16,128]{2,1,0:T(8,128)S(1)}, f32[32,16,128]{2,1,0:T(8,128)S(1)}, f32[32,16,128]{2,1,0:T(8,128)S(1)}, f32[32,16,128]{2,1,0:T(8,128)S(1...) custom-call(f32[256]{0:T(256)S(1)} %copy-done.3, f32[1,64]{1,0:T(1,128)S(1)} %bitcast.2, f32[64]{0:T(128)S(1)} %copy-done.5, ...), custom_call_target="tpu_custom_call" | custom-call | flops 20971520 | bytes 1572864 | tf_op jit(solution)/shard_map/reduced_terms/pallas_call | solution.py:260
  25.2 0.8 collective-permute-done.2.refs_3_
  26.1 0.0 collective-permute-done.3.refs_4_
  26.1 5.6 %collective-permute-done.4.refs_5_ = f32[8,64,128]{2,1,0:T(8,128)S(1)} collective-permute-done((f32[8,64,128]{2,1,0:T(8,128)S(1)}, f32[8,64,128]{2,1,0:T(8,128)S(1)}, u32[]{:S(2)}, u32[]{:S(2)}) %collective-permute-start.4) | collective-permute-done | bytes 262176 | tf_op jit(solution)/shard_map/ppermute | solution.py:32
  31.7 0.1 collective-permute-done.5.refs_6_
  31.8 0.0 collective-permute-done.6.refs_7_
  31.8 0.0 copy-done
  31.8 3.1 %eliminate.1 = (f32[8,512,128]{2,1,0:T(8,128)S(1)}, f32[32,2,16,128]{3,2,1,0:T(8,128)S(1)}) custom-call(f32[256]{0:T(256)S(1)} %copy-done.3, f32[1,64]{1,0:T(1,128)S(1)} %bitcast.3, f32[64]{0:T(128)S(1)} %copy-done.5, f32[1,128]{1,0:T(1,128)S(1)} %bitcast.6, f32[64,64]{1,0:T(8,128)S(1)} %copy-done, f32[8,64,128]{2,1,0:T(8,128)S(1)} %get-tuple-element.33.refs_0_, ...), custom_call_target="tpu_custom_call" | custom-call | flops 201326592 | bytes 4194304 | tf_op jit(solution)/shard_map/eliminate/pallas_call | solution.py:373
  35.0 25.1 %all_to_all.10.g_ref = f32[32,2,16,128]{3,2,1,0:T(8,128)S(1)} all-to-all(f32[32,2,16,128]{3,2,1,0:T(8,128)S(1)} %get-tuple-element.42), channel_id=1, replica_groups=mesh['ta'=32,'gx'=8] {'ta'}, dimensions={0} | all-to-all | bytes 1048576 | tf_op jit(solution)/shard_map/all_to_all | solution.py:470
  60.1 0.3 interface_solve.1
  60.4 0.0 copy-start.1
  60.4 0.0 copy-start.2
  60.4 22.1 %all_to_all.11.ends_ref = f32[32,2,16,128]{3,2,1,0:T(8,128)S(1)} all-to-all(f32[32,2,16,128]{3,2,1,0:T(8,128)S(1)} %interface_solve.1), channel_id=1, replica_groups=mesh['ta'=32,'gx'=8] {'ta'}, dimensions={0} | all-to-all | bytes 1048576 | tf_op jit(solution)/shard_map/all_to_all | solution.py:472
  82.5 3.0 %return_x.1 = (f32[8,64,128]{2,1,0:T(8,128)S(1)}, f32[8,64,128]{2,1,0:T(8,128)S(1)}, f32[8,64,128]{2,1,0:T(8,128)S(1)}, f32[8,64,128]{2,1,0:T(8,128)S(1)}, f32[8...) custom-call(f32[256]{0:T(256)S(1)} %copy-done.3, ...), custom_call_target="tpu_custom_call" | custom-call | flops 201326592 | bytes 4194304 | tf_op jit(solution)/shard_map/return_x/pallas_call | solution.py:440
  85.5 2.9 %collective-permute-start.7 = (f32[8,64,128]{2,1,0:T(8,128)S(1)}, f32[8,64,128]{2,1,0:T(8,128)S(1)}, u32[]{:S(2)}, u32[]{:S(2)}) collective-permute-start(f32[8,64,128]{2,1,0:T(8,128)S(1)} %get-tuple-element.50), channel_id=1, source_target_pairs={{0,4},{1,5},{2,6},{3,7},{4,0},{5,1},{6,2},{7,3},{8,12},{9,13},{10,... | collective-permute-start | bytes 786440 | tf_op jit(solution)/shard_map/ppermute | solution.py:32
  88.4 4.4 %collective-permute-start.8 = (f32[8,64,128]{2,1,0:T(8,128)S(1)}, f32[8,64,128]{2,1,0:T(8,128)S(1)}, u32[]{:S(2)}, u32[]{:S(2)}) collective-permute-start(f32[8,64,128]{2,1,0:T(8,128)S(1)} %get-tuple-element.51), channel_id=1, source_target_pairs={{0,5},{1,4},{2,7},{3,6},{4,1},{5,0},{6,3},{7,2},{8,13},{9,12},{10,... | collective-permute-start | bytes 786440 | tf_op jit(solution)/shard_map/ppermute | solution.py:32
  92.8 1.2 %collective-permute-start.9 = (f32[8,64,128]{2,1,0:T(8,128)S(1)}, f32[8,64,128]{2,1,0:T(8,128)S(1)}, u32[]{:S(2)}, u32[]{:S(2)}) collective-permute-start(f32[8,64,128]{2,1,0:T(8,128)S(1)} %get-tuple-element.52), channel_id=1, source_target_pairs={{0,2},{1,3},{2,4},{3,5},{4,6},{5,7},{6,0},{7,1},{8,10},{9,11},{10,... | collective-permute-start | bytes 786440 | tf_op jit(solution)/shard_map/ppermute | solution.py:32
  94.0 1.5 %collective-permute-start.10 = (f32[8,64,128]{2,1,0:T(8,128)S(1)}, f32[8,64,128]{2,1,0:T(8,128)S(1)}, u32[]{:S(2)}, u32[]{:S(2)}) collective-permute-start(f32[8,64,128]{2,1,0:T(8,128)S(1)} %get-tuple-element.53), channel_id=1, source_target_pairs={{0,6},{1,7},{2,0},{3,1},{4,2},{5,3},{6,4},{7,5},{8,14},{9,15},{10,... | collective-permute-start | bytes 786440 | tf_op jit(solution)/shard_map/ppermute | solution.py:32
  95.5 0.0 collective-permute-start.11
  95.5 0.0 collective-permute-done.7.refs_1_
  95.5 6.4 %collective-permute-start.12 = (f32[8,64,128]{2,1,0:T(8,128)S(1)}, f32[8,64,128]{2,1,0:T(8,128)S(1)}, u32[]{:S(2)}, u32[]{:S(2)}) collective-permute-start(f32[8,64,128]{2,1,0:T(8,128)S(1)} %get-tuple-element.55), channel_id=1, source_target_pairs={{0,7},{1,6},{2,1},{3,0},{4,3},{5,2},{6,5},{7,4},{8,15},{9,14},{10,... | collective-permute-start | bytes 786440 | tf_op jit(solution)/shard_map/ppermute | solution.py:32
  101.8 0.9 collective-permute-done.8.refs_2_
  102.8 2.3 %collective-permute-start.13 = (f32[8,64,128]{2,1,0:T(8,128)S(1)}, f32[8,64,128]{2,1,0:T(8,128)S(1)}, u32[]{:S(2)}, u32[]{:S(2)}) collective-permute-start(f32[8,64,128]{2,1,0:T(8,128)S(1)} %get-tuple-element.56), channel_id=1, source_target_pairs={{0,1},{1,0},{2,3},{3,2},{4,5},{5,4},{6,7},{7,6},{8,9},{9,8},{10,11... | collective-permute-start | bytes 786440 | tf_op jit(solution)/shard_map/ppermute | solution.py:32
  105.1 3.3 %collective-permute-done.9.refs_3_ = f32[8,64,128]{2,1,0:T(8,128)S(1)} collective-permute-done((f32[8,64,128]{2,1,0:T(8,128)S(1)}, f32[8,64,128]{2,1,0:T(8,128)S(1)}, u32[]{:S(2)}, u32[]{:S(2)}) %collective-permute-start.9) | collective-permute-done | bytes 262176 | tf_op jit(solution)/shard_map/ppermute | solution.py:32
  108.3 0.0 collective-permute-done.10.refs_4_
  108.3 5.6 %collective-permute-done.11.refs_5_ = f32[8,64,128]{2,1,0:T(8,128)S(1)} collective-permute-done((f32[8,64,128]{2,1,0:T(8,128)S(1)}, f32[8,64,128]{2,1,0:T(8,128)S(1)}, u32[]{:S(2)}, u32[]{:S(2)}) %collective-permute-start.11) | collective-permute-done | bytes 262176 | tf_op jit(solution)/shard_map/ppermute | solution.py:32
  114.0 0.0 collective-permute-done.12.refs_6_
  114.0 0.0 collective-permute-done.13.refs_7_
  114.0 0.0 copy-done.1
  114.0 0.0 copy-done.2
  114.0 3.6 %backward_yz.1 = f32[8,8,64,128]{3,2,1,0:T(8,128)} custom-call(f32[64,64]{1,0:T(8,128)S(1)} %copy-done.2, f32[128,128]{1,0:T(8,128)S(1)} %copy-done.1, f32[8,64,128]{2,1,0:T(8,128)S(1)} %get-tuple-element.49.refs_0_, f32[8,64,128]{2,1,0:T(8,128)S(1)} %collective-permute-done.7.refs_1_, f32[8,64,128]{2,1,0:T(8,128)S(1)} %collective-permute-done.8.refs_2_, ...), custom_call_target="tpu_custom_call" | custom-call | flops 603979776 | bytes 4194304 | tf_op jit(solution)/shard_map/backward_yz/pallas_call | solution.py:160
  (2 shorter events, 0.0 us)
Async XLA Ops:
  0.0 22.5 %copy-start.3 = (f32[256]{0:T(256)S(1)}, f32[256]{0:T(256)}, u32[]{:S(2)}) copy-start(f32[256]{0:T(256)} %steps_ref.5) | copy-start | bytes 3076
  0.0 22.5 %copy-start.5 = (f32[64]{0:T(128)S(1)}, f32[64]{0:T(128)}, u32[]{:S(2)}) copy-start(f32[64]{0:T(128)} %ey_ref.5) | copy-start | bytes 772
  0.0 22.5 %copy-start.6 = (f32[128]{0:T(128)S(1)}, f32[128]{0:T(128)}, u32[]{:S(2)}) copy-start(f32[128]{0:T(128)} %param.14) | copy-start | bytes 1540
  0.0 22.5 %copy-start.4 = (f32[64]{0:T(128)S(1)}, f32[64]{0:T(128)}, u32[]{:S(2)}) copy-start(f32[64]{0:T(128)} %param.12) | copy-start | bytes 772
  0.0 31.8 %copy-start = (f32[64,64]{1,0:T(8,128)S(1)}, f32[64,64]{1,0:T(8,128)}, u32[]{:S(2)}) copy-start(f32[64,64]{1,0:T(8,128)} %bx_ref.3) | copy-start | bytes 49156
  4.2 9.1 %collective-permute-start = (f32[8,64,128]{2,1,0:T(8,128)S(1)}, f32[8,64,128]{2,1,0:T(8,128)S(1)}, u32[]{:S(2)}, u32[]{:S(2)}) collective-permute-start(f32[8,64,128]{2,1,0:T(8,128)S(1)} %get-tuple-element.34), channel_id=1, source_target_pairs={{0,4},{1,5},{2,6},{3,7},{4,0},{5,1},{6,2},{7,3},{8,12},{9,13},{10,... | collective-permute-start | bytes 786440 | tf_op jit(solution)/shard_map/ppermute | solution.py:32
  7.8 14.6 %collective-permute-start.1 = (f32[8,64,128]{2,1,0:T(8,128)S(1)}, f32[8,64,128]{2,1,0:T(8,128)S(1)}, u32[]{:S(2)}, u32[]{:S(2)}) collective-permute-start(f32[8,64,128]{2,1,0:T(8,128)S(1)} %get-tuple-element.35), channel_id=1, source_target_pairs={{0,5},{1,4},{2,7},{3,6},{4,1},{5,0},{6,3},{7,2},{8,13},{9,12},{10,... | collective-permute-start | bytes 786440 | tf_op jit(solution)/shard_map/ppermute | solution.py:32
  10.6 15.5 %collective-permute-start.2 = (f32[8,64,128]{2,1,0:T(8,128)S(1)}, f32[8,64,128]{2,1,0:T(8,128)S(1)}, u32[]{:S(2)}, u32[]{:S(2)}) collective-permute-start(f32[8,64,128]{2,1,0:T(8,128)S(1)} %get-tuple-element.36), channel_id=1, source_target_pairs={{0,2},{1,3},{2,4},{3,5},{4,6},{5,7},{6,0},{7,1},{8,10},{9,11},{10,... | collective-permute-start | bytes 786440 | tf_op jit(solution)/shard_map/ppermute | solution.py:32
  10.6 15.5 %collective-permute-start.3 = (f32[8,64,128]{2,1,0:T(8,128)S(1)}, f32[8,64,128]{2,1,0:T(8,128)S(1)}, u32[]{:S(2)}, u32[]{:S(2)}) collective-permute-start(f32[8,64,128]{2,1,0:T(8,128)S(1)} %get-tuple-element.37), channel_id=1, source_target_pairs={{0,6},{1,7},{2,0},{3,1},{4,2},{5,3},{6,4},{7,5},{8,14},{9,15},{10,... | collective-permute-start | bytes 786440 | tf_op jit(solution)/shard_map/ppermute | solution.py:32
  13.3 18.4 %collective-permute-start.4 = (f32[8,64,128]{2,1,0:T(8,128)S(1)}, f32[8,64,128]{2,1,0:T(8,128)S(1)}, u32[]{:S(2)}, u32[]{:S(2)}) collective-permute-start(f32[8,64,128]{2,1,0:T(8,128)S(1)} %get-tuple-element.38), channel_id=1, source_target_pairs={{0,3},{1,2},{2,5},{3,4},{4,7},{5,6},{6,1},{7,0},{8,11},{9,10},{10,... | collective-permute-start | bytes 786440 | tf_op jit(solution)/shard_map/ppermute | solution.py:32
  13.3 18.5 %collective-permute-start.5 = (f32[8,64,128]{2,1,0:T(8,128)S(1)}, f32[8,64,128]{2,1,0:T(8,128)S(1)}, u32[]{:S(2)}, u32[]{:S(2)}) collective-permute-start(f32[8,64,128]{2,1,0:T(8,128)S(1)} %get-tuple-element.39), channel_id=1, source_target_pairs={{0,7},{1,6},{2,1},{3,0},{4,3},{5,2},{6,5},{7,4},{8,15},{9,14},{10,... | collective-permute-start | bytes 786440 | tf_op jit(solution)/shard_map/ppermute | solution.py:32
  22.5 9.4 %collective-permute-start.6 = (f32[8,64,128]{2,1,0:T(8,128)S(1)}, f32[8,64,128]{2,1,0:T(8,128)S(1)}, u32[]{:S(2)}, u32[]{:S(2)}) collective-permute-start(f32[8,64,128]{2,1,0:T(8,128)S(1)} %get-tuple-element.40), channel_id=1, source_target_pairs={{0,1},{1,0},{2,3},{3,2},{4,5},{5,4},{6,7},{7,6},{8,9},{9,8},{10,11... | collective-permute-start | bytes 786440 | tf_op jit(solution)/shard_map/ppermute | solution.py:32
  60.4 53.5 %copy-start.1 = (f32[128,128]{1,0:T(8,128)S(1)}, f32[128,128]{1,0:T(8,128)}, u32[]{:S(2)}) copy-start(f32[128,128]{1,0:T(8,128)} %bz_ref.3) | copy-start | bytes 196612
  60.4 53.5 %copy-start.2 = (f32[64,64]{1,0:T(8,128)S(1)}, f32[64,64]{1,0:T(8,128)}, u32[]{:S(2)}) copy-start(f32[64,64]{1,0:T(8,128)} %by_ref.3) | copy-start | bytes 49156
  85.5 9.9 %collective-permute-start.7 = (f32[8,64,128]{2,1,0:T(8,128)S(1)}, f32[8,64,128]{2,1,0:T(8,128)S(1)}, u32[]{:S(2)}, u32[]{:S(2)}) collective-permute-start(f32[8,64,128]{2,1,0:T(8,128)S(1)} %get-tuple-element.50), channel_id=1, source_target_pairs={{0,4},{1,5},{2,6},{3,7},{4,0},{5,1},{6,2},{7,3},{8,12},{9,13},{10,... | collective-permute-start | bytes 786440 | tf_op jit(solution)/shard_map/ppermute | solution.py:32
  88.4 14.4 %collective-permute-start.8 = (f32[8,64,128]{2,1,0:T(8,128)S(1)}, f32[8,64,128]{2,1,0:T(8,128)S(1)}, u32[]{:S(2)}, u32[]{:S(2)}) collective-permute-start(f32[8,64,128]{2,1,0:T(8,128)S(1)} %get-tuple-element.51), channel_id=1, source_target_pairs={{0,5},{1,4},{2,7},{3,6},{4,1},{5,0},{6,3},{7,2},{8,13},{9,12},{10,... | collective-permute-start | bytes 786440 | tf_op jit(solution)/shard_map/ppermute | solution.py:32
  92.8 15.5 %collective-permute-start.9 = (f32[8,64,128]{2,1,0:T(8,128)S(1)}, f32[8,64,128]{2,1,0:T(8,128)S(1)}, u32[]{:S(2)}, u32[]{:S(2)}) collective-permute-start(f32[8,64,128]{2,1,0:T(8,128)S(1)} %get-tuple-element.52), channel_id=1, source_target_pairs={{0,2},{1,3},{2,4},{3,5},{4,6},{5,7},{6,0},{7,1},{8,10},{9,11},{10,... | collective-permute-start | bytes 786440 | tf_op jit(solution)/shard_map/ppermute | solution.py:32
  94.0 14.3 %collective-permute-start.10 = (f32[8,64,128]{2,1,0:T(8,128)S(1)}, f32[8,64,128]{2,1,0:T(8,128)S(1)}, u32[]{:S(2)}, u32[]{:S(2)}) collective-permute-start(f32[8,64,128]{2,1,0:T(8,128)S(1)} %get-tuple-element.53), channel_id=1, source_target_pairs={{0,6},{1,7},{2,0},{3,1},{4,2},{5,3},{6,4},{7,5},{8,14},{9,15},{10,... | collective-permute-start | bytes 786440 | tf_op jit(solution)/shard_map/ppermute | solution.py:32
  95.5 18.5 %collective-permute-start.11 = (f32[8,64,128]{2,1,0:T(8,128)S(1)}, f32[8,64,128]{2,1,0:T(8,128)S(1)}, u32[]{:S(2)}, u32[]{:S(2)}) collective-permute-start(f32[8,64,128]{2,1,0:T(8,128)S(1)} %get-tuple-element.54), channel_id=1, source_target_pairs={{0,3},{1,2},{2,5},{3,4},{4,7},{5,6},{6,1},{7,0},{8,11},{9,10},{10,... | collective-permute-start | bytes 786440 | tf_op jit(solution)/shard_map/ppermute | solution.py:32
  95.5 18.5 %collective-permute-start.12 = (f32[8,64,128]{2,1,0:T(8,128)S(1)}, f32[8,64,128]{2,1,0:T(8,128)S(1)}, u32[]{:S(2)}, u32[]{:S(2)}) collective-permute-start(f32[8,64,128]{2,1,0:T(8,128)S(1)} %get-tuple-element.55), channel_id=1, source_target_pairs={{0,7},{1,6},{2,1},{3,0},{4,3},{5,2},{6,5},{7,4},{8,15},{9,14},{10,... | collective-permute-start | bytes 786440 | tf_op jit(solution)/shard_map/ppermute | solution.py:32
  102.8 11.2 %collective-permute-start.13 = (f32[8,64,128]{2,1,0:T(8,128)S(1)}, f32[8,64,128]{2,1,0:T(8,128)S(1)}, u32[]{:S(2)}, u32[]{:S(2)}) collective-permute-start(f32[8,64,128]{2,1,0:T(8,128)S(1)} %get-tuple-element.56), channel_id=1, source_target_pairs={{0,1},{1,0},{2,3},{3,2},{4,5},{5,4},{6,7},{7,6},{8,9},{9,8},{10,11... | collective-permute-start | bytes 786440 | tf_op jit(solution)/shard_map/ppermute | solution.py:32

commit v4 on v3

--- a/solution.py
+++ b/solution.py
@@ -8,9 +8,10 @@
 from jax.sharding import PartitionSpec as P
 
 f32, bf16 = jnp.float32, jnp.bfloat16
-params = partial(pltpu.CompilerParams, vmem_limit_bytes=24 * 2**20)
+params = partial(pltpu.CompilerParams, vmem_limit_bytes=12 * 2**20)
 VMEM = pl.BlockSpec(memory_space=pltpu.VMEM)
 SMEM = pl.BlockSpec(memory_space=pltpu.SMEM)
+ANY = pl.BlockSpec(memory_space=pl.ANY)
 
 PEERS = ((0, 0), (2, 0), (2, 1), (1, 0), (3, 0), (1, 1), (3, 1), (0, 1))
 
@@ -55,10 +56,6 @@
     return pl.CostEstimate(flops=int(flops), bytes_accessed=int(bytes_accessed), transcendentals=0)
 
 
-def whole(*shape):
-    return pl.BlockSpec(shape, lambda k: (0,) * len(shape))
-
-
 def array(*shape):
     return jax.ShapeDtypeStruct(shape, f32)
 
@@ -72,27 +69,38 @@
         target_ref[k * span : (k + 1) * span] = source_ref[pl.ds(start, span), :]
 
 
-def forward_body(x_ref, by_ref, bz_ref, *refs):
-    outs, (turn_ref, rows_ref, by3_ref, bz3_ref) = refs[:-4], refs[-4:]
-    times, rows, y, z = x_ref.shape
+def forward_body(x_any, by_any, bz_any, *refs):
+    outs, refs = refs[: len(PEERS)], refs[len(PEERS) :]
+    x_ref, by_ref, bz_ref, turn_ref, rows_ref, by3_ref, bz3_ref, x_sem, b_sem = refs
+    total, rows, y, z = x_ref.shape
     span = y // len(outs)
-
-    @pl.when(pl.program_id(0) == 0)
-    def _():
-        turn_ref[...] = by_ref[...].T
-        gather_rows(turn_ref, rows_ref, PEERS, 1)
-        by3_ref[...] = left3(rows_ref[...])
-        bz3_ref[...] = right3(bz_ref[...])
-
-    vol = [mm(left3(x_ref[t].reshape(rows * y, z)), bz3_ref[...]) for t in range(times)]
-    for a in range(rows):
-        plane = jnp.concatenate([v[a * y : (a + 1) * y] for v in vol], axis=1)
-        plane = mm(by3_ref[...], right3(plane))
-        for k, out in enumerate(outs):
-            for t in range(times):
-                out[t, pl.ds(a, span, stride=rows), :] = plane[
-                    k * span : (k + 1) * span, t * z : (t + 1) * z
-                ]
+    tables = [
+        pltpu.make_async_copy(source, target, b_sem.at[k])
+        for k, (source, target) in enumerate(((by_any, by_ref), (bz_any, bz_ref)))
+    ]
+    planes = [pltpu.make_async_copy(x_any.at[t], x_ref.at[t], x_sem.at[t]) for t in range(total)]
+    for copy in tables + planes:
+        copy.start()
+    for copy in tables:
+        copy.wait()
+    turn_ref[...] = by_ref[...].T
+    gather_rows(turn_ref, rows_ref, PEERS, 1)
+    by3_ref[...] = left3(rows_ref[...])
+    bz3_ref[...] = right3(bz_ref[...])
+
+    for first in range(0, total, 4):
+        times = range(first, first + 4)
+        for t in times:
+            planes[t].wait()
+        vol = [mm(left3(x_ref[t].reshape(rows * y, z)), bz3_ref[...]) for t in times]
+        for a in range(rows):
+            plane = jnp.concatenate([v[a * y : (a + 1) * y] for v in vol], axis=1)
+            plane = mm(by3_ref[...], right3(plane))
+            for k, out in enumerate(outs):
+                for i, t in enumerate(times):
+                    out[t, pl.ds(a, span, stride=rows), :] = plane[
+                        k * span : (k + 1) * span, i * z : (i + 1) * z
+                    ]
 
 
 def forward_yz(x, by, bz):
@@ -101,19 +109,19 @@
     rows = a * y // members
     return pl.pallas_call(
         forward_body,
-        grid=(t // 2,),
-        in_specs=[
-            pl.BlockSpec((2, a, y, z), lambda k: (k, 0, 0, 0)),
-            whole(y, y),
-            whole(z, z),
-        ],
-        out_specs=[pl.BlockSpec((2, rows, z), lambda k: (k, 0, 0))] * members,
+        in_specs=[ANY] * 3,
+        out_specs=[VMEM] * members,
         out_shape=[array(t, rows, z)] * members,
         scratch_shapes=[
+            pltpu.VMEM(x.shape, f32),
+            pltpu.VMEM((y, y), f32),
+            pltpu.VMEM((z, z), f32),
             pltpu.VMEM((y, y), f32),
             pltpu.VMEM((y, y), f32),
             pltpu.VMEM((y, 3 * y), bf16),
             pltpu.VMEM((3 * z, z), bf16),
+            pltpu.SemaphoreType.DMA((t,)),
+            pltpu.SemaphoreType.DMA((2,)),
         ],
         compiler_params=params(),
         cost_estimate=cost(6 * t * a * y * z * (y + z), 8 * t * a * y * z),
@@ -122,34 +130,38 @@
 
 
 def backward_body(by_ref, bz_ref, *refs):
-    pieces, (out_ref, turn_ref, rows_ref, by3_ref, bz3_ref) = refs[:-5], refs[-5:]
-    times, rows, y, z = out_ref.shape
+    pieces, refs = refs[: len(PEERS)], refs[len(PEERS) :]
+    out_any, out_ref, turn_ref, rows_ref, by3_ref, bz3_ref, sem = refs
+    total, rows, y, z = out_ref.shape
     span = y // len(pieces)
-
-    @pl.when(pl.program_id(0) == 0)
-    def _():
-        turn_ref[...] = by_ref[...].T
-        gather_rows(turn_ref, rows_ref, PEERS, -1)
-        by3_ref[...] = left3(rows_ref[...].T)
-        bz3_ref[...] = right3(bz_ref[...].T)
-
-    vol = [[] for t in range(times)]
-    for a in range(rows):
-        plane = jnp.concatenate(
-            [
-                jnp.concatenate(
-                    [piece[t, pl.ds(a, span, stride=rows), :] for piece in pieces], axis=0
-                )
-                for t in range(times)
-            ],
-            axis=1,
-        )
-        plane = mm(by3_ref[...], right3(plane))
-        for t in range(times):
-            vol[t].append(plane[:, t * z : (t + 1) * z])
-    for t in range(times):
-        flat = jnp.concatenate(vol[t], axis=0)
-        out_ref[t] = mm(left3(flat), bz3_ref[...]).reshape(rows, y, z)
+    turn_ref[...] = by_ref[...].T
+    gather_rows(turn_ref, rows_ref, PEERS, -1)
+    by3_ref[...] = left3(rows_ref[...].T)
+    bz3_ref[...] = right3(bz_ref[...].T)
+
+    copies = []
+    for first in range(0, total, 4):
+        times = range(first, first + 4)
+        vol = []
+        for a in range(rows):
+            plane = jnp.concatenate(
+                [
+                    jnp.concatenate(
+                        [piece[t, pl.ds(a, span, stride=rows), :] for piece in pieces], axis=0
+                    )
+                    for t in times
+                ],
+                axis=1,
+            )
+            vol.append(mm(by3_ref[...], right3(plane)))
+        for i, t in enumerate(times):
+            flat = jnp.concatenate([v[:, i * z : (i + 1) * z] for v in vol], axis=0)
+            out_ref[t] = mm(left3(flat), bz3_ref[...]).reshape(rows, y, z)
+        for t in times:
+            copies.append(pltpu.make_async_copy(out_ref.at[t], out_any.at[t], sem.at[t]))
+            copies[-1].start()
+    for copy in copies:
+        copy.wait()
 
 
 def backward_yz(pieces, by, bz):
@@ -159,16 +171,16 @@
     a = rows * members // y
     return pl.pallas_call(
         backward_body,
-        grid=(t // 2,),
-        in_specs=[whole(y, y), whole(z, z)]
-        + [pl.BlockSpec((2, rows, z), lambda k: (k, 0, 0))] * members,
-        out_specs=pl.BlockSpec((2, a, y, z), lambda k: (k, 0, 0, 0)),
+        in_specs=[VMEM] * (2 + members),
+        out_specs=ANY,
         out_shape=array(t, a, y, z),
         scratch_shapes=[
+            pltpu.VMEM((t, a, y, z), f32),
             pltpu.VMEM((y, y), f32),
             pltpu.VMEM((y, y), f32),
             pltpu.VMEM((y, 3 * y), bf16),
             pltpu.VMEM((3 * z, z), bf16),
+            pltpu.SemaphoreType.DMA((t,)),
         ],
         compiler_params=params(),
         cost_estimate=cost(6 * t * a * y * z * (y + z), 8 * t * a * y * z),
@@ -307,76 +319,60 @@
     )(g, *terms)
 
 
+def transform_pair(table, planes):
+    lanes = planes[0].shape[1]
+    both = mm(table, right3(jnp.concatenate(planes, axis=1)))
+    return both[:, :lanes], both[:, lanes:]
+
+
 def eliminate_body(steps_ref, ex_ref, ey_ref, ez_ref, bx_ref, *refs):
-    pieces, (g_ref, ends_ref, ratio_ref, sums_ref, rows_ref, bx3_ref) = refs[:-6], refs[-6:]
-    step = pl.program_id(0)
+    pieces, refs = refs[: len(PEERS)], refs[len(PEERS) :]
+    g_ref, ends_ref, ratio_ref, sums_ref, rows_ref, bx3_ref = refs
     total, modes, lanes = g_ref.shape
-    times = pieces[0].shape[0]
     x = bx_ref.shape[0]
     span = x // len(pieces)
-
-    @pl.when(step == 0)
-    def _():
-        gather_rows(bx_ref, rows_ref, PEERS, -1)
-        bx3_ref[...] = left3(rows_ref[...].T)
-        fill_sums(ex_ref, ey_ref, ez_ref, sums_ref)
-
-    spectral = [[] for k in range(times)]
-    for j in range(modes // x):
-        plane = jnp.concatenate(
-            [
-                jnp.concatenate([piece[k, j * span : (j + 1) * span, :] for piece in pieces], axis=0)
-                for k in range(times)
-            ],
-            axis=1,
-        )
-        plane = mm(bx3_ref[...], right3(plane))
-        for k in range(times):
-            spectral[k].append(plane[:, k * lanes : (k + 1) * lanes])
-    for k in range(times):
-        t = step * times + k
-        values = jnp.concatenate(spectral[k], axis=0)
-        main, sub, sup = row_terms(sums_ref[...], steps_ref, lax.axis_index("ta") * total + t)
-
-        def begin():
-            inverse = 1.0 / main
-            ratio_ref[t] = sup * inverse
-            g_ref[t] = values * inverse
-
-        def follow():
-            inverse = 1.0 / (main - sub * ratio_ref[t - 1])
-            ratio_ref[t] = sup * inverse
-            g_ref[t] = (values - sub * g_ref[t - 1]) * inverse
-
-        if k:
-            follow()
-        else:
-            pl.when(step == 0)(begin)
-            pl.when(step > 0)(follow)
-
-    @pl.when(step == pl.num_programs(0) - 1)
-    def _():
-        split_shape = (ends_ref.shape[0], modes // ends_ref.shape[0], lanes)
-        now = g_ref[total - 1]
-        ends_ref[:, 1] = now.reshape(split_shape)
-        for k in reversed(range(total - 1)):
-            now = g_ref[k] - ratio_ref[k] * now
-            g_ref[k] = now
-        ends_ref[:, 0] = now.reshape(split_shape)
+    gather_rows(bx_ref, rows_ref, PEERS, -1)
+    bx3_ref[...] = left3(rows_ref[...].T)
+    fill_sums(ex_ref, ey_ref, ez_ref, sums_ref)
+    begin = lax.axis_index("ta") * total
+
+    for t in range(0, total, 2):
+        for j in range(modes // x):
+            mine = slice(j * x, (j + 1) * x)
+            spectral = transform_pair(
+                bx3_ref[...],
+                [
+                    jnp.concatenate([piece[k, j * span : (j + 1) * span, :] for piece in pieces], axis=0)
+                    for k in (t, t + 1)
+                ],
+            )
+            for k, values in zip((t, t + 1), spectral):
+                main, sub, sup = row_terms(sums_ref[mine], steps_ref, begin + k)
+                if k:
+                    main = main - sub * ratio_ref[k - 1, mine]
+                    values = values - sub * g_ref[k - 1, mine]
+                inverse = 1.0 / main
+                ratio_ref[k, mine] = sup * inverse
+                g_ref[k, mine] = values * inverse
+
+    split_shape = (ends_ref.shape[0], modes // ends_ref.shape[0], lanes)
+    now = g_ref[total - 1]
+    ends_ref[:, 1] = now.reshape(split_shape)
+    for k in reversed(range(total - 1)):
+        now = g_ref[k] - ratio_ref[k] * now
+        g_ref[k] = now
+    ends_ref[:, 0] = now.reshape(split_shape)
 
 
 def eliminate(pieces, sums, bx, steps, count):
     t, rows, z = pieces[0].shape
     x = bx.shape[0]
     modes = rows * len(pieces)
-    outs = [array(t, modes, z), array(count, 2, modes // count, z)]
     return pl.pallas_call(
         eliminate_body,
-        grid=(t // 2,),
-        in_specs=[SMEM, whole(1, x), SMEM, whole(1, z), whole(x, x)]
-        + [pl.BlockSpec((2, rows, z), lambda k: (k, 0, 0))] * len(pieces),
-        out_specs=[whole(*o.shape) for o in outs],
-        out_shape=outs,
+        in_specs=[SMEM, VMEM, SMEM, VMEM, VMEM] + [VMEM] * len(pieces),
+        out_specs=[VMEM] * 2,
+        out_shape=[array(t, modes, z), array(count, 2, modes // count, z)],
         scratch_shapes=[
             pltpu.VMEM((t, modes, z), f32),
             pltpu.VMEM((modes, z), f32),
@@ -391,58 +387,49 @@
 
 def return_body(steps_ref, ex_ref, ey_ref, ez_ref, bx_ref, g_ref, ends_ref, *refs):
     outs, (sol_ref, sums_ref, rows_ref, bx3_ref) = refs[:-4], refs[-4:]
-    step = pl.program_id(0)
     total, modes, lanes = g_ref.shape
-    times = outs[0].shape[0]
     x = bx_ref.shape[0]
     span = x // len(outs)
-
-    @pl.when(step == 0)
-    def _():
-        gather_rows(bx_ref, rows_ref, PEERS, 1)
-        bx3_ref[...] = left3(rows_ref[...])
-        fill_sums(ex_ref, ey_ref, ez_ref, sums_ref)
-        eigen = sums_ref[...]
-        begin = lax.axis_index("ta") * total
-        before = ends_ref[:, 0].reshape(modes, lanes)
-        after = ends_ref[:, 1].reshape(modes, lanes)
-        ratios, values = [], []
-        for k in range(total):
-            main, sub, sup = row_terms(eigen, steps_ref, begin + k)
-            inverse = 1.0 / (main - sub * ratios[-1] if k else main)
-            ratios.append(sup * inverse)
-            value = -(sub * inverse) * (values[-1] if k else before)
-            if k == total - 1:
-                value = value - ratios[-1] * after
-            values.append(value)
-        now = values[total - 1]
-        sol_ref[total - 1] = g_ref[total - 1] + now
-        for k in reversed(range(total - 1)):
-            now = values[k] - ratios[k] * now
-            sol_ref[k] = g_ref[k] + now
-
-    for j in range(modes // x):
-        plane = jnp.concatenate(
-            [sol_ref[step * times + k, j * x : (j + 1) * x, :] for k in range(times)], axis=1
-        )
-        plane = mm(bx3_ref[...], right3(plane))
-        for i, out in enumerate(outs):
-            for k in range(times):
-                out[k, j * span : (j + 1) * span, :] = plane[
-                    i * span : (i + 1) * span, k * lanes : (k + 1) * lanes
-                ]
+    gather_rows(bx_ref, rows_ref, PEERS, 1)
+    bx3_ref[...] = left3(rows_ref[...])
+    fill_sums(ex_ref, ey_ref, ez_ref, sums_ref)
+    begin = lax.axis_index("ta") * total
+    before = ends_ref[:, 0].reshape(modes, lanes)
+    after = ends_ref[:, 1].reshape(modes, lanes)
+    eigen = sums_ref[...]
+    ratios, values = [], []
+    for k in range(total):
+        main, sub, sup = row_terms(eigen, steps_ref, begin + k)
+        inverse = 1.0 / (main - sub * ratios[-1] if k else main)
+        ratios.append(sup * inverse)
+        value = -(sub * inverse) * (values[-1] if k else before)
+        if k == total - 1:
+            value = value - ratios[-1] * after
+        values.append(value)
+    now = values[total - 1]
+    sol_ref[total - 1] = g_ref[total - 1] + now
+    for k in reversed(range(total - 1)):
+        now = values[k] - ratios[k] * now
+        sol_ref[k] = g_ref[k] + now
+
+    for t in range(0, total, 2):
+        for j in range(modes // x):
+            cells = transform_pair(
+                bx3_ref[...], [sol_ref[k, j * x : (j + 1) * x, :] for k in (t, t + 1)]
+            )
+            for k, cell in zip((t, t + 1), cells):
+                for i, out in enumerate(outs):
+                    out[k, j * span : (j + 1) * span, :] = cell[i * span : (i + 1) * span]
 
 
 def return_x(g, ends, sums, bx, steps):
     t, modes, z = g.shape
     x, members = bx.shape[0], len(PEERS)
-    rows = modes // members
     return pl.pallas_call(
         return_body,
-        grid=(t // 2,),
-        in_specs=[SMEM, whole(1, x), SMEM, whole(1, z), whole(x, x), whole(*g.shape), whole(*ends.shape)],
-        out_specs=[pl.BlockSpec((2, rows, z), lambda k: (k, 0, 0))] * members,
-        out_shape=[array(t, rows, z)] * members,
+        in_specs=[SMEM, VMEM, SMEM, VMEM, VMEM, VMEM, VMEM],
+        out_specs=[VMEM] * members,
+        out_shape=[array(t, modes // members, z)] * members,
         scratch_shapes=[
             pltpu.VMEM((t, modes, z), f32),
             pltpu.VMEM((modes, z), f32),

time: 118 us -> 115 us (0.975)
  Pallas kernels: 16.9 us -> 14 us
    pallas_call x4, Pallas kernels: 13.8 us -> 10.9 us  [the longest x1 3.45 us: forward_yz(): pl.pallas_call(forward_body, in_specs=[ANY] * 3, out_specs=[VMEM] * membe...]
where the time goes in v4:
time: 115 us
  blocking collectives  47.2 us (41%)
  starting transfers between devices  33.4 us (29%)
  waiting for transfers between devices  19.8 us (17%)
  Pallas kernels  14 us (12%)
    all_to_all x2, blocking collectives, local(): ends = lax.all_to_all(ends, 'ta', 0, 0, tiled=True)  47.2 us
    ppermute x14, starting transfers between devices, exchange(): moved.append(lax.ppermute(pieces[k], 'gx', pairs))  33.4 us
    ppermute x14, waiting for transfers between devices, exchange(): moved.append(lax.ppermute(pieces[k], 'gx', pairs))  19.8 us
    pallas_call x1, Pallas kernels, forward_yz(): pl.pallas_call(forward_body, in_specs=[ANY] * 3, out_specs=[VMEM] * membe...  3.45 us
    pallas_call x1, Pallas kernels, backward_yz(): pl.pallas_call(backward_body, in_specs=[VMEM] * (2 + members), out_specs=...  2.97 us
    pallas_call x1, Pallas kernels, reduced_terms(): pl.pallas_call(partial(reduced_body, rows), in_specs=[SMEM, VMEM, SMEM, V...  2.75 us
    pallas_call x1, Pallas kernels, return_x(): pl.pallas_call(return_body, in_specs=[SMEM, VMEM, SMEM, VMEM, VMEM, VMEM,...  2.33 us
  transfers between devices with their start and end apart: 14, of which 7 were waited for; matrix products, arithmetic and copies ran while one was open for 0% of the time, Pallas kernels for 2%

profile of v4, /device:TPU:1, one launch (start us, length us, event | category | flops | bytes accessed | tf_op | source)
XLA Modules:
  0.0 114.8 jit_solution(8474261449220054502)
XLA Ops:
  0.0 0.0 copy-start.5
  0.0 0.0 copy-start.4
  0.0 0.0 copy-start
  0.0 3.5 %forward_yz.1 = (f32[8,64,128]{2,1,0:T(8,128)S(1)}, f32[8,64,128]{2,1,0:T(8,128)S(1)}, f32[8,64,128]{2,1,0:T(8,128)S(1)}, f32[8,64,128]{2,1,0:T(8,128)S(1)}, f32...) custom-call(f32[8,8,64,128]{3,2,1,0:T(8,128)} %x_any.1, ...), custom_call_target="tpu_custom_call" | custom-call | flops 603979776 | bytes 4194304 | tf_op jit(solution)/shard_map/forward_yz/pallas_call | solution.py:110
  3.5 3.7 %collective-permute-start = (f32[8,64,128]{2,1,0:T(8,128)S(1)}, f32[8,64,128]{2,1,0:T(8,128)S(1)}, u32[]{:S(2)}, u32[]{:S(2)}) collective-permute-start(f32[8,64,128]{2,1,0:T(8,128)S(1)} %get-tuple-element.34), channel_id=1, source_target_pairs={{0,4},{1,5},{2,6},{3,7},{4,0},{5,1},{6,2},{7,3},{8,12},{9,13},{10,... | collective-permute-start | bytes 786440 | tf_op jit(solution)/shard_map/ppermute | solution.py:33
  7.1 2.8 %collective-permute-start.1 = (f32[8,64,128]{2,1,0:T(8,128)S(1)}, f32[8,64,128]{2,1,0:T(8,128)S(1)}, u32[]{:S(2)}, u32[]{:S(2)}) collective-permute-start(f32[8,64,128]{2,1,0:T(8,128)S(1)} %get-tuple-element.35), channel_id=1, source_target_pairs={{0,5},{1,4},{2,7},{3,6},{4,1},{5,0},{6,3},{7,2},{8,13},{9,12},{10,... | collective-permute-start | bytes 786440 | tf_op jit(solution)/shard_map/ppermute | solution.py:33
  9.9 0.0 collective-permute-start.2
  10.0 2.7 %collective-permute-start.3 = (f32[8,64,128]{2,1,0:T(8,128)S(1)}, f32[8,64,128]{2,1,0:T(8,128)S(1)}, u32[]{:S(2)}, u32[]{:S(2)}) collective-permute-start(f32[8,64,128]{2,1,0:T(8,128)S(1)} %get-tuple-element.37), channel_id=1, source_target_pairs={{0,6},{1,7},{2,0},{3,1},{4,2},{5,3},{6,4},{7,5},{8,14},{9,15},{10,... | collective-permute-start | bytes 786440 | tf_op jit(solution)/shard_map/ppermute | solution.py:33
  12.6 0.0 collective-permute-start.4
  12.6 0.0 collective-permute-done.refs_1_
  12.6 5.6 %collective-permute-start.5 = (f32[8,64,128]{2,1,0:T(8,128)S(1)}, f32[8,64,128]{2,1,0:T(8,128)S(1)}, u32[]{:S(2)}, u32[]{:S(2)}) collective-permute-start(f32[8,64,128]{2,1,0:T(8,128)S(1)} %get-tuple-element.39), channel_id=1, source_target_pairs={{0,7},{1,6},{2,1},{3,0},{4,3},{5,2},{6,5},{7,4},{8,15},{9,14},{10,... | collective-permute-start | bytes 786440 | tf_op jit(solution)/shard_map/ppermute | solution.py:33
  18.2 3.6 %collective-permute-done.1.refs_2_ = f32[8,64,128]{2,1,0:T(8,128)S(1)} collective-permute-done((f32[8,64,128]{2,1,0:T(8,128)S(1)}, f32[8,64,128]{2,1,0:T(8,128)S(1)}, u32[]{:S(2)}, u32[]{:S(2)}) %collective-permute-start.1) | collective-permute-done | bytes 262176 | tf_op jit(solution)/shard_map/ppermute | solution.py:33
  21.8 0.0 collective-permute-start.6
  21.8 0.0 copy-done.3
  21.8 0.0 copy-done.5
  21.8 0.0 copy-done.6
  21.8 0.0 copy-done.4
  21.8 2.7 %reduced_terms.1 = (f32[32,16,128]{2,1,0:T(8,128)S(1)}, f32[32,16,128]{2,1,0:T(8,128)S(1)}, f32[32,16,128]{2,1,0:T(8,128)S(1)}, f32[32,16,128]{2,1,0:T(8,128)S(1...) custom-call(f32[256]{0:T(256)S(1)} %copy-done.3, f32[1,64]{1,0:T(1,128)S(1)} %bitcast.2, f32[64]{0:T(128)S(1)} %copy-done.5, ...), custom_call_target="tpu_custom_call" | custom-call | flops 20971520 | bytes 1572864 | tf_op jit(solution)/shard_map/reduced_terms/pallas_call | solution.py:272
  24.6 0.8 collective-permute-done.2.refs_3_
  25.4 0.0 collective-permute-done.3.refs_4_
  25.4 5.6 %collective-permute-done.4.refs_5_ = f32[8,64,128]{2,1,0:T(8,128)S(1)} collective-permute-done((f32[8,64,128]{2,1,0:T(8,128)S(1)}, f32[8,64,128]{2,1,0:T(8,128)S(1)}, u32[]{:S(2)}, u32[]{:S(2)}) %collective-permute-start.4) | collective-permute-done | bytes 262176 | tf_op jit(solution)/shard_map/ppermute | solution.py:33
  31.1 0.1 collective-permute-done.5.refs_6_
  31.1 0.0 collective-permute-done.6.refs_7_
  31.2 0.0 copy-done
  31.2 2.2 %eliminate.1 = (f32[8,512,128]{2,1,0:T(8,128)S(1)}, f32[32,2,16,128]{3,2,1,0:T(8,128)S(1)}) custom-call(f32[256]{0:T(256)S(1)} %copy-done.3, f32[1,64]{1,0:T(1,128)S(1)} %bitcast.3, f32[64]{0:T(128)S(1)} %copy-done.5, f32[1,128]{1,0:T(1,128)S(1)} %bitcast.6, f32[64,64]{1,0:T(8,128)S(1)} %copy-done, f32[8,64,128]{2,1,0:T(8,128)S(1)} %get-tuple-element.33.refs_0_, ...), custom_call_target="tpu_custom_call" | custom-call | flops 201326592 | bytes 4194304 | tf_op jit(solution)/shard_map/eliminate/pallas_call | solution.py:371
  33.3 25.1 %all_to_all.10.g_ref = f32[32,2,16,128]{3,2,1,0:T(8,128)S(1)} all-to-all(f32[32,2,16,128]{3,2,1,0:T(8,128)S(1)} %get-tuple-element.42), channel_id=1, replica_groups=mesh['ta'=32,'gx'=8] {'ta'}, dimensions={0} | all-to-all | bytes 1048576 | tf_op jit(solution)/shard_map/all_to_all | solution.py:457
  58.4 0.3 interface_solve.1
  58.8 0.0 copy-start.1
  58.8 0.0 copy-start.2
  58.8 22.1 %all_to_all.11.ends_ref = f32[32,2,16,128]{3,2,1,0:T(8,128)S(1)} all-to-all(f32[32,2,16,128]{3,2,1,0:T(8,128)S(1)} %interface_solve.1), channel_id=1, replica_groups=mesh['ta'=32,'gx'=8] {'ta'}, dimensions={0} | all-to-all | bytes 1048576 | tf_op jit(solution)/shard_map/all_to_all | solution.py:459
  80.9 2.3 %return_x.1 = (f32[8,64,128]{2,1,0:T(8,128)S(1)}, f32[8,64,128]{2,1,0:T(8,128)S(1)}, f32[8,64,128]{2,1,0:T(8,128)S(1)}, f32[8,64,128]{2,1,0:T(8,128)S(1)}, f32[8...) custom-call(f32[256]{0:T(256)S(1)} %copy-done.3, ...), custom_call_target="tpu_custom_call" | custom-call | flops 201326592 | bytes 4194304 | tf_op jit(solution)/shard_map/return_x/pallas_call | solution.py:428
  83.2 2.9 %collective-permute-start.7 = (f32[8,64,128]{2,1,0:T(8,128)S(1)}, f32[8,64,128]{2,1,0:T(8,128)S(1)}, u32[]{:S(2)}, u32[]{:S(2)}) collective-permute-start(f32[8,64,128]{2,1,0:T(8,128)S(1)} %get-tuple-element.50), channel_id=1, source_target_pairs={{0,4},{1,5},{2,6},{3,7},{4,0},{5,1},{6,2},{7,3},{8,12},{9,13},{10,... | collective-permute-start | bytes 786440 | tf_op jit(solution)/shard_map/ppermute | solution.py:33
  86.1 4.4 %collective-permute-start.8 = (f32[8,64,128]{2,1,0:T(8,128)S(1)}, f32[8,64,128]{2,1,0:T(8,128)S(1)}, u32[]{:S(2)}, u32[]{:S(2)}) collective-permute-start(f32[8,64,128]{2,1,0:T(8,128)S(1)} %get-tuple-element.51), channel_id=1, source_target_pairs={{0,5},{1,4},{2,7},{3,6},{4,1},{5,0},{6,3},{7,2},{8,13},{9,12},{10,... | collective-permute-start | bytes 786440 | tf_op jit(solution)/shard_map/ppermute | solution.py:33
  90.5 1.2 %collective-permute-start.9 = (f32[8,64,128]{2,1,0:T(8,128)S(1)}, f32[8,64,128]{2,1,0:T(8,128)S(1)}, u32[]{:S(2)}, u32[]{:S(2)}) collective-permute-start(f32[8,64,128]{2,1,0:T(8,128)S(1)} %get-tuple-element.52), channel_id=1, source_target_pairs={{0,2},{1,3},{2,4},{3,5},{4,6},{5,7},{6,0},{7,1},{8,10},{9,11},{10,... | collective-permute-start | bytes 786440 | tf_op jit(solution)/shard_map/ppermute | solution.py:33
  91.7 1.5 %collective-permute-start.10 = (f32[8,64,128]{2,1,0:T(8,128)S(1)}, f32[8,64,128]{2,1,0:T(8,128)S(1)}, u32[]{:S(2)}, u32[]{:S(2)}) collective-permute-start(f32[8,64,128]{2,1,0:T(8,128)S(1)} %get-tuple-element.53), channel_id=1, source_target_pairs={{0,6},{1,7},{2,0},{3,1},{4,2},{5,3},{6,4},{7,5},{8,14},{9,15},{10,... | collective-permute-start | bytes 786440 | tf_op jit(solution)/shard_map/ppermute | solution.py:33
  93.1 0.0 collective-permute-start.11
  93.1 0.0 collective-permute-done.7.refs_1_
  93.1 6.4 %collective-permute-start.12 = (f32[8,64,128]{2,1,0:T(8,128)S(1)}, f32[8,64,128]{2,1,0:T(8,128)S(1)}, u32[]{:S(2)}, u32[]{:S(2)}) collective-permute-start(f32[8,64,128]{2,1,0:T(8,128)S(1)} %get-tuple-element.55), channel_id=1, source_target_pairs={{0,7},{1,6},{2,1},{3,0},{4,3},{5,2},{6,5},{7,4},{8,15},{9,14},{10,... | collective-permute-start | bytes 786440 | tf_op jit(solution)/shard_map/ppermute | solution.py:33
  99.6 0.8 collective-permute-done.8.refs_2_
  100.4 2.3 %collective-permute-start.13 = (f32[8,64,128]{2,1,0:T(8,128)S(1)}, f32[8,64,128]{2,1,0:T(8,128)S(1)}, u32[]{:S(2)}, u32[]{:S(2)}) collective-permute-start(f32[8,64,128]{2,1,0:T(8,128)S(1)} %get-tuple-element.56), channel_id=1, source_target_pairs={{0,1},{1,0},{2,3},{3,2},{4,5},{5,4},{6,7},{7,6},{8,9},{9,8},{10,11... | collective-permute-start | bytes 786440 | tf_op jit(solution)/shard_map/ppermute | solution.py:33
  102.7 3.3 %collective-permute-done.9.refs_3_ = f32[8,64,128]{2,1,0:T(8,128)S(1)} collective-permute-done((f32[8,64,128]{2,1,0:T(8,128)S(1)}, f32[8,64,128]{2,1,0:T(8,128)S(1)}, u32[]{:S(2)}, u32[]{:S(2)}) %collective-permute-start.9) | collective-permute-done | bytes 262176 | tf_op jit(solution)/shard_map/ppermute | solution.py:33
  106.0 0.0 collective-permute-done.10.refs_4_
  106.0 5.6 %collective-permute-done.11.refs_5_ = f32[8,64,128]{2,1,0:T(8,128)S(1)} collective-permute-done((f32[8,64,128]{2,1,0:T(8,128)S(1)}, f32[8,64,128]{2,1,0:T(8,128)S(1)}, u32[]{:S(2)}, u32[]{:S(2)}) %collective-permute-start.11) | collective-permute-done | bytes 262176 | tf_op jit(solution)/shard_map/ppermute | solution.py:33
  111.6 0.0 collective-permute-done.12.refs_6_
  111.6 0.0 collective-permute-done.13.refs_7_
  111.6 0.0 copy-done.1
  111.6 0.0 copy-done.2
  111.6 3.0 %backward_yz.1 = f32[8,8,64,128]{3,2,1,0:T(8,128)} custom-call(f32[64,64]{1,0:T(8,128)S(1)} %copy-done.2, f32[128,128]{1,0:T(8,128)S(1)} %copy-done.1, f32[8,64,128]{2,1,0:T(8,128)S(1)} %get-tuple-element.49.refs_0_, f32[8,64,128]{2,1,0:T(8,128)S(1)} %collective-permute-done.7.refs_1_, f32[8,64,128]{2,1,0:T(8,128)S(1)} %collective-permute-done.8.refs_2_, ...), custom_call_target="tpu_custom_call" | custom-call | flops 603979776 | bytes 4194304 | tf_op jit(solution)/shard_map/backward_yz/pallas_call | solution.py:172
  (2 shorter events, 0.0 us)
Async XLA Ops:
  0.0 21.8 %copy-start.3 = (f32[256]{0:T(256)S(1)}, f32[256]{0:T(256)}, u32[]{:S(2)}) copy-start(f32[256]{0:T(256)} %steps_ref.5) | copy-start | bytes 3076
  0.0 21.8 %copy-start.5 = (f32[64]{0:T(128)S(1)}, f32[64]{0:T(128)}, u32[]{:S(2)}) copy-start(f32[64]{0:T(128)} %ey_ref.5) | copy-start | bytes 772
  0.0 21.8 %copy-start.6 = (f32[128]{0:T(128)S(1)}, f32[128]{0:T(128)}, u32[]{:S(2)}) copy-start(f32[128]{0:T(128)} %param.14) | copy-start | bytes 1540
  0.0 21.8 %copy-start.4 = (f32[64]{0:T(128)S(1)}, f32[64]{0:T(128)}, u32[]{:S(2)}) copy-start(f32[64]{0:T(128)} %param.12) | copy-start | bytes 772
  0.0 31.1 %copy-start = (f32[64,64]{1,0:T(8,128)S(1)}, f32[64,64]{1,0:T(8,128)}, u32[]{:S(2)}) copy-start(f32[64,64]{1,0:T(8,128)} %bx_ref.3) | copy-start | bytes 49156
  3.5 9.1 %collective-permute-start = (f32[8,64,128]{2,1,0:T(8,128)S(1)}, f32[8,64,128]{2,1,0:T(8,128)S(1)}, u32[]{:S(2)}, u32[]{:S(2)}) collective-permute-start(f32[8,64,128]{2,1,0:T(8,128)S(1)} %get-tuple-element.34), channel_id=1, source_target_pairs={{0,4},{1,5},{2,6},{3,7},{4,0},{5,1},{6,2},{7,3},{8,12},{9,13},{10,... | collective-permute-start | bytes 786440 | tf_op jit(solution)/shard_map/ppermute | solution.py:33
  7.1 14.6 %collective-permute-start.1 = (f32[8,64,128]{2,1,0:T(8,128)S(1)}, f32[8,64,128]{2,1,0:T(8,128)S(1)}, u32[]{:S(2)}, u32[]{:S(2)}) collective-permute-start(f32[8,64,128]{2,1,0:T(8,128)S(1)} %get-tuple-element.35), channel_id=1, source_target_pairs={{0,5},{1,4},{2,7},{3,6},{4,1},{5,0},{6,3},{7,2},{8,13},{9,12},{10,... | collective-permute-start | bytes 786440 | tf_op jit(solution)/shard_map/ppermute | solution.py:33
  9.9 15.5 %collective-permute-start.2 = (f32[8,64,128]{2,1,0:T(8,128)S(1)}, f32[8,64,128]{2,1,0:T(8,128)S(1)}, u32[]{:S(2)}, u32[]{:S(2)}) collective-permute-start(f32[8,64,128]{2,1,0:T(8,128)S(1)} %get-tuple-element.36), channel_id=1, source_target_pairs={{0,2},{1,3},{2,4},{3,5},{4,6},{5,7},{6,0},{7,1},{8,10},{9,11},{10,... | collective-permute-start | bytes 786440 | tf_op jit(solution)/shard_map/ppermute | solution.py:33
  10.0 15.5 %collective-permute-start.3 = (f32[8,64,128]{2,1,0:T(8,128)S(1)}, f32[8,64,128]{2,1,0:T(8,128)S(1)}, u32[]{:S(2)}, u32[]{:S(2)}) collective-permute-start(f32[8,64,128]{2,1,0:T(8,128)S(1)} %get-tuple-element.37), channel_id=1, source_target_pairs={{0,6},{1,7},{2,0},{3,1},{4,2},{5,3},{6,4},{7,5},{8,14},{9,15},{10,... | collective-permute-start | bytes 786440 | tf_op jit(solution)/shard_map/ppermute | solution.py:33
  12.6 18.4 %collective-permute-start.4 = (f32[8,64,128]{2,1,0:T(8,128)S(1)}, f32[8,64,128]{2,1,0:T(8,128)S(1)}, u32[]{:S(2)}, u32[]{:S(2)}) collective-permute-start(f32[8,64,128]{2,1,0:T(8,128)S(1)} %get-tuple-element.38), channel_id=1, source_target_pairs={{0,3},{1,2},{2,5},{3,4},{4,7},{5,6},{6,1},{7,0},{8,11},{9,10},{10,... | collective-permute-start | bytes 786440 | tf_op jit(solution)/shard_map/ppermute | solution.py:33
  12.6 18.5 %collective-permute-start.5 = (f32[8,64,128]{2,1,0:T(8,128)S(1)}, f32[8,64,128]{2,1,0:T(8,128)S(1)}, u32[]{:S(2)}, u32[]{:S(2)}) collective-permute-start(f32[8,64,128]{2,1,0:T(8,128)S(1)} %get-tuple-element.39), channel_id=1, source_target_pairs={{0,7},{1,6},{2,1},{3,0},{4,3},{5,2},{6,5},{7,4},{8,15},{9,14},{10,... | collective-permute-start | bytes 786440 | tf_op jit(solution)/shard_map/ppermute | solution.py:33
  21.8 9.4 %collective-permute-start.6 = (f32[8,64,128]{2,1,0:T(8,128)S(1)}, f32[8,64,128]{2,1,0:T(8,128)S(1)}, u32[]{:S(2)}, u32[]{:S(2)}) collective-permute-start(f32[8,64,128]{2,1,0:T(8,128)S(1)} %get-tuple-element.40), channel_id=1, source_target_pairs={{0,1},{1,0},{2,3},{3,2},{4,5},{5,4},{6,7},{7,6},{8,9},{9,8},{10,11... | collective-permute-start | bytes 786440 | tf_op jit(solution)/shard_map/ppermute | solution.py:33
  58.8 52.9 %copy-start.1 = (f32[128,128]{1,0:T(8,128)S(1)}, f32[128,128]{1,0:T(8,128)}, u32[]{:S(2)}) copy-start(f32[128,128]{1,0:T(8,128)} %bz_ref.1) | copy-start | bytes 196612
  58.8 52.9 %copy-start.2 = (f32[64,64]{1,0:T(8,128)S(1)}, f32[64,64]{1,0:T(8,128)}, u32[]{:S(2)}) copy-start(f32[64,64]{1,0:T(8,128)} %by_ref.1) | copy-start | bytes 49156
  83.2 9.9 %collective-permute-start.7 = (f32[8,64,128]{2,1,0:T(8,128)S(1)}, f32[8,64,128]{2,1,0:T(8,128)S(1)}, u32[]{:S(2)}, u32[]{:S(2)}) collective-permute-start(f32[8,64,128]{2,1,0:T(8,128)S(1)} %get-tuple-element.50), channel_id=1, source_target_pairs={{0,4},{1,5},{2,6},{3,7},{4,0},{5,1},{6,2},{7,3},{8,12},{9,13},{10,... | collective-permute-start | bytes 786440 | tf_op jit(solution)/shard_map/ppermute | solution.py:33
  86.1 14.4 %collective-permute-start.8 = (f32[8,64,128]{2,1,0:T(8,128)S(1)}, f32[8,64,128]{2,1,0:T(8,128)S(1)}, u32[]{:S(2)}, u32[]{:S(2)}) collective-permute-start(f32[8,64,128]{2,1,0:T(8,128)S(1)} %get-tuple-element.51), channel_id=1, source_target_pairs={{0,5},{1,4},{2,7},{3,6},{4,1},{5,0},{6,3},{7,2},{8,13},{9,12},{10,... | collective-permute-start | bytes 786440 | tf_op jit(solution)/shard_map/ppermute | solution.py:33
  90.5 15.5 %collective-permute-start.9 = (f32[8,64,128]{2,1,0:T(8,128)S(1)}, f32[8,64,128]{2,1,0:T(8,128)S(1)}, u32[]{:S(2)}, u32[]{:S(2)}) collective-permute-start(f32[8,64,128]{2,1,0:T(8,128)S(1)} %get-tuple-element.52), channel_id=1, source_target_pairs={{0,2},{1,3},{2,4},{3,5},{4,6},{5,7},{6,0},{7,1},{8,10},{9,11},{10,... | collective-permute-start | bytes 786440 | tf_op jit(solution)/shard_map/ppermute | solution.py:33
  91.7 14.3 %collective-permute-start.10 = (f32[8,64,128]{2,1,0:T(8,128)S(1)}, f32[8,64,128]{2,1,0:T(8,128)S(1)}, u32[]{:S(2)}, u32[]{:S(2)}) collective-permute-start(f32[8,64,128]{2,1,0:T(8,128)S(1)} %get-tuple-element.53), channel_id=1, source_target_pairs={{0,6},{1,7},{2,0},{3,1},{4,2},{5,3},{6,4},{7,5},{8,14},{9,15},{10,... | collective-permute-start | bytes 786440 | tf_op jit(solution)/shard_map/ppermute | solution.py:33
  93.1 18.5 %collective-permute-start.11 = (f32[8,64,128]{2,1,0:T(8,128)S(1)}, f32[8,64,128]{2,1,0:T(8,128)S(1)}, u32[]{:S(2)}, u32[]{:S(2)}) collective-permute-start(f32[8,64,128]{2,1,0:T(8,128)S(1)} %get-tuple-element.54), channel_id=1, source_target_pairs={{0,3},{1,2},{2,5},{3,4},{4,7},{5,6},{6,1},{7,0},{8,11},{9,10},{10,... | collective-permute-start | bytes 786440 | tf_op jit(solution)/shard_map/ppermute | solution.py:33
  93.1 18.5 %collective-permute-start.12 = (f32[8,64,128]{2,1,0:T(8,128)S(1)}, f32[8,64,128]{2,1,0:T(8,128)S(1)}, u32[]{:S(2)}, u32[]{:S(2)}) collective-permute-start(f32[8,64,128]{2,1,0:T(8,128)S(1)} %get-tuple-element.55), channel_id=1, source_target_pairs={{0,7},{1,6},{2,1},{3,0},{4,3},{5,2},{6,5},{7,4},{8,15},{9,14},{10,... | collective-permute-start | bytes 786440 | tf_op jit(solution)/shard_map/ppermute | solution.py:33
  100.4 11.2 %collective-permute-start.13 = (f32[8,64,128]{2,1,0:T(8,128)S(1)}, f32[8,64,128]{2,1,0:T(8,128)S(1)}, u32[]{:S(2)}, u32[]{:S(2)}) collective-permute-start(f32[8,64,128]{2,1,0:T(8,128)S(1)} %get-tuple-element.56), channel_id=1, source_target_pairs={{0,1},{1,0},{2,3},{3,2},{4,5},{5,4},{6,7},{7,6},{8,9},{9,8},{10,11... | collective-permute-start | bytes 786440 | tf_op jit(solution)/shard_map/ppermute | solution.py:33

commit v5 on v4

--- a/solution.py
+++ b/solution.py
@@ -129,19 +129,13 @@
     )(x, by, bz)
 
 
-def backward_body(by_ref, bz_ref, *refs):
-    pieces, refs = refs[: len(PEERS)], refs[len(PEERS) :]
-    out_any, out_ref, turn_ref, rows_ref, by3_ref, bz3_ref, sem = refs
+def backward_body(by3_ref, bz3_ref, *refs):
+    pieces, (out_any, out_ref, sem) = refs[: len(PEERS)], refs[len(PEERS) :]
     total, rows, y, z = out_ref.shape
     span = y // len(pieces)
-    turn_ref[...] = by_ref[...].T
-    gather_rows(turn_ref, rows_ref, PEERS, -1)
-    by3_ref[...] = left3(rows_ref[...].T)
-    bz3_ref[...] = right3(bz_ref[...].T)
-
     copies = []
-    for first in range(0, total, 4):
-        times = range(first, first + 4)
+    for first in range(0, total, 2):
+        times = (first, first + 1)
         vol = []
         for a in range(rows):
             plane = jnp.concatenate(
@@ -164,9 +158,9 @@
         copy.wait()
 
 
-def backward_yz(pieces, by, bz):
+def backward_yz(pieces, by3, bz3):
     members = len(pieces)
-    y, z = by.shape[0], bz.shape[0]
+    y, z = by3.shape[0], bz3.shape[1]
     t, rows = pieces[0].shape[:2]
     a = rows * members // y
     return pl.pallas_call(
@@ -174,18 +168,11 @@
         in_specs=[VMEM] * (2 + members),
         out_specs=ANY,
         out_shape=array(t, a, y, z),
-        scratch_shapes=[
-            pltpu.VMEM((t, a, y, z), f32),
-            pltpu.VMEM((y, y), f32),
-            pltpu.VMEM((y, y), f32),
-            pltpu.VMEM((y, 3 * y), bf16),
-            pltpu.VMEM((3 * z, z), bf16),
-            pltpu.SemaphoreType.DMA((t,)),
-        ],
+        scratch_shapes=[pltpu.VMEM((t, a, y, z), f32), pltpu.SemaphoreType.DMA((t,))],
         compiler_params=params(),
         cost_estimate=cost(6 * t * a * y * z * (y + z), 8 * t * a * y * z),
         name="backward_yz",
-    )(by, bz, *pieces)
+    )(by3, bz3, *pieces)
 
 
 def length(steps_ref, at):
@@ -209,12 +196,72 @@
     return (along_x + ey_ref[j]) + ez_ref[...]
 
 
-def fill_sums(ex_ref, ey_ref, ez_ref, sums_ref):
+def prepare_body(steps_ref, ex_ref, ey_ref, ez_ref, bx_ref, by_ref, bz_ref, *refs):
+    inv_ref, mul_ref, ratio_ref, v_ref, w_ref, bx3_ref, bx3_back_ref, by3_ref, bz3_ref = refs[:9]
+    sums_ref, turn_ref, rows_ref = refs[9:]
+    total, modes, lanes = inv_ref.shape
     x, members = ex_ref.shape[1], len(PEERS)
+    gather_rows(bx_ref, rows_ref, PEERS, -1)
+    bx3_ref[...] = left3(rows_ref[...].T)
+    gather_rows(bx_ref, rows_ref, PEERS, 1)
+    bx3_back_ref[...] = left3(rows_ref[...])
+    turn_ref[...] = by_ref[...].T
+    gather_rows(turn_ref, rows_ref, PEERS, -1)
+    by3_ref[...] = left3(rows_ref[...].T)
+    bz3_ref[...] = right3(bz_ref[...].T)
+
     span = ey_ref.shape[0] // members
     member = lax.axis_index("gx")
     for j in range(span):
         sums_ref[j * x : (j + 1) * x] = mode_sums(ex_ref, ey_ref, ez_ref, member * span + j)
+    begin = lax.axis_index("ta") * total
+    size = 32
+
+    def block(n, carry):
+        mine = pl.ds(pl.multiple_of(n * size, size), size)
+        eigen = sums_ref[mine, :]
+        ratios, fronts = [], []
+        for k in range(total):
+            main, sub, sup = row_terms(eigen, steps_ref, begin + k)
+            inverse = 1.0 / (main - sub * ratios[-1] if k else main)
+            factor = sub * inverse
+            ratios.append(sup * inverse)
+            fronts.append(-factor * fronts[-1] if k else factor)
+            inv_ref[k, mine, :] = inverse
+            mul_ref[k, mine, :] = factor
+            ratio_ref[k, mine, :] = ratios[-1]
+        low, last = fronts[-1], ratios[-1]
+        v_ref[total - 1, mine, :] = low
+        w_ref[total - 1, mine, :] = last
+        for k in reversed(range(total - 1)):
+            low = fronts[k] - ratios[k] * low
+            last = -ratios[k] * last
+            v_ref[k, mine, :] = low
+            w_ref[k, mine, :] = last
+        return carry
+
+    lax.fori_loop(0, modes // size, block, 0)
+
+
+def prepare(steps, sums, bx, by, bz, rows):
+    x, y, z = bx.shape[0], by.shape[0], bz.shape[0]
+    modes = x * y // len(PEERS)
+    table = lambda *shape: jax.ShapeDtypeStruct(shape, bf16)
+    return pl.pallas_call(
+        prepare_body,
+        in_specs=[SMEM, VMEM, SMEM, VMEM, VMEM, VMEM, VMEM],
+        out_specs=[VMEM] * 9,
+        out_shape=[array(rows, modes, z)] * 5
+        + [table(x, 3 * x), table(x, 3 * x), table(y, 3 * y), table(3 * z, z)],
+        scratch_shapes=[
+            pltpu.VMEM((modes, z), f32),
+            pltpu.VMEM((y, y), f32),
+            pltpu.VMEM((x, x), f32),
+        ],
+        compiler_params=params(),
+        cost_estimate=cost(30 * rows * modes * z, 20 * rows * modes * z),
+        name="prepare",
+    )(steps, *sums, bx, by, bz)
 
 
 def reduced_body(rows, steps_ref, ex_ref, ey_ref, ez_ref, cl_ref, e_ref, a_ref, k_ref, b_ref, q_ref, sums_ref):
@@ -325,17 +372,11 @@
     return both[:, :lanes], both[:, lanes:]
 
 
-def eliminate_body(steps_ref, ex_ref, ey_ref, ez_ref, bx_ref, *refs):
-    pieces, refs = refs[: len(PEERS)], refs[len(PEERS) :]
-    g_ref, ends_ref, ratio_ref, sums_ref, rows_ref, bx3_ref = refs
+def eliminate_body(bx3_ref, inv_ref, mul_ref, ratio_ref, *refs):
+    pieces, (g_ref, ends_ref) = refs[:-2], refs[-2:]
     total, modes, lanes = g_ref.shape
-    x = bx_ref.shape[0]
+    x = bx3_ref.shape[0]
     span = x // len(pieces)
-    gather_rows(bx_ref, rows_ref, PEERS, -1)
-    bx3_ref[...] = left3(rows_ref[...].T)
-    fill_sums(ex_ref, ey_ref, ez_ref, sums_ref)
-    begin = lax.axis_index("ta") * total
-
     for t in range(0, total, 2):
         for j in range(modes // x):
             mine = slice(j * x, (j + 1) * x)
@@ -347,13 +388,8 @@
                 ],
             )
             for k, values in zip((t, t + 1), spectral):
-                main, sub, sup = row_terms(sums_ref[mine], steps_ref, begin + k)
-                if k:
-                    main = main - sub * ratio_ref[k - 1, mine]
-                    values = values - sub * g_ref[k - 1, mine]
-                inverse = 1.0 / main
-                ratio_ref[k, mine] = sup * inverse
-                g_ref[k, mine] = values * inverse
+                values = values * inv_ref[k, mine]
+                g_ref[k, mine] = values - mul_ref[k, mine] * g_ref[k - 1, mine] if k else values
 
     split_shape = (ends_ref.shape[0], modes // ends_ref.shape[0], lanes)
     now = g_ref[total - 1]
@@ -364,82 +400,56 @@
     ends_ref[:, 0] = now.reshape(split_shape)
 
 
-def eliminate(pieces, sums, bx, steps, count):
+def eliminate(pieces, bx3, factors, count):
     t, rows, z = pieces[0].shape
-    x = bx.shape[0]
+    x = bx3.shape[0]
     modes = rows * len(pieces)
     return pl.pallas_call(
         eliminate_body,
-        in_specs=[SMEM, VMEM, SMEM, VMEM, VMEM] + [VMEM] * len(pieces),
+        in_specs=[VMEM] * (4 + len(pieces)),
         out_specs=[VMEM] * 2,
         out_shape=[array(t, modes, z), array(count, 2, modes // count, z)],
-        scratch_shapes=[
-            pltpu.VMEM((t, modes, z), f32),
-            pltpu.VMEM((modes, z), f32),
-            pltpu.VMEM((x, x), f32),
-            pltpu.VMEM((x, 3 * x), bf16),
-        ],
-        compiler_params=params(),
-        cost_estimate=cost(6 * t * modes * x * z, 8 * t * modes * z),
+        compiler_params=params(),
+        cost_estimate=cost(6 * t * modes * x * z, 20 * t * modes * z),
         name="eliminate",
-    )(steps, *sums, bx, *pieces)
-
-
-def return_body(steps_ref, ex_ref, ey_ref, ez_ref, bx_ref, g_ref, ends_ref, *refs):
-    outs, (sol_ref, sums_ref, rows_ref, bx3_ref) = refs[:-4], refs[-4:]
+    )(bx3, *factors, *pieces)
+
+
+def return_body(bx3_ref, v_ref, w_ref, g_ref, ends_ref, *outs):
     total, modes, lanes = g_ref.shape
-    x = bx_ref.shape[0]
+    x = bx3_ref.shape[0]
     span = x // len(outs)
-    gather_rows(bx_ref, rows_ref, PEERS, 1)
-    bx3_ref[...] = left3(rows_ref[...])
-    fill_sums(ex_ref, ey_ref, ez_ref, sums_ref)
-    begin = lax.axis_index("ta") * total
-    before = ends_ref[:, 0].reshape(modes, lanes)
-    after = ends_ref[:, 1].reshape(modes, lanes)
-    eigen = sums_ref[...]
-    ratios, values = [], []
-    for k in range(total):
-        main, sub, sup = row_terms(eigen, steps_ref, begin + k)
-        inverse = 1.0 / (main - sub * ratios[-1] if k else main)
-        ratios.append(sup * inverse)
-        value = -(sub * inverse) * (values[-1] if k else before)
-        if k == total - 1:
-            value = value - ratios[-1] * after
-        values.append(value)
-    now = values[total - 1]
-    sol_ref[total - 1] = g_ref[total - 1] + now
-    for k in reversed(range(total - 1)):
-        now = values[k] - ratios[k] * now
-        sol_ref[k] = g_ref[k] + now
-
-    for t in range(0, total, 2):
-        for j in range(modes // x):
+    share = modes // ends_ref.shape[0]
+    for j in range(modes // x):
+        mine = slice(j * x, (j + 1) * x)
+        owners = slice(j * x // share, (j + 1) * x // share)
+        before = ends_ref[owners, 0].reshape(x, lanes)
+        after = ends_ref[owners, 1].reshape(x, lanes)
+        for t in range(0, total, 2):
             cells = transform_pair(
-                bx3_ref[...], [sol_ref[k, j * x : (j + 1) * x, :] for k in (t, t + 1)]
+                bx3_ref[...],
+                [
+                    g_ref[k, mine] - v_ref[k, mine] * before - w_ref[k, mine] * after
+                    for k in (t, t + 1)
+                ],
             )
             for k, cell in zip((t, t + 1), cells):
                 for i, out in enumerate(outs):
                     out[k, j * span : (j + 1) * span, :] = cell[i * span : (i + 1) * span]
 
 
-def return_x(g, ends, sums, bx, steps):
+def return_x(g, ends, bx3, v, w):
     t, modes, z = g.shape
-    x, members = bx.shape[0], len(PEERS)
+    x, members = bx3.shape[0], len(PEERS)
     return pl.pallas_call(
         return_body,
-        in_specs=[SMEM, VMEM, SMEM, VMEM, VMEM, VMEM, VMEM],
+        in_specs=[VMEM] * 5,
         out_specs=[VMEM] * members,
         out_shape=[array(t, modes // members, z)] * members,
-        scratch_shapes=[
-            pltpu.VMEM((t, modes, z), f32),
-            pltpu.VMEM((modes, z), f32),
-            pltpu.VMEM((x, x), f32),
-            pltpu.VMEM((x, 3 * x), bf16),
-        ],
-        compiler_params=params(),
-        cost_estimate=cost(6 * t * modes * x * z, 8 * t * modes * z),
+        compiler_params=params(),
+        cost_estimate=cost(6 * t * modes * x * z, 16 * t * modes * z),
         name="return_x",
-    )(steps, *sums, bx, g, ends)
+    )(bx3, v, w, g, ends)
 
 
 def local(right_side, basis_x, basis_y, basis_z, eig_x, eig_y, eig_z, steps):
@@ -452,13 +462,14 @@
     sent = forward_yz(hbm(right_side), hbm(basis_y), hbm(basis_z))
     moved = exchange(sent, PEERS)
     terms = list(reduced_terms(steps, sums, count, rows, share))
-    moved[0], terms[0] = lax.optimization_barrier((moved[0], terms[0]))
-    g, ends = eliminate(moved, sums, basis_x, steps, count)
+    *factors, v, w, bx3, bx3_back, by3, bz3 = prepare(steps, sums, basis_x, basis_y, basis_z, rows)
+    moved[0], terms[0], bx3 = lax.optimization_barrier((moved[0], terms[0], bx3))
+    g, ends = eliminate(moved, bx3, factors, count)
     ends = lax.all_to_all(ends, "ta", 0, 0, tiled=True)
     ends = interface_solve(ends, terms)
     ends = lax.all_to_all(ends, "ta", 0, 0, tiled=True)
-    moved = exchange(return_x(g, ends, sums, basis_x, steps), PEERS)
-    return backward_yz(moved, basis_y, basis_z)
+    moved = exchange(return_x(g, ends, bx3_back, v, w), PEERS)
+    return backward_yz(moved, by3, bz3)
 
 
 def solution(mesh):

time: 115 us -> 112 us (0.974)
  waiting for transfers between devices: 19.8 us -> 17.3 us
    ppermute x14, waiting for transfers between devices: 19.8 us -> 17.3 us  [exchange(): moved.append(lax.ppermute(pieces[k], 'gx', pairs))]
    pallas_call x2 -> x3, Pallas kernels: 4.48 us -> 4.23 us  [the longest x1 2.52 us: prepare(): pl.pallas_call(prepare_body, in_specs=[SMEM, VMEM, SMEM, VMEM, VMEM, VMEM...]
  transfers between devices with their start and end apart: 14 -> 14, of which waited for: 7 -> 6; matrix products, arithmetic and copies ran while one was open for 0% -> 0% of each run, Pallas kernels for 2% -> 5%
where the time goes in v5:
time: 112 us; the launch traced here: 111 us
  blocking collectives  47 us (42%)
  starting transfers between devices  33.4 us (30%)
  waiting for transfers between devices  17.3 us (15%)
  Pallas kernels  13.4 us (12%)
    all_to_all x2, blocking collectives, local(): ends = lax.all_to_all(ends, 'ta', 0, 0, tiled=True)  47 us
    ppermute x14, starting transfers between devices, exchange(): moved.append(lax.ppermute(pieces[k], 'gx', pairs))  33.4 us
    ppermute x14, waiting for transfers between devices, exchange(): moved.append(lax.ppermute(pieces[k], 'gx', pairs))  17.3 us
    pallas_call x1, Pallas kernels, forward_yz(): pl.pallas_call(forward_body, in_specs=[ANY] * 3, out_specs=[VMEM] * membe...  3.5 us
    pallas_call x1, Pallas kernels, reduced_terms(): pl.pallas_call(partial(reduced_body, rows), in_specs=[SMEM, VMEM, SMEM, V...  2.75 us
    pallas_call x1, Pallas kernels, backward_yz(): pl.pallas_call(backward_body, in_specs=[VMEM] * (2 + members), out_specs=...  2.53 us
    pallas_call x1, Pallas kernels, prepare(): pl.pallas_call(prepare_body, in_specs=[SMEM, VMEM, SMEM, VMEM, VMEM, VMEM...  2.52 us
  transfers between devices with their start and end apart: 14, of which 6 were waited for; matrix products, arithmetic and copies ran while one was open for 0% of the time, Pallas kernels for 5%

profile of v5, /device:TPU:1, one launch (start us, length us, event | category | flops | bytes accessed | tf_op | source)
XLA Modules:
  0.0 111.5 jit_solution(2767575225642350817)
XLA Ops:
  0.0 0.0 copy-start.5
  0.0 0.0 copy-start.6
  0.0 0.0 copy-start.4
  0.0 0.0 copy-start.1
  0.0 3.5 %forward_yz.1 = (f32[8,64,128]{2,1,0:T(8,128)S(1)}, f32[8,64,128]{2,1,0:T(8,128)S(1)}, f32[8,64,128]{2,1,0:T(8,128)S(1)}, f32[8,64,128]{2,1,0:T(8,128)S(1)}, f32...) custom-call(f32[8,8,64,128]{3,2,1,0:T(8,128)} %x_any.1, ...), custom_call_target="tpu_custom_call" | custom-call | flops 603979776 | bytes 4194304 | tf_op jit(solution)/shard_map/forward_yz/pallas_call | solution.py:110
  3.6 3.7 %collective-permute-start = (f32[8,64,128]{2,1,0:T(8,128)S(1)}, f32[8,64,128]{2,1,0:T(8,128)S(1)}, u32[]{:S(2)}, u32[]{:S(2)}) collective-permute-start(f32[8,64,128]{2,1,0:T(8,128)S(1)} %get-tuple-element.54), channel_id=1, source_target_pairs={{0,4},{1,5},{2,6},{3,7},{4,0},{5,1},{6,2},{7,3},{8,12},{9,13},{10,... | collective-permute-start | bytes 786440 | tf_op jit(solution)/shard_map/ppermute | solution.py:33
  7.2 2.8 %collective-permute-start.1 = (f32[8,64,128]{2,1,0:T(8,128)S(1)}, f32[8,64,128]{2,1,0:T(8,128)S(1)}, u32[]{:S(2)}, u32[]{:S(2)}) collective-permute-start(f32[8,64,128]{2,1,0:T(8,128)S(1)} %get-tuple-element.55), channel_id=1, source_target_pairs={{0,5},{1,4},{2,7},{3,6},{4,1},{5,0},{6,3},{7,2},{8,13},{9,12},{10,... | collective-permute-start | bytes 786440 | tf_op jit(solution)/shard_map/ppermute | solution.py:33
  10.0 0.0 collective-permute-start.2
  10.0 2.7 %collective-permute-start.3 = (f32[8,64,128]{2,1,0:T(8,128)S(1)}, f32[8,64,128]{2,1,0:T(8,128)S(1)}, u32[]{:S(2)}, u32[]{:S(2)}) collective-permute-start(f32[8,64,128]{2,1,0:T(8,128)S(1)} %get-tuple-element.57), channel_id=1, source_target_pairs={{0,6},{1,7},{2,0},{3,1},{4,2},{5,3},{6,4},{7,5},{8,14},{9,15},{10,... | collective-permute-start | bytes 786440 | tf_op jit(solution)/shard_map/ppermute | solution.py:33
  12.7 0.0 collective-permute-start.4
  12.7 0.0 collective-permute-done.refs_1_
  12.7 5.6 %collective-permute-start.5 = (f32[8,64,128]{2,1,0:T(8,128)S(1)}, f32[8,64,128]{2,1,0:T(8,128)S(1)}, u32[]{:S(2)}, u32[]{:S(2)}) collective-permute-start(f32[8,64,128]{2,1,0:T(8,128)S(1)} %get-tuple-element.59), channel_id=1, source_target_pairs={{0,7},{1,6},{2,1},{3,0},{4,3},{5,2},{6,5},{7,4},{8,15},{9,14},{10,... | collective-permute-start | bytes 786440 | tf_op jit(solution)/shard_map/ppermute | solution.py:33
  18.3 3.5 %collective-permute-done.1.refs_2_ = f32[8,64,128]{2,1,0:T(8,128)S(1)} collective-permute-done((f32[8,64,128]{2,1,0:T(8,128)S(1)}, f32[8,64,128]{2,1,0:T(8,128)S(1)}, u32[]{:S(2)}, u32[]{:S(2)}) %collective-permute-start.1) | collective-permute-done | bytes 262176 | tf_op jit(solution)/shard_map/ppermute | solution.py:33
  21.8 0.0 collective-permute-start.6
  21.8 0.0 copy-done
  21.8 0.0 copy-done.2
  21.8 0.0 copy-done.3
  21.9 0.0 copy-done.5
  21.9 0.0 copy-done.6
  21.9 0.0 copy-done.4
  21.9 0.0 copy-done.1
  21.9 2.5 %prepare.1 = (f32[8,512,128]{2,1,0:T(8,128)S(1)}, f32[8,512,128]{2,1,0:T(8,128)S(1)}, f32[8,512,128]{2,1,0:T(8,128)S(1)}, f32[8,512,128]{2,1,0:T(8,128)S(1)}, f3...) custom-call(f32[256]{0:T(256)S(1)} %copy-done.3, ...), custom_call_target="tpu_custom_call" | custom-call | flops 15728640 | bytes 10485760 | tf_op jit(solution)/shard_map/prepare/pallas_call | solution.py:250
  24.4 2.7 %reduced_terms.1 = (f32[32,16,128]{2,1,0:T(8,128)S(1)}, f32[32,16,128]{2,1,0:T(8,128)S(1)}, f32[32,16,128]{2,1,0:T(8,128)S(1)}, f32[32,16,128]{2,1,0:T(8,128)S(1...) custom-call(f32[256]{0:T(256)S(1)} %copy-done.3, f32[1,64]{1,0:T(1,128)S(1)} %bitcast.3, f32[64]{0:T(128)S(1)} %copy-done.5, ...), custom_call_target="tpu_custom_call" | custom-call | flops 20971520 | bytes 1572864 | tf_op jit(solution)/shard_map/reduced_terms/pallas_call | solution.py:319
  27.2 0.0 collective-permute-done.2.refs_3_
  27.2 0.0 collective-permute-done.3.refs_4_
  27.2 3.9 %collective-permute-done.4.refs_5_ = f32[8,64,128]{2,1,0:T(8,128)S(1)} collective-permute-done((f32[8,64,128]{2,1,0:T(8,128)S(1)}, f32[8,64,128]{2,1,0:T(8,128)S(1)}, u32[]{:S(2)}, u32[]{:S(2)}) %collective-permute-start.4) | collective-permute-done | bytes 262176 | tf_op jit(solution)/shard_map/ppermute | solution.py:33
  31.1 0.1 collective-permute-done.5.refs_6_
  31.2 0.0 collective-permute-done.6.refs_7_
  31.2 0.9 eliminate.1
  32.1 25.1 %all_to_all.10.g_ref = f32[32,2,16,128]{3,2,1,0:T(8,128)S(1)} all-to-all(f32[32,2,16,128]{3,2,1,0:T(8,128)S(1)} %get-tuple-element.62), channel_id=1, replica_groups=mesh['ta'=32,'gx'=8] {'ta'}, dimensions={0} | all-to-all | bytes 1048576 | tf_op jit(solution)/shard_map/all_to_all | solution.py:468
  57.2 0.3 interface_solve.1
  57.6 22.0 %all_to_all.11.ends_ref = f32[32,2,16,128]{3,2,1,0:T(8,128)S(1)} all-to-all(f32[32,2,16,128]{3,2,1,0:T(8,128)S(1)} %interface_solve.1), channel_id=1, replica_groups=mesh['ta'=32,'gx'=8] {'ta'}, dimensions={0} | all-to-all | bytes 1048576 | tf_op jit(solution)/shard_map/all_to_all | solution.py:470
  79.5 0.8 return_x.1
  80.3 2.9 %collective-permute-start.7 = (f32[8,64,128]{2,1,0:T(8,128)S(1)}, f32[8,64,128]{2,1,0:T(8,128)S(1)}, u32[]{:S(2)}, u32[]{:S(2)}) collective-permute-start(f32[8,64,128]{2,1,0:T(8,128)S(1)} %get-tuple-element.70), channel_id=1, source_target_pairs={{0,4},{1,5},{2,6},{3,7},{4,0},{5,1},{6,2},{7,3},{8,12},{9,13},{10,... | collective-permute-start | bytes 786440 | tf_op jit(solution)/shard_map/ppermute | solution.py:33
  83.2 4.4 %collective-permute-start.8 = (f32[8,64,128]{2,1,0:T(8,128)S(1)}, f32[8,64,128]{2,1,0:T(8,128)S(1)}, u32[]{:S(2)}, u32[]{:S(2)}) collective-permute-start(f32[8,64,128]{2,1,0:T(8,128)S(1)} %get-tuple-element.71), channel_id=1, source_target_pairs={{0,5},{1,4},{2,7},{3,6},{4,1},{5,0},{6,3},{7,2},{8,13},{9,12},{10,... | collective-permute-start | bytes 786440 | tf_op jit(solution)/shard_map/ppermute | solution.py:33
  87.6 1.2 %collective-permute-start.9 = (f32[8,64,128]{2,1,0:T(8,128)S(1)}, f32[8,64,128]{2,1,0:T(8,128)S(1)}, u32[]{:S(2)}, u32[]{:S(2)}) collective-permute-start(f32[8,64,128]{2,1,0:T(8,128)S(1)} %get-tuple-element.72), channel_id=1, source_target_pairs={{0,2},{1,3},{2,4},{3,5},{4,6},{5,7},{6,0},{7,1},{8,10},{9,11},{10,... | collective-permute-start | bytes 786440 | tf_op jit(solution)/shard_map/ppermute | solution.py:33
  88.8 1.5 %collective-permute-start.10 = (f32[8,64,128]{2,1,0:T(8,128)S(1)}, f32[8,64,128]{2,1,0:T(8,128)S(1)}, u32[]{:S(2)}, u32[]{:S(2)}) collective-permute-start(f32[8,64,128]{2,1,0:T(8,128)S(1)} %get-tuple-element.73), channel_id=1, source_target_pairs={{0,6},{1,7},{2,0},{3,1},{4,2},{5,3},{6,4},{7,5},{8,14},{9,15},{10,... | collective-permute-start | bytes 786440 | tf_op jit(solution)/shard_map/ppermute | solution.py:33
  90.3 0.0 collective-permute-start.11
  90.3 0.0 collective-permute-done.7.refs_1_
  90.3 6.5 %collective-permute-start.12 = (f32[8,64,128]{2,1,0:T(8,128)S(1)}, f32[8,64,128]{2,1,0:T(8,128)S(1)}, u32[]{:S(2)}, u32[]{:S(2)}) collective-permute-start(f32[8,64,128]{2,1,0:T(8,128)S(1)} %get-tuple-element.75), channel_id=1, source_target_pairs={{0,7},{1,6},{2,1},{3,0},{4,3},{5,2},{6,5},{7,4},{8,15},{9,14},{10,... | collective-permute-start | bytes 786440 | tf_op jit(solution)/shard_map/ppermute | solution.py:33
  96.7 0.8 collective-permute-done.8.refs_2_
  97.6 2.3 %collective-permute-start.13 = (f32[8,64,128]{2,1,0:T(8,128)S(1)}, f32[8,64,128]{2,1,0:T(8,128)S(1)}, u32[]{:S(2)}, u32[]{:S(2)}) collective-permute-start(f32[8,64,128]{2,1,0:T(8,128)S(1)} %get-tuple-element.76), channel_id=1, source_target_pairs={{0,1},{1,0},{2,3},{3,2},{4,5},{5,4},{6,7},{7,6},{8,9},{9,8},{10,11... | collective-permute-start | bytes 786440 | tf_op jit(solution)/shard_map/ppermute | solution.py:33
  99.9 3.3 %collective-permute-done.9.refs_3_ = f32[8,64,128]{2,1,0:T(8,128)S(1)} collective-permute-done((f32[8,64,128]{2,1,0:T(8,128)S(1)}, f32[8,64,128]{2,1,0:T(8,128)S(1)}, u32[]{:S(2)}, u32[]{:S(2)}) %collective-permute-start.9) | collective-permute-done | bytes 262176 | tf_op jit(solution)/shard_map/ppermute | solution.py:33
  103.1 0.0 collective-permute-done.10.refs_4_
  103.1 5.6 %collective-permute-done.11.refs_5_ = f32[8,64,128]{2,1,0:T(8,128)S(1)} collective-permute-done((f32[8,64,128]{2,1,0:T(8,128)S(1)}, f32[8,64,128]{2,1,0:T(8,128)S(1)}, u32[]{:S(2)}, u32[]{:S(2)}) %collective-permute-start.11) | collective-permute-done | bytes 262176 | tf_op jit(solution)/shard_map/ppermute | solution.py:33
  108.8 0.0 collective-permute-done.12.refs_6_
  108.8 0.0 collective-permute-done.13.refs_7_
  108.8 2.5 %backward_yz.1 = f32[8,8,64,128]{3,2,1,0:T(8,128)} custom-call(bf16[64,192]{1,0:T(8,128)(2,1)S(1)} %get-tuple-element.41.by3_ref, bf16[384,128]{1,0:T(8,128)(2,1)S(1)} %get-tuple-element.42.bz3_ref, f32[8,64,128]{2,1,0:T(8,128)S(1)} %get-tuple-element.69.refs_0_, f32[8,64,128]{2,1,0:T(8,128)S(1)} %collective-permute-done.7.refs_1_, ...), custom_call_target="tpu_custom_call" | custom-call | flops 603979776 | bytes 4194304 | tf_op jit(solution)/shard_map/backward_yz/pallas_call | solution.py:166
  (3 shorter events, 0.0 us)
Async XLA Ops:
  0.0 21.8 %copy-start = (f32[128,128]{1,0:T(8,128)S(1)}, f32[128,128]{1,0:T(8,128)}, u32[]{:S(2)}) copy-start(f32[128,128]{1,0:T(8,128)} %bz_any.1) | copy-start | bytes 196612
  0.0 21.8 %copy-start.2 = (f32[64,64]{1,0:T(8,128)S(1)}, f32[64,64]{1,0:T(8,128)}, u32[]{:S(2)}) copy-start(f32[64,64]{1,0:T(8,128)} %by_any.1) | copy-start | bytes 49156
  0.0 21.8 %copy-start.3 = (f32[256]{0:T(256)S(1)}, f32[256]{0:T(256)}, u32[]{:S(2)}) copy-start(f32[256]{0:T(256)} %steps_ref.3) | copy-start | bytes 3076
  0.0 21.8 %copy-start.5 = (f32[64]{0:T(128)S(1)}, f32[64]{0:T(128)}, u32[]{:S(2)}) copy-start(f32[64]{0:T(128)} %ey_ref.3) | copy-start | bytes 772
  0.0 21.8 %copy-start.6 = (f32[128]{0:T(128)S(1)}, f32[128]{0:T(128)}, u32[]{:S(2)}) copy-start(f32[128]{0:T(128)} %param.14) | copy-start | bytes 1540
  0.0 21.8 %copy-start.4 = (f32[64]{0:T(128)S(1)}, f32[64]{0:T(128)}, u32[]{:S(2)}) copy-start(f32[64]{0:T(128)} %param.12) | copy-start | bytes 772
  0.0 21.8 %copy-start.1 = (f32[64,64]{1,0:T(8,128)S(1)}, f32[64,64]{1,0:T(8,128)}, u32[]{:S(2)}) copy-start(f32[64,64]{1,0:T(8,128)} %bx_ref.1) | copy-start | bytes 49156
  3.6 9.1 %collective-permute-start = (f32[8,64,128]{2,1,0:T(8,128)S(1)}, f32[8,64,128]{2,1,0:T(8,128)S(1)}, u32[]{:S(2)}, u32[]{:S(2)}) collective-permute-start(f32[8,64,128]{2,1,0:T(8,128)S(1)} %get-tuple-element.54), channel_id=1, source_target_pairs={{0,4},{1,5},{2,6},{3,7},{4,0},{5,1},{6,2},{7,3},{8,12},{9,13},{10,... | collective-permute-start | bytes 786440 | tf_op jit(solution)/shard_map/ppermute | solution.py:33
  7.2 14.6 %collective-permute-start.1 = (f32[8,64,128]{2,1,0:T(8,128)S(1)}, f32[8,64,128]{2,1,0:T(8,128)S(1)}, u32[]{:S(2)}, u32[]{:S(2)}) collective-permute-start(f32[8,64,128]{2,1,0:T(8,128)S(1)} %get-tuple-element.55), channel_id=1, source_target_pairs={{0,5},{1,4},{2,7},{3,6},{4,1},{5,0},{6,3},{7,2},{8,13},{9,12},{10,... | collective-permute-start | bytes 786440 | tf_op jit(solution)/shard_map/ppermute | solution.py:33
  10.0 17.2 %collective-permute-start.2 = (f32[8,64,128]{2,1,0:T(8,128)S(1)}, f32[8,64,128]{2,1,0:T(8,128)S(1)}, u32[]{:S(2)}, u32[]{:S(2)}) collective-permute-start(f32[8,64,128]{2,1,0:T(8,128)S(1)} %get-tuple-element.56), channel_id=1, source_target_pairs={{0,2},{1,3},{2,4},{3,5},{4,6},{5,7},{6,0},{7,1},{8,10},{9,11},{10,... | collective-permute-start | bytes 786440 | tf_op jit(solution)/shard_map/ppermute | solution.py:33
  10.0 17.2 %collective-permute-start.3 = (f32[8,64,128]{2,1,0:T(8,128)S(1)}, f32[8,64,128]{2,1,0:T(8,128)S(1)}, u32[]{:S(2)}, u32[]{:S(2)}) collective-permute-start(f32[8,64,128]{2,1,0:T(8,128)S(1)} %get-tuple-element.57), channel_id=1, source_target_pairs={{0,6},{1,7},{2,0},{3,1},{4,2},{5,3},{6,4},{7,5},{8,14},{9,15},{10,... | collective-permute-start | bytes 786440 | tf_op jit(solution)/shard_map/ppermute | solution.py:33
  12.7 18.4 %collective-permute-start.4 = (f32[8,64,128]{2,1,0:T(8,128)S(1)}, f32[8,64,128]{2,1,0:T(8,128)S(1)}, u32[]{:S(2)}, u32[]{:S(2)}) collective-permute-start(f32[8,64,128]{2,1,0:T(8,128)S(1)} %get-tuple-element.58), channel_id=1, source_target_pairs={{0,3},{1,2},{2,5},{3,4},{4,7},{5,6},{6,1},{7,0},{8,11},{9,10},{10,... | collective-permute-start | bytes 786440 | tf_op jit(solution)/shard_map/ppermute | solution.py:33
  12.7 18.5 %collective-permute-start.5 = (f32[8,64,128]{2,1,0:T(8,128)S(1)}, f32[8,64,128]{2,1,0:T(8,128)S(1)}, u32[]{:S(2)}, u32[]{:S(2)}) collective-permute-start(f32[8,64,128]{2,1,0:T(8,128)S(1)} %get-tuple-element.59), channel_id=1, source_target_pairs={{0,7},{1,6},{2,1},{3,0},{4,3},{5,2},{6,5},{7,4},{8,15},{9,14},{10,... | collective-permute-start | bytes 786440 | tf_op jit(solution)/shard_map/ppermute | solution.py:33
  21.8 9.4 %collective-permute-start.6 = (f32[8,64,128]{2,1,0:T(8,128)S(1)}, f32[8,64,128]{2,1,0:T(8,128)S(1)}, u32[]{:S(2)}, u32[]{:S(2)}) collective-permute-start(f32[8,64,128]{2,1,0:T(8,128)S(1)} %get-tuple-element.60), channel_id=1, source_target_pairs={{0,1},{1,0},{2,3},{3,2},{4,5},{5,4},{6,7},{7,6},{8,9},{9,8},{10,11... | collective-permute-start | bytes 786440 | tf_op jit(solution)/shard_map/ppermute | solution.py:33
  80.3 9.9 %collective-permute-start.7 = (f32[8,64,128]{2,1,0:T(8,128)S(1)}, f32[8,64,128]{2,1,0:T(8,128)S(1)}, u32[]{:S(2)}, u32[]{:S(2)}) collective-permute-start(f32[8,64,128]{2,1,0:T(8,128)S(1)} %get-tuple-element.70), channel_id=1, source_target_pairs={{0,4},{1,5},{2,6},{3,7},{4,0},{5,1},{6,2},{7,3},{8,12},{9,13},{10,... | collective-permute-start | bytes 786440 | tf_op jit(solution)/shard_map/ppermute | solution.py:33
  83.2 14.4 %collective-permute-start.8 = (f32[8,64,128]{2,1,0:T(8,128)S(1)}, f32[8,64,128]{2,1,0:T(8,128)S(1)}, u32[]{:S(2)}, u32[]{:S(2)}) collective-permute-start(f32[8,64,128]{2,1,0:T(8,128)S(1)} %get-tuple-element.71), channel_id=1, source_target_pairs={{0,5},{1,4},{2,7},{3,6},{4,1},{5,0},{6,3},{7,2},{8,13},{9,12},{10,... | collective-permute-start | bytes 786440 | tf_op jit(solution)/shard_map/ppermute | solution.py:33
  87.6 15.5 %collective-permute-start.9 = (f32[8,64,128]{2,1,0:T(8,128)S(1)}, f32[8,64,128]{2,1,0:T(8,128)S(1)}, u32[]{:S(2)}, u32[]{:S(2)}) collective-permute-start(f32[8,64,128]{2,1,0:T(8,128)S(1)} %get-tuple-element.72), channel_id=1, source_target_pairs={{0,2},{1,3},{2,4},{3,5},{4,6},{5,7},{6,0},{7,1},{8,10},{9,11},{10,... | collective-permute-start | bytes 786440 | tf_op jit(solution)/shard_map/ppermute | solution.py:33
  88.8 14.3 %collective-permute-start.10 = (f32[8,64,128]{2,1,0:T(8,128)S(1)}, f32[8,64,128]{2,1,0:T(8,128)S(1)}, u32[]{:S(2)}, u32[]{:S(2)}) collective-permute-start(f32[8,64,128]{2,1,0:T(8,128)S(1)} %get-tuple-element.73), channel_id=1, source_target_pairs={{0,6},{1,7},{2,0},{3,1},{4,2},{5,3},{6,4},{7,5},{8,14},{9,15},{10,... | collective-permute-start | bytes 786440 | tf_op jit(solution)/shard_map/ppermute | solution.py:33
  90.3 18.5 %collective-permute-start.11 = (f32[8,64,128]{2,1,0:T(8,128)S(1)}, f32[8,64,128]{2,1,0:T(8,128)S(1)}, u32[]{:S(2)}, u32[]{:S(2)}) collective-permute-start(f32[8,64,128]{2,1,0:T(8,128)S(1)} %get-tuple-element.74), channel_id=1, source_target_pairs={{0,3},{1,2},{2,5},{3,4},{4,7},{5,6},{6,1},{7,0},{8,11},{9,10},{10,... | collective-permute-start | bytes 786440 | tf_op jit(solution)/shard_map/ppermute | solution.py:33
  90.3 18.5 %collective-permute-start.12 = (f32[8,64,128]{2,1,0:T(8,128)S(1)}, f32[8,64,128]{2,1,0:T(8,128)S(1)}, u32[]{:S(2)}, u32[]{:S(2)}) collective-permute-start(f32[8,64,128]{2,1,0:T(8,128)S(1)} %get-tuple-element.75), channel_id=1, source_target_pairs={{0,7},{1,6},{2,1},{3,0},{4,3},{5,2},{6,5},{7,4},{8,15},{9,14},{10,... | collective-permute-start | bytes 786440 | tf_op jit(solution)/shard_map/ppermute | solution.py:33
  97.6 11.2 %collective-permute-start.13 = (f32[8,64,128]{2,1,0:T(8,128)S(1)}, f32[8,64,128]{2,1,0:T(8,128)S(1)}, u32[]{:S(2)}, u32[]{:S(2)}) collective-permute-start(f32[8,64,128]{2,1,0:T(8,128)S(1)} %get-tuple-element.76), channel_id=1, source_target_pairs={{0,1},{1,0},{2,3},{3,2},{4,5},{5,4},{6,7},{7,6},{8,9},{9,8},{10,11... | collective-permute-start | bytes 786440 | tf_op jit(solution)/shard_map/ppermute | solution.py:33

commit v6 on v5

--- a/solution.py
+++ b/solution.py
@@ -24,14 +24,15 @@
     return far * 2 + (1 - own if core else own)
 
 
-def exchange(pieces, peers):
-    members = len(pieces)
-    moved = [pieces[0]]
-    for k in range(1, members):
-        chips, core = peers[k]
-        pairs = [(i, ((i // 2 + chips) * 2 + (i % 2 + core) % 2) % members) for i in range(members)]
-        moved.append(lax.ppermute(pieces[k], "gx", pairs))
-    return moved
+def send(piece, place, members):
+    chips, core = place
+    pairs = [(i, ((i // 2 + chips) * 2 + (i % 2 + core) % 2) % members) for i in range(members)]
+    return lax.ppermute(piece, "gx", pairs)
+
+
+def exchange(pieces):
+    moved = [send(piece, place, len(PEERS)) for piece, place in zip(pieces[1:], PEERS[1:])]
+    return [pieces[0]] + moved
 
 
 def split(x):
@@ -61,40 +62,38 @@
 
 
 def gather_rows(source_ref, target_ref, peers, sign):
-    members = len(peers)
-    span = target_ref.shape[0] // members
+    span = target_ref.shape[0] // len(peers)
     member = lax.axis_index("gx")
     for k, place in enumerate(peers):
-        start = pl.multiple_of(peer(member, members, place, sign) * span, span)
+        start = pl.multiple_of(peer(member, len(PEERS), place, sign) * span, span)
         target_ref[k * span : (k + 1) * span] = source_ref[pl.ds(start, span), :]
 
 
-def forward_body(x_any, by_any, bz_any, *refs):
-    outs, refs = refs[: len(PEERS)], refs[len(PEERS) :]
+def forward_body(peers, x_any, by_any, bz_any, *refs):
+    outs, refs = refs[: len(peers)], refs[len(peers) :]
     x_ref, by_ref, bz_ref, turn_ref, rows_ref, by3_ref, bz3_ref, x_sem, b_sem = refs
     total, rows, y, z = x_ref.shape
-    span = y // len(outs)
+    size = outs[0].shape[1]
+    span = size // rows
     tables = [
         pltpu.make_async_copy(source, target, b_sem.at[k])
         for k, (source, target) in enumerate(((by_any, by_ref), (bz_any, bz_ref)))
     ]
     planes = [pltpu.make_async_copy(x_any.at[t], x_ref.at[t], x_sem.at[t]) for t in range(total)]
-    for copy in tables + planes:
+    for copy in planes + tables:
         copy.start()
-    for copy in tables:
+    for copy in planes + tables:
         copy.wait()
     turn_ref[...] = by_ref[...].T
-    gather_rows(turn_ref, rows_ref, PEERS, 1)
+    gather_rows(turn_ref, rows_ref, peers, 1)
     by3_ref[...] = left3(rows_ref[...])
     bz3_ref[...] = right3(bz_ref[...])
 
+    vol = [mm(left3(x_ref[t].reshape(rows * y, z)), bz3_ref[...]) for t in range(total)]
     for first in range(0, total, 4):
         times = range(first, first + 4)
-        for t in times:
-            planes[t].wait()
-        vol = [mm(left3(x_ref[t].reshape(rows * y, z)), bz3_ref[...]) for t in times]
         for a in range(rows):
-            plane = jnp.concatenate([v[a * y : (a + 1) * y] for v in vol], axis=1)
+            plane = jnp.concatenate([vol[t][a * y : (a + 1) * y] for t in times], axis=1)
             plane = mm(by3_ref[...], right3(plane))
             for k, out in enumerate(outs):
                 for i, t in enumerate(times):
@@ -103,54 +102,67 @@
                     ]
 
 
-def forward_yz(x, by, bz):
+def forward_yz(x, by, bz, peers):
     t, a, y, z = x.shape
-    members = len(PEERS)
-    rows = a * y // members
-    return pl.pallas_call(
-        forward_body,
+    span = y // len(PEERS)
+    return pl.pallas_call(
+        partial(forward_body, peers),
         in_specs=[ANY] * 3,
-        out_specs=[VMEM] * members,
-        out_shape=[array(t, rows, z)] * members,
+        out_specs=[VMEM] * len(peers),
+        out_shape=[array(t, a * span, z)] * len(peers),
         scratch_shapes=[
             pltpu.VMEM(x.shape, f32),
             pltpu.VMEM((y, y), f32),
             pltpu.VMEM((z, z), f32),
             pltpu.VMEM((y, y), f32),
-            pltpu.VMEM((y, y), f32),
-            pltpu.VMEM((y, 3 * y), bf16),
+            pltpu.VMEM((len(peers) * span, y), f32),
+            pltpu.VMEM((len(peers) * span, 3 * y), bf16),
             pltpu.VMEM((3 * z, z), bf16),
             pltpu.SemaphoreType.DMA((t,)),
             pltpu.SemaphoreType.DMA((2,)),
         ],
         compiler_params=params(),
-        cost_estimate=cost(6 * t * a * y * z * (y + z), 8 * t * a * y * z),
+        cost_estimate=cost(6 * t * a * len(peers) * span * z * (y + z), 8 * t * a * y * z),
         name="forward_yz",
     )(x, by, bz)
 
 
-def backward_body(by3_ref, bz3_ref, *refs):
-    pieces, (out_any, out_ref, sem) = refs[: len(PEERS)], refs[len(PEERS) :]
-    total, rows, y, z = out_ref.shape
-    span = y // len(pieces)
+def backward_planes(times, rows, by3_ref, bz3_ref, pieces, mid_ref):
+    size, z = pieces[0].shape[1:]
+    span = size // rows
+    for t in times:
+        flat = jnp.concatenate([piece[t] for piece in pieces], axis=0)
+        mid_ref[t] = mm(left3(flat), bz3_ref[...])
+    for a in range(rows):
+        plane = [
+            jnp.concatenate(
+                [mid_ref[t, pl.ds(k * size + a, span, stride=rows), :] for k in range(len(pieces))],
+                axis=0,
+            )
+            for t in times
+        ]
+        plane = mm(by3_ref[...], right3(jnp.concatenate(plane, axis=1)))
+        for i, t in enumerate(times):
+            yield t, a, plane[:, i * z : (i + 1) * z]
+
+
+def backward_early_body(by3_ref, bz3_ref, *refs):
+    pieces, (out_ref, mid_ref) = refs[:-2], refs[-2:]
+    total, rows = out_ref.shape[:2]
+    for first in range(0, total, 2):
+        times = (first, first + 1)
+        for t, a, plane in backward_planes(times, rows, by3_ref, bz3_ref, pieces, mid_ref):
+            out_ref[t, a] = plane
+
+
+def backward_late_body(by3_ref, bz3_ref, early_ref, *refs):
+    pieces, (out_any, out_ref, mid_ref, sem) = refs[:-4], refs[-4:]
+    total, rows = out_ref.shape[:2]
     copies = []
     for first in range(0, total, 2):
         times = (first, first + 1)
-        vol = []
-        for a in range(rows):
-            plane = jnp.concatenate(
-                [
-                    jnp.concatenate(
-                        [piece[t, pl.ds(a, span, stride=rows), :] for piece in pieces], axis=0
-                    )
-                    for t in times
-                ],
-                axis=1,
-            )
-            vol.append(mm(by3_ref[...], right3(plane)))
-        for i, t in enumerate(times):
-            flat = jnp.concatenate([v[:, i * z : (i + 1) * z] for v in vol], axis=0)
-            out_ref[t] = mm(left3(flat), bz3_ref[...]).reshape(rows, y, z)
+        for t, a, plane in backward_planes(times, rows, by3_ref, bz3_ref, pieces, mid_ref):
+            out_ref[t, a] = early_ref[t, a] + plane
         for t in times:
             copies.append(pltpu.make_async_copy(out_ref.at[t], out_any.at[t], sem.at[t]))
             copies[-1].start()
@@ -158,21 +170,22 @@
         copy.wait()
 
 
-def backward_yz(pieces, by3, bz3):
-    members = len(pieces)
+def backward_yz(pieces, by3, bz3, early=()):
     y, z = by3.shape[0], bz3.shape[1]
-    t, rows = pieces[0].shape[:2]
-    a = rows * members // y
-    return pl.pallas_call(
-        backward_body,
-        in_specs=[VMEM] * (2 + members),
-        out_specs=ANY,
+    t, size = pieces[0].shape[:2]
+    a = size * len(PEERS) // y
+    mid = pltpu.VMEM((t, len(pieces) * size, z), f32)
+    scratch = [pltpu.VMEM((t, a, y, z), f32), mid, pltpu.SemaphoreType.DMA((t,))]
+    return pl.pallas_call(
+        backward_late_body if early else backward_early_body,
+        in_specs=[VMEM] * (2 + len(early) + len(pieces)),
+        out_specs=ANY if early else VMEM,
         out_shape=array(t, a, y, z),
-        scratch_shapes=[pltpu.VMEM((t, a, y, z), f32), pltpu.SemaphoreType.DMA((t,))],
-        compiler_params=params(),
-        cost_estimate=cost(6 * t * a * y * z * (y + z), 8 * t * a * y * z),
+        scratch_shapes=scratch if early else [mid],
+        compiler_params=params(),
+        cost_estimate=cost(6 * t * size * len(pieces) * z * (y + z), 8 * t * a * y * z),
         name="backward_yz",
-    )(by3, bz3, *pieces)
+    )(by3, bz3, *early, *pieces)
 
 
 def length(steps_ref, at):
@@ -197,8 +210,8 @@
 
 
 def prepare_body(steps_ref, ex_ref, ey_ref, ez_ref, bx_ref, by_ref, bz_ref, *refs):
-    inv_ref, mul_ref, ratio_ref, v_ref, w_ref, bx3_ref, bx3_back_ref, by3_ref, bz3_ref = refs[:9]
-    sums_ref, turn_ref, rows_ref = refs[9:]
+    inv_ref, mul_ref, ratio_ref, v_ref, w_ref, bx3_ref, bx3_back_ref, *by3_refs, bz3_ref = refs[:10]
+    sums_ref, turn_ref, rows_ref = refs[10:]
     total, modes, lanes = inv_ref.shape
     x, members = ex_ref.shape[1], len(PEERS)
     gather_rows(bx_ref, rows_ref, PEERS, -1)
@@ -207,7 +220,9 @@
     bx3_back_ref[...] = left3(rows_ref[...])
     turn_ref[...] = by_ref[...].T
     gather_rows(turn_ref, rows_ref, PEERS, -1)
-    by3_ref[...] = left3(rows_ref[...].T)
+    half = rows_ref.shape[0] // 2
+    for k, ref in enumerate(by3_refs):
+        ref[...] = left3(rows_ref[k * half : (k + 1) * half].T)
     bz3_ref[...] = right3(bz_ref[...].T)
 
     span = ey_ref.shape[0] // members
@@ -250,9 +265,11 @@
     return pl.pallas_call(
         prepare_body,
         in_specs=[SMEM, VMEM, SMEM, VMEM, VMEM, VMEM, VMEM],
-        out_specs=[VMEM] * 9,
+        out_specs=[VMEM] * 10,
         out_shape=[array(rows, modes, z)] * 5
-        + [table(x, 3 * x), table(x, 3 * x), table(y, 3 * y), table(3 * z, z)],
+        + [table(x, 3 * x)] * 2
+        + [table(y, 3 * y // 2)] * 2
+        + [table(3 * z, z)],
         scratch_shapes=[
             pltpu.VMEM((modes, z), f32),
             pltpu.VMEM((y, y), f32),
@@ -459,17 +476,21 @@
     share = basis_x.shape[0] * basis_y.shape[0] // (lax.axis_size("gx") * count)
     hbm = lambda value: pltpu.with_memory_space_constraint(value, pltpu.HBM)
 
-    sent = forward_yz(hbm(right_side), hbm(basis_y), hbm(basis_z))
-    moved = exchange(sent, PEERS)
+    given = (hbm(right_side), hbm(basis_y), hbm(basis_z))
+    far, near = PEERS[1:5], PEERS[:1] + PEERS[5:]
+    sent = forward_yz(*given, far)
+    rest = forward_yz(*given, near)
+    moved = exchange([rest[0], *sent, *rest[1:]])
     terms = list(reduced_terms(steps, sums, count, rows, share))
-    *factors, v, w, bx3, bx3_back, by3, bz3 = prepare(steps, sums, basis_x, basis_y, basis_z, rows)
+    *factors, v, w, bx3, bx3_back, by3_early, by3_late, bz3 = prepare(steps, sums, basis_x, basis_y, basis_z, rows)
     moved[0], terms[0], bx3 = lax.optimization_barrier((moved[0], terms[0], bx3))
     g, ends = eliminate(moved, bx3, factors, count)
     ends = lax.all_to_all(ends, "ta", 0, 0, tiled=True)
     ends = interface_solve(ends, terms)
     ends = lax.all_to_all(ends, "ta", 0, 0, tiled=True)
-    moved = exchange(return_x(g, ends, bx3_back, v, w), PEERS)
-    return backward_yz(moved, by3, bz3)
+    moved = exchange(return_x(g, ends, bx3_back, v, w))
+    early = backward_yz(moved[:4], by3_early, bz3)
+    return backward_yz(moved[4:], by3_late, bz3, (early,))
 
 
 def solution(mesh):

time: 112 us -> 111 us (level)
  Pallas kernels: 13.4 us -> 17.3 us
  starting transfers between devices: 33.4 us -> 30.9 us
  waiting for transfers between devices: 17.3 us -> 15.3 us
    pallas_call x2 -> x4, Pallas kernels: 6.03 us -> 9.94 us  [the longest x2 6.06 us: forward_yz(): pl.pallas_call(partial(forward_body, peers), in_specs=[ANY] * 3, out_spec...]
    ppermute x14, starting transfers between devices: 33.4 us -> 30.9 us  [send(): return lax.ppermute(piece, 'gx', pairs)]
    ppermute x14, waiting for transfers between devices: 17.3 us -> 15.3 us  [send(): return lax.ppermute(piece, 'gx', pairs)]
  transfers between devices with their start and end apart: 14 -> 14, of which waited for: 6 -> 6; matrix products, arithmetic and copies ran while one was open for 0% -> 0% of each run, Pallas kernels for 5% -> 9%
where the time goes in v6:
time: 111 us
  blocking collectives  47 us (42%)
  starting transfers between devices  30.9 us (28%)
  Pallas kernels  17.3 us (16%)
  waiting for transfers between devices  15.3 us (14%)
    all_to_all x2, blocking collectives, local(): ends = lax.all_to_all(ends, 'ta', 0, 0, tiled=True)  47 us
    ppermute x14, starting transfers between devices, send(): return lax.ppermute(piece, 'gx', pairs)  30.9 us
    ppermute x14, waiting for transfers between devices, send(): return lax.ppermute(piece, 'gx', pairs)  15.3 us
    pallas_call x2, Pallas kernels, forward_yz(): pl.pallas_call(partial(forward_body, peers), in_specs=[ANY] * 3, out_spec...  6.06 us
    pallas_call x2, Pallas kernels, backward_yz(): pl.pallas_call(backward_late_body if early else backward_early_body, in_s...  3.87 us
    pallas_call x1, Pallas kernels, reduced_terms(): pl.pallas_call(partial(reduced_body, rows), in_specs=[SMEM, VMEM, SMEM, V...  2.75 us
    pallas_call x1, Pallas kernels, prepare(): pl.pallas_call(prepare_body, in_specs=[SMEM, VMEM, SMEM, VMEM, VMEM, VMEM...  2.59 us
  transfers between devices with their start and end apart: 14, of which 6 were waited for; matrix products, arithmetic and copies ran while one was open for 0% of the time, Pallas kernels for 9%

profile of v6, /device:TPU:1, one launch (start us, length us, event | category | flops | bytes accessed | tf_op | source)
XLA Modules:
  0.0 110.9 jit_solution(983734066123089565)
XLA Ops:
  0.0 0.0 copy-start.5
  0.0 0.0 copy-start.6
  0.0 0.0 copy-start.4
  0.0 0.0 copy-start.2
  0.0 3.1 %forward_yz.3 = (f32[8,64,128]{2,1,0:T(8,128)S(1)}, f32[8,64,128]{2,1,0:T(8,128)S(1)}, f32[8,64,128]{2,1,0:T(8,128)S(1)}, f32[8,64,128]{2,1,0:T(8,128)S(1)}) custom-call(f32[8,8,64,128]{3,2,1,0:T(8,128)} %x_any.3, f32[64,64]{1,0:T(8,128)} %by_any.3, f32[128,128]{1,0:T(8,128)} %bz_any.3), custom_call_target="tpu_custom_call" | custom-call | flops 301989888 | bytes 4194304 | tf_op jit(solution)/shard_map/forward_yz/pallas_call | solution.py:108
  3.1 3.7 %collective-permute-start = (f32[8,64,128]{2,1,0:T(8,128)S(1)}, f32[8,64,128]{2,1,0:T(8,128)S(1)}, u32[]{:S(2)}, u32[]{:S(2)}) collective-permute-start(f32[8,64,128]{2,1,0:T(8,128)S(1)} %get-tuple-element.56), channel_id=1, source_target_pairs={{0,4},{1,5},{2,6},{3,7},{4,0},{5,1},{6,2},{7,3},{8,12},{9,13},{10,... | collective-permute-start | bytes 786440 | tf_op jit(solution)/shard_map/ppermute | solution.py:30
  6.8 2.8 %collective-permute-start.1 = (f32[8,64,128]{2,1,0:T(8,128)S(1)}, f32[8,64,128]{2,1,0:T(8,128)S(1)}, u32[]{:S(2)}, u32[]{:S(2)}) collective-permute-start(f32[8,64,128]{2,1,0:T(8,128)S(1)} %get-tuple-element.57), channel_id=1, source_target_pairs={{0,5},{1,4},{2,7},{3,6},{4,1},{5,0},{6,3},{7,2},{8,13},{9,12},{10,... | collective-permute-start | bytes 786440 | tf_op jit(solution)/shard_map/ppermute | solution.py:30
  9.6 0.0 collective-permute-start.2
  9.6 2.7 %collective-permute-start.3 = (f32[8,64,128]{2,1,0:T(8,128)S(1)}, f32[8,64,128]{2,1,0:T(8,128)S(1)}, u32[]{:S(2)}, u32[]{:S(2)}) collective-permute-start(f32[8,64,128]{2,1,0:T(8,128)S(1)} %get-tuple-element.59), channel_id=1, source_target_pairs={{0,6},{1,7},{2,0},{3,1},{4,2},{5,3},{6,4},{7,5},{8,14},{9,15},{10,... | collective-permute-start | bytes 786440 | tf_op jit(solution)/shard_map/ppermute | solution.py:30
  12.3 3.0 %forward_yz.2 = (f32[8,64,128]{2,1,0:T(8,128)S(1)}, f32[8,64,128]{2,1,0:T(8,128)S(1)}, f32[8,64,128]{2,1,0:T(8,128)S(1)}, f32[8,64,128]{2,1,0:T(8,128)S(1)}) custom-call(f32[8,8,64,128]{3,2,1,0:T(8,128)} %x_any.3, f32[64,64]{1,0:T(8,128)} %by_any.3, f32[128,128]{1,0:T(8,128)} %bz_any.3), custom_call_target="tpu_custom_call" | custom-call | flops 301989888 | bytes 4194304 | tf_op jit(solution)/shard_map/forward_yz/pallas_call | solution.py:108
  15.3 0.1 collective-permute-start.4
  15.4 0.0 collective-permute-done.refs_1_
  15.4 2.9 %collective-permute-start.5 = (f32[8,64,128]{2,1,0:T(8,128)S(1)}, f32[8,64,128]{2,1,0:T(8,128)S(1)}, u32[]{:S(2)}, u32[]{:S(2)}) collective-permute-start(f32[8,64,128]{2,1,0:T(8,128)S(1)} %get-tuple-element.61), channel_id=1, source_target_pairs={{0,7},{1,6},{2,1},{3,0},{4,3},{5,2},{6,5},{7,4},{8,15},{9,14},{10,... | collective-permute-start | bytes 786440 | tf_op jit(solution)/shard_map/ppermute | solution.py:30
  18.3 3.1 %collective-permute-done.1.refs_2_ = f32[8,64,128]{2,1,0:T(8,128)S(1)} collective-permute-done((f32[8,64,128]{2,1,0:T(8,128)S(1)}, f32[8,64,128]{2,1,0:T(8,128)S(1)}, u32[]{:S(2)}, u32[]{:S(2)}) %collective-permute-start.1) | collective-permute-done | bytes 262176 | tf_op jit(solution)/shard_map/ppermute | solution.py:30
  21.4 0.0 collective-permute-start.6
  21.4 0.0 copy-done
  21.4 0.0 copy-done.1
  21.4 0.0 copy-done.3
  21.5 0.0 copy-done.5
  21.5 0.0 copy-done.6
  21.5 2.6 %prepare.1 = (f32[8,512,128]{2,1,0:T(8,128)S(1)}, f32[8,512,128]{2,1,0:T(8,128)S(1)}, f32[8,512,128]{2,1,0:T(8,128)S(1)}, f32[8,512,128]{2,1,0:T(8,128)S(1)}, f3...) custom-call(f32[256]{0:T(256)S(1)} %copy-done.3, ...), custom_call_target="tpu_custom_call" | custom-call | flops 15728640 | bytes 10485760 | tf_op jit(solution)/shard_map/prepare/pallas_call | solution.py:265
  24.1 2.7 %reduced_terms.1 = (f32[32,16,128]{2,1,0:T(8,128)S(1)}, f32[32,16,128]{2,1,0:T(8,128)S(1)}, f32[32,16,128]{2,1,0:T(8,128)S(1)}, f32[32,16,128]{2,1,0:T(8,128)S(1...) custom-call(f32[256]{0:T(256)S(1)} %copy-done.3, f32[1,64]{1,0:T(1,128)S(1)} %bitcast.3, f32[64]{0:T(128)S(1)} %copy-done.5, ...), custom_call_target="tpu_custom_call" | custom-call | flops 20971520 | bytes 1572864 | tf_op jit(solution)/shard_map/reduced_terms/pallas_call | solution.py:336
  26.9 0.0 collective-permute-done.2.refs_3_
  26.9 0.0 collective-permute-done.3.refs_4_
  26.9 3.8 %collective-permute-done.4.refs_5_ = f32[8,64,128]{2,1,0:T(8,128)S(1)} collective-permute-done((f32[8,64,128]{2,1,0:T(8,128)S(1)}, f32[8,64,128]{2,1,0:T(8,128)S(1)}, u32[]{:S(2)}, u32[]{:S(2)}) %collective-permute-start.4) | collective-permute-done | bytes 262176 | tf_op jit(solution)/shard_map/ppermute | solution.py:30
  30.7 0.1 collective-permute-done.5.refs_6_
  30.8 0.0 collective-permute-done.6.refs_7_
  30.8 0.9 eliminate.1
  31.7 25.1 %all_to_all.10.g_ref = f32[32,2,16,128]{3,2,1,0:T(8,128)S(1)} all-to-all(f32[32,2,16,128]{3,2,1,0:T(8,128)S(1)} %get-tuple-element.64), channel_id=1, replica_groups=mesh['ta'=32,'gx'=8] {'ta'}, dimensions={0} | all-to-all | bytes 1048576 | tf_op jit(solution)/shard_map/all_to_all | solution.py:488
  56.8 0.3 interface_solve.1
  57.1 22.0 %all_to_all.11.ends_ref = f32[32,2,16,128]{3,2,1,0:T(8,128)S(1)} all-to-all(f32[32,2,16,128]{3,2,1,0:T(8,128)S(1)} %interface_solve.1), channel_id=1, replica_groups=mesh['ta'=32,'gx'=8] {'ta'}, dimensions={0} | all-to-all | bytes 1048576 | tf_op jit(solution)/shard_map/all_to_all | solution.py:490
  79.1 0.8 return_x.1
  79.9 2.9 %collective-permute-start.7 = (f32[8,64,128]{2,1,0:T(8,128)S(1)}, f32[8,64,128]{2,1,0:T(8,128)S(1)}, u32[]{:S(2)}, u32[]{:S(2)}) collective-permute-start(f32[8,64,128]{2,1,0:T(8,128)S(1)} %get-tuple-element.72), channel_id=1, source_target_pairs={{0,4},{1,5},{2,6},{3,7},{4,0},{5,1},{6,2},{7,3},{8,12},{9,13},{10,... | collective-permute-start | bytes 786440 | tf_op jit(solution)/shard_map/ppermute | solution.py:30
  82.8 4.4 %collective-permute-start.8 = (f32[8,64,128]{2,1,0:T(8,128)S(1)}, f32[8,64,128]{2,1,0:T(8,128)S(1)}, u32[]{:S(2)}, u32[]{:S(2)}) collective-permute-start(f32[8,64,128]{2,1,0:T(8,128)S(1)} %get-tuple-element.73), channel_id=1, source_target_pairs={{0,5},{1,4},{2,7},{3,6},{4,1},{5,0},{6,3},{7,2},{8,13},{9,12},{10,... | collective-permute-start | bytes 786440 | tf_op jit(solution)/shard_map/ppermute | solution.py:30
  87.2 1.2 %collective-permute-start.9 = (f32[8,64,128]{2,1,0:T(8,128)S(1)}, f32[8,64,128]{2,1,0:T(8,128)S(1)}, u32[]{:S(2)}, u32[]{:S(2)}) collective-permute-start(f32[8,64,128]{2,1,0:T(8,128)S(1)} %get-tuple-element.74), channel_id=1, source_target_pairs={{0,2},{1,3},{2,4},{3,5},{4,6},{5,7},{6,0},{7,1},{8,10},{9,11},{10,... | collective-permute-start | bytes 786440 | tf_op jit(solution)/shard_map/ppermute | solution.py:30
  88.4 1.5 %collective-permute-start.10 = (f32[8,64,128]{2,1,0:T(8,128)S(1)}, f32[8,64,128]{2,1,0:T(8,128)S(1)}, u32[]{:S(2)}, u32[]{:S(2)}) collective-permute-start(f32[8,64,128]{2,1,0:T(8,128)S(1)} %get-tuple-element.75), channel_id=1, source_target_pairs={{0,6},{1,7},{2,0},{3,1},{4,2},{5,3},{6,4},{7,5},{8,14},{9,15},{10,... | collective-permute-start | bytes 786440 | tf_op jit(solution)/shard_map/ppermute | solution.py:30
  89.8 0.0 collective-permute-start.11
  89.9 0.0 collective-permute-done.7.refs_1_
  89.9 6.5 %collective-permute-start.12 = (f32[8,64,128]{2,1,0:T(8,128)S(1)}, f32[8,64,128]{2,1,0:T(8,128)S(1)}, u32[]{:S(2)}, u32[]{:S(2)}) collective-permute-start(f32[8,64,128]{2,1,0:T(8,128)S(1)} %get-tuple-element.77), channel_id=1, source_target_pairs={{0,7},{1,6},{2,1},{3,0},{4,3},{5,2},{6,5},{7,4},{8,15},{9,14},{10,... | collective-permute-start | bytes 786440 | tf_op jit(solution)/shard_map/ppermute | solution.py:30
  96.3 0.8 collective-permute-done.8.refs_2_
  97.1 2.3 %collective-permute-start.13 = (f32[8,64,128]{2,1,0:T(8,128)S(1)}, f32[8,64,128]{2,1,0:T(8,128)S(1)}, u32[]{:S(2)}, u32[]{:S(2)}) collective-permute-start(f32[8,64,128]{2,1,0:T(8,128)S(1)} %get-tuple-element.78), channel_id=1, source_target_pairs={{0,1},{1,0},{2,3},{3,2},{4,5},{5,4},{6,7},{7,6},{8,9},{9,8},{10,11... | collective-permute-start | bytes 786440 | tf_op jit(solution)/shard_map/ppermute | solution.py:30
  99.5 3.3 %collective-permute-done.9.refs_3_ = f32[8,64,128]{2,1,0:T(8,128)S(1)} collective-permute-done((f32[8,64,128]{2,1,0:T(8,128)S(1)}, f32[8,64,128]{2,1,0:T(8,128)S(1)}, u32[]{:S(2)}, u32[]{:S(2)}) %collective-permute-start.9) | collective-permute-done | bytes 262176 | tf_op jit(solution)/shard_map/ppermute | solution.py:30
  102.7 1.5 %backward_yz.2.early_ref = f32[8,8,64,128]{3,2,1,0:T(8,128)S(1)} custom-call(bf16[64,96]{1,0:T(8,128)(2,1)S(1)} %get-tuple-element.44.by3_ref, bf16[384,128]{1,0:T(8,128)(2,1)S(1)} %get-tuple-element.43.bz3_ref, f32[8,64,128]{2,1,0:T(8,128)S(1)} %get-tuple-element.71.refs_0_, f32[8,64,128]{2,1,0:T(8,128)S(1)} %collective-permute-done.7.refs_1_, ...), custom_call_target="tpu_custom_call" | custom-call | flops 301989888 | bytes 4194304 | tf_op jit(solution)/shard_map/backward_yz/pallas_call | solution.py:179
  104.2 0.0 collective-permute-done.10.refs_0_
  104.2 4.1 %collective-permute-done.11.refs_1_ = f32[8,64,128]{2,1,0:T(8,128)S(1)} collective-permute-done((f32[8,64,128]{2,1,0:T(8,128)S(1)}, f32[8,64,128]{2,1,0:T(8,128)S(1)}, u32[]{:S(2)}, u32[]{:S(2)}) %collective-permute-start.11) | collective-permute-done | bytes 262176 | tf_op jit(solution)/shard_map/ppermute | solution.py:30
  108.3 0.0 collective-permute-done.12.refs_2_
  108.3 0.0 collective-permute-done.13.refs_3_
  108.3 2.4 %backward_yz.3 = f32[8,8,64,128]{3,2,1,0:T(8,128)} custom-call(bf16[64,96]{1,0:T(8,128)(2,1)S(1)} %get-tuple-element.42.by3_ref, bf16[384,128]{1,0:T(8,128)(2,1)S(1)} %get-tuple-element.43.bz3_ref, f32[8,8,64,128]{3,2,1,0:T(8,128)S(1)} %backward_yz.2.early_ref, f32[8,64,128]{2,1,0:T(8,128)S(1)} %collective-permute-done.10.refs_0_, ...), custom_call_target="tpu_custom_call" | custom-call | flops 301989888 | bytes 4194304 | tf_op jit(solution)/shard_map/backward_yz/pallas_call | solution.py:179
  (5 shorter events, 0.0 us)
Async XLA Ops:
  0.0 21.4 %copy-start = (f32[128,128]{1,0:T(8,128)S(1)}, f32[128,128]{1,0:T(8,128)}, u32[]{:S(2)}) copy-start(f32[128,128]{1,0:T(8,128)} %bz_any.3) | copy-start | bytes 196612
  0.0 21.4 %copy-start.1 = (f32[64,64]{1,0:T(8,128)S(1)}, f32[64,64]{1,0:T(8,128)}, u32[]{:S(2)}) copy-start(f32[64,64]{1,0:T(8,128)} %by_any.3) | copy-start | bytes 49156
  0.0 21.4 %copy-start.3 = (f32[256]{0:T(256)S(1)}, f32[256]{0:T(256)}, u32[]{:S(2)}) copy-start(f32[256]{0:T(256)} %steps_ref.3) | copy-start | bytes 3076
  0.0 21.4 %copy-start.5 = (f32[64]{0:T(128)S(1)}, f32[64]{0:T(128)}, u32[]{:S(2)}) copy-start(f32[64]{0:T(128)} %ey_ref.3) | copy-start | bytes 772
  0.0 21.4 %copy-start.6 = (f32[128]{0:T(128)S(1)}, f32[128]{0:T(128)}, u32[]{:S(2)}) copy-start(f32[128]{0:T(128)} %param.14) | copy-start | bytes 1540
  0.0 21.4 %copy-start.4 = (f32[64]{0:T(128)S(1)}, f32[64]{0:T(128)}, u32[]{:S(2)}) copy-start(f32[64]{0:T(128)} %param.12) | copy-start | bytes 772
  0.0 21.4 %copy-start.2 = (f32[64,64]{1,0:T(8,128)S(1)}, f32[64,64]{1,0:T(8,128)}, u32[]{:S(2)}) copy-start(f32[64,64]{1,0:T(8,128)} %bx_ref.1) | copy-start | bytes 49156
  3.1 12.2 %collective-permute-start = (f32[8,64,128]{2,1,0:T(8,128)S(1)}, f32[8,64,128]{2,1,0:T(8,128)S(1)}, u32[]{:S(2)}, u32[]{:S(2)}) collective-permute-start(f32[8,64,128]{2,1,0:T(8,128)S(1)} %get-tuple-element.56), channel_id=1, source_target_pairs={{0,4},{1,5},{2,6},{3,7},{4,0},{5,1},{6,2},{7,3},{8,12},{9,13},{10,... | collective-permute-start | bytes 786440 | tf_op jit(solution)/shard_map/ppermute | solution.py:30
  6.8 14.6 %collective-permute-start.1 = (f32[8,64,128]{2,1,0:T(8,128)S(1)}, f32[8,64,128]{2,1,0:T(8,128)S(1)}, u32[]{:S(2)}, u32[]{:S(2)}) collective-permute-start(f32[8,64,128]{2,1,0:T(8,128)S(1)} %get-tuple-element.57), channel_id=1, source_target_pairs={{0,5},{1,4},{2,7},{3,6},{4,1},{5,0},{6,3},{7,2},{8,13},{9,12},{10,... | collective-permute-start | bytes 786440 | tf_op jit(solution)/shard_map/ppermute | solution.py:30
  9.6 17.3 %collective-permute-start.2 = (f32[8,64,128]{2,1,0:T(8,128)S(1)}, f32[8,64,128]{2,1,0:T(8,128)S(1)}, u32[]{:S(2)}, u32[]{:S(2)}) collective-permute-start(f32[8,64,128]{2,1,0:T(8,128)S(1)} %get-tuple-element.58), channel_id=1, source_target_pairs={{0,2},{1,3},{2,4},{3,5},{4,6},{5,7},{6,0},{7,1},{8,10},{9,11},{10,... | collective-permute-start | bytes 786440 | tf_op jit(solution)/shard_map/ppermute | solution.py:30
  9.6 17.3 %collective-permute-start.3 = (f32[8,64,128]{2,1,0:T(8,128)S(1)}, f32[8,64,128]{2,1,0:T(8,128)S(1)}, u32[]{:S(2)}, u32[]{:S(2)}) collective-permute-start(f32[8,64,128]{2,1,0:T(8,128)S(1)} %get-tuple-element.59), channel_id=1, source_target_pairs={{0,6},{1,7},{2,0},{3,1},{4,2},{5,3},{6,4},{7,5},{8,14},{9,15},{10,... | collective-permute-start | bytes 786440 | tf_op jit(solution)/shard_map/ppermute | solution.py:30
  15.3 15.4 %collective-permute-start.4 = (f32[8,64,128]{2,1,0:T(8,128)S(1)}, f32[8,64,128]{2,1,0:T(8,128)S(1)}, u32[]{:S(2)}, u32[]{:S(2)}) collective-permute-start(f32[8,64,128]{2,1,0:T(8,128)S(1)} %get-tuple-element.60), channel_id=1, source_target_pairs={{0,3},{1,2},{2,5},{3,4},{4,7},{5,6},{6,1},{7,0},{8,11},{9,10},{10,... | collective-permute-start | bytes 786440 | tf_op jit(solution)/shard_map/ppermute | solution.py:30
  15.4 15.4 %collective-permute-start.5 = (f32[8,64,128]{2,1,0:T(8,128)S(1)}, f32[8,64,128]{2,1,0:T(8,128)S(1)}, u32[]{:S(2)}, u32[]{:S(2)}) collective-permute-start(f32[8,64,128]{2,1,0:T(8,128)S(1)} %get-tuple-element.61), channel_id=1, source_target_pairs={{0,7},{1,6},{2,1},{3,0},{4,3},{5,2},{6,5},{7,4},{8,15},{9,14},{10,... | collective-permute-start | bytes 786440 | tf_op jit(solution)/shard_map/ppermute | solution.py:30
  21.4 9.4 %collective-permute-start.6 = (f32[8,64,128]{2,1,0:T(8,128)S(1)}, f32[8,64,128]{2,1,0:T(8,128)S(1)}, u32[]{:S(2)}, u32[]{:S(2)}) collective-permute-start(f32[8,64,128]{2,1,0:T(8,128)S(1)} %get-tuple-element.62), channel_id=1, source_target_pairs={{0,1},{1,0},{2,3},{3,2},{4,5},{5,4},{6,7},{7,6},{8,9},{9,8},{10,11... | collective-permute-start | bytes 786440 | tf_op jit(solution)/shard_map/ppermute | solution.py:30
  79.9 9.9 %collective-permute-start.7 = (f32[8,64,128]{2,1,0:T(8,128)S(1)}, f32[8,64,128]{2,1,0:T(8,128)S(1)}, u32[]{:S(2)}, u32[]{:S(2)}) collective-permute-start(f32[8,64,128]{2,1,0:T(8,128)S(1)} %get-tuple-element.72), channel_id=1, source_target_pairs={{0,4},{1,5},{2,6},{3,7},{4,0},{5,1},{6,2},{7,3},{8,12},{9,13},{10,... | collective-permute-start | bytes 786440 | tf_op jit(solution)/shard_map/ppermute | solution.py:30
  82.8 14.4 %collective-permute-start.8 = (f32[8,64,128]{2,1,0:T(8,128)S(1)}, f32[8,64,128]{2,1,0:T(8,128)S(1)}, u32[]{:S(2)}, u32[]{:S(2)}) collective-permute-start(f32[8,64,128]{2,1,0:T(8,128)S(1)} %get-tuple-element.73), channel_id=1, source_target_pairs={{0,5},{1,4},{2,7},{3,6},{4,1},{5,0},{6,3},{7,2},{8,13},{9,12},{10,... | collective-permute-start | bytes 786440 | tf_op jit(solution)/shard_map/ppermute | solution.py:30
  87.2 15.5 %collective-permute-start.9 = (f32[8,64,128]{2,1,0:T(8,128)S(1)}, f32[8,64,128]{2,1,0:T(8,128)S(1)}, u32[]{:S(2)}, u32[]{:S(2)}) collective-permute-start(f32[8,64,128]{2,1,0:T(8,128)S(1)} %get-tuple-element.74), channel_id=1, source_target_pairs={{0,2},{1,3},{2,4},{3,5},{4,6},{5,7},{6,0},{7,1},{8,10},{9,11},{10,... | collective-permute-start | bytes 786440 | tf_op jit(solution)/shard_map/ppermute | solution.py:30
  88.4 15.8 %collective-permute-start.10 = (f32[8,64,128]{2,1,0:T(8,128)S(1)}, f32[8,64,128]{2,1,0:T(8,128)S(1)}, u32[]{:S(2)}, u32[]{:S(2)}) collective-permute-start(f32[8,64,128]{2,1,0:T(8,128)S(1)} %get-tuple-element.75), channel_id=1, source_target_pairs={{0,6},{1,7},{2,0},{3,1},{4,2},{5,3},{6,4},{7,5},{8,14},{9,15},{10,... | collective-permute-start | bytes 786440 | tf_op jit(solution)/shard_map/ppermute | solution.py:30
  89.8 18.5 %collective-permute-start.11 = (f32[8,64,128]{2,1,0:T(8,128)S(1)}, f32[8,64,128]{2,1,0:T(8,128)S(1)}, u32[]{:S(2)}, u32[]{:S(2)}) collective-permute-start(f32[8,64,128]{2,1,0:T(8,128)S(1)} %get-tuple-element.76), channel_id=1, source_target_pairs={{0,3},{1,2},{2,5},{3,4},{4,7},{5,6},{6,1},{7,0},{8,11},{9,10},{10,... | collective-permute-start | bytes 786440 | tf_op jit(solution)/shard_map/ppermute | solution.py:30
  89.9 18.5 %collective-permute-start.12 = (f32[8,64,128]{2,1,0:T(8,128)S(1)}, f32[8,64,128]{2,1,0:T(8,128)S(1)}, u32[]{:S(2)}, u32[]{:S(2)}) collective-permute-start(f32[8,64,128]{2,1,0:T(8,128)S(1)} %get-tuple-element.77), channel_id=1, source_target_pairs={{0,7},{1,6},{2,1},{3,0},{4,3},{5,2},{6,5},{7,4},{8,15},{9,14},{10,... | collective-permute-start | bytes 786440 | tf_op jit(solution)/shard_map/ppermute | solution.py:30
  97.1 11.2 %collective-permute-start.13 = (f32[8,64,128]{2,1,0:T(8,128)S(1)}, f32[8,64,128]{2,1,0:T(8,128)S(1)}, u32[]{:S(2)}, u32[]{:S(2)}) collective-permute-start(f32[8,64,128]{2,1,0:T(8,128)S(1)} %get-tuple-element.78), channel_id=1, source_target_pairs={{0,1},{1,0},{2,3},{3,2},{4,5},{5,4},{6,7},{7,6},{8,9},{9,8},{10,11... | collective-permute-start | bytes 786440 | tf_op jit(solution)/shard_map/ppermute | solution.py:30

commit v7 on v6

--- a/solution.py
+++ b/solution.py
@@ -59,6 +59,9 @@
 
 def array(*shape):
     return jax.ShapeDtypeStruct(shape, f32)
+
+
+FAR, NEAR = PEERS[1:5], PEERS[:1] + PEERS[5:]
 
 
 def gather_rows(source_ref, target_ref, peers, sign):
@@ -163,7 +166,9 @@
         times = (first, first + 1)
         for t, a, plane in backward_planes(times, rows, by3_ref, bz3_ref, pieces, mid_ref):
             out_ref[t, a] = early_ref[t, a] + plane
-        for t in times:
+        if first == 0:
+            continue
+        for t in range(0 if first == 2 else first, first + 2):
             copies.append(pltpu.make_async_copy(out_ref.at[t], out_any.at[t], sem.at[t]))
             copies[-1].start()
     for copy in copies:
@@ -210,17 +215,19 @@
 
 
 def prepare_body(steps_ref, ex_ref, ey_ref, ez_ref, bx_ref, by_ref, bz_ref, *refs):
-    inv_ref, mul_ref, ratio_ref, v_ref, w_ref, bx3_ref, bx3_back_ref, *by3_refs, bz3_ref = refs[:10]
-    sums_ref, turn_ref, rows_ref = refs[10:]
+    inv_ref, mul_ref, ratio_ref, v_ref, w_ref, bx3_ref, *more, bz3_ref = refs[:11]
+    bx3_back_refs, by3_refs = more[:2], more[2:]
+    sums_ref, turn_ref, rows_ref = refs[11:]
+    half = rows_ref.shape[0] // 2
     total, modes, lanes = inv_ref.shape
     x, members = ex_ref.shape[1], len(PEERS)
     gather_rows(bx_ref, rows_ref, PEERS, -1)
     bx3_ref[...] = left3(rows_ref[...].T)
-    gather_rows(bx_ref, rows_ref, PEERS, 1)
-    bx3_back_ref[...] = left3(rows_ref[...])
+    for peers, ref in zip((FAR, NEAR), bx3_back_refs):
+        gather_rows(bx_ref, rows_ref.at[:half], peers, 1)
+        ref[...] = left3(rows_ref[:half])
     turn_ref[...] = by_ref[...].T
     gather_rows(turn_ref, rows_ref, PEERS, -1)
-    half = rows_ref.shape[0] // 2
     for k, ref in enumerate(by3_refs):
         ref[...] = left3(rows_ref[k * half : (k + 1) * half].T)
     bz3_ref[...] = right3(bz_ref[...].T)
@@ -265,9 +272,10 @@
     return pl.pallas_call(
         prepare_body,
         in_specs=[SMEM, VMEM, SMEM, VMEM, VMEM, VMEM, VMEM],
-        out_specs=[VMEM] * 10,
+        out_specs=[VMEM] * 11,
         out_shape=[array(rows, modes, z)] * 5
-        + [table(x, 3 * x)] * 2
+        + [table(x, 3 * x)]
+        + [table(x // 2, 3 * x)] * 2
         + [table(y, 3 * y // 2)] * 2
         + [table(3 * z, z)],
         scratch_shapes=[
@@ -434,8 +442,8 @@
 
 def return_body(bx3_ref, v_ref, w_ref, g_ref, ends_ref, *outs):
     total, modes, lanes = g_ref.shape
-    x = bx3_ref.shape[0]
-    span = x // len(outs)
+    span = bx3_ref.shape[0] // len(outs)
+    x = bx3_ref.shape[1] // 3
     share = modes // ends_ref.shape[0]
     for j in range(modes // x):
         mine = slice(j * x, (j + 1) * x)
@@ -457,14 +465,14 @@
 
 def return_x(g, ends, bx3, v, w):
     t, modes, z = g.shape
-    x, members = bx3.shape[0], len(PEERS)
+    x, pieces = bx3.shape[1] // 3, len(PEERS) * 3 * bx3.shape[0] // bx3.shape[1]
     return pl.pallas_call(
         return_body,
         in_specs=[VMEM] * 5,
-        out_specs=[VMEM] * members,
-        out_shape=[array(t, modes // members, z)] * members,
-        compiler_params=params(),
-        cost_estimate=cost(6 * t * modes * x * z, 16 * t * modes * z),
+        out_specs=[VMEM] * pieces,
+        out_shape=[array(t, modes // len(PEERS), z)] * pieces,
+        compiler_params=params(),
+        cost_estimate=cost(6 * t * modes * bx3.shape[0] * z, 16 * t * modes * z),
         name="return_x",
     )(bx3, v, w, g, ends)
 
@@ -477,18 +485,19 @@
     hbm = lambda value: pltpu.with_memory_space_constraint(value, pltpu.HBM)
 
     given = (hbm(right_side), hbm(basis_y), hbm(basis_z))
-    far, near = PEERS[1:5], PEERS[:1] + PEERS[5:]
-    sent = forward_yz(*given, far)
-    rest = forward_yz(*given, near)
+    sent = forward_yz(*given, FAR)
+    rest = forward_yz(*given, NEAR)
     moved = exchange([rest[0], *sent, *rest[1:]])
     terms = list(reduced_terms(steps, sums, count, rows, share))
-    *factors, v, w, bx3, bx3_back, by3_early, by3_late, bz3 = prepare(steps, sums, basis_x, basis_y, basis_z, rows)
+    *factors, v, w, bx3, bx3_far, bx3_near, by3_early, by3_late, bz3 = prepare(steps, sums, basis_x, basis_y, basis_z, rows)
     moved[0], terms[0], bx3 = lax.optimization_barrier((moved[0], terms[0], bx3))
     g, ends = eliminate(moved, bx3, factors, count)
     ends = lax.all_to_all(ends, "ta", 0, 0, tiled=True)
     ends = interface_solve(ends, terms)
     ends = lax.all_to_all(ends, "ta", 0, 0, tiled=True)
-    moved = exchange(return_x(g, ends, bx3_back, v, w))
+    sent = return_x(g, ends, bx3_far, v, w)
+    rest = return_x(g, ends, bx3_near, v, w)
+    moved = exchange([rest[0], *sent, *rest[1:]])
     early = backward_yz(moved[:4], by3_early, bz3)
     return backward_yz(moved[4:], by3_late, bz3, (early,))
 

time: 111 us -> 111 us (level)
  transfers between devices with their start and end apart: 14 -> 14, of which waited for: 6 -> 6; matrix products, arithmetic and copies ran while one was open for 0% -> 0% of each run, Pallas kernels for 9% -> 10%
where the time goes in v7:
time: 111 us
  blocking collectives  47 us (42%)
  starting transfers between devices  30.1 us (27%)
  Pallas kernels  18.1 us (16%)
  waiting for transfers between devices  15.3 us (14%)
    all_to_all x2, blocking collectives, local(): ends = lax.all_to_all(ends, 'ta', 0, 0, tiled=True)  47 us
    ppermute x14, starting transfers between devices, send(): return lax.ppermute(piece, 'gx', pairs)  30.1 us
    ppermute x14, waiting for transfers between devices, send(): return lax.ppermute(piece, 'gx', pairs)  15.3 us
    pallas_call x2, Pallas kernels, forward_yz(): pl.pallas_call(partial(forward_body, peers), in_specs=[ANY] * 3, out_spec...  6.06 us
    pallas_call x2, Pallas kernels, backward_yz(): pl.pallas_call(backward_late_body if early else backward_early_body, in_s...  3.87 us
    pallas_call x1, Pallas kernels, reduced_terms(): pl.pallas_call(partial(reduced_body, rows), in_specs=[SMEM, VMEM, SMEM, V...  2.75 us
    pallas_call x1, Pallas kernels, prepare(): pl.pallas_call(prepare_body, in_specs=[SMEM, VMEM, SMEM, VMEM, VMEM, VMEM...  2.6 us
  transfers between devices with their start and end apart: 14, of which 6 were waited for; matrix products, arithmetic and copies ran while one was open for 0% of the time, Pallas kernels for 10%

profile of v7, /device:TPU:1, one launch (start us, length us, event | category | flops | bytes accessed | tf_op | source)
XLA Modules:
  0.0 110.8 jit_solution(15133801699029942675)
XLA Ops:
  0.0 0.0 copy-start.5
  0.0 0.0 copy-start.6
  0.0 0.0 copy-start.4
  0.0 3.1 %forward_yz.3 = (f32[8,64,128]{2,1,0:T(8,128)S(1)}, f32[8,64,128]{2,1,0:T(8,128)S(1)}, f32[8,64,128]{2,1,0:T(8,128)S(1)}, f32[8,64,128]{2,1,0:T(8,128)S(1)}) custom-call(f32[8,8,64,128]{3,2,1,0:T(8,128)} %x_any.3, f32[64,64]{1,0:T(8,128)} %by_any.3, f32[128,128]{1,0:T(8,128)} %bz_any.3), custom_call_target="tpu_custom_call" | custom-call | flops 301989888 | bytes 4194304 | tf_op jit(solution)/shard_map/forward_yz/pallas_call | solution.py:111
  3.1 3.7 %collective-permute-start = (f32[8,64,128]{2,1,0:T(8,128)S(1)}, f32[8,64,128]{2,1,0:T(8,128)S(1)}, u32[]{:S(2)}, u32[]{:S(2)}) collective-permute-start(f32[8,64,128]{2,1,0:T(8,128)S(1)} %get-tuple-element.57), channel_id=1, source_target_pairs={{0,4},{1,5},{2,6},{3,7},{4,0},{5,1},{6,2},{7,3},{8,12},{9,13},{10,... | collective-permute-start | bytes 786440 | tf_op jit(solution)/shard_map/ppermute | solution.py:30
  6.8 2.8 %collective-permute-start.1 = (f32[8,64,128]{2,1,0:T(8,128)S(1)}, f32[8,64,128]{2,1,0:T(8,128)S(1)}, u32[]{:S(2)}, u32[]{:S(2)}) collective-permute-start(f32[8,64,128]{2,1,0:T(8,128)S(1)} %get-tuple-element.58), channel_id=1, source_target_pairs={{0,5},{1,4},{2,7},{3,6},{4,1},{5,0},{6,3},{7,2},{8,13},{9,12},{10,... | collective-permute-start | bytes 786440 | tf_op jit(solution)/shard_map/ppermute | solution.py:30
  9.6 0.0 collective-permute-start.2
  9.6 2.7 %collective-permute-start.3 = (f32[8,64,128]{2,1,0:T(8,128)S(1)}, f32[8,64,128]{2,1,0:T(8,128)S(1)}, u32[]{:S(2)}, u32[]{:S(2)}) collective-permute-start(f32[8,64,128]{2,1,0:T(8,128)S(1)} %get-tuple-element.60), channel_id=1, source_target_pairs={{0,6},{1,7},{2,0},{3,1},{4,2},{5,3},{6,4},{7,5},{8,14},{9,15},{10,... | collective-permute-start | bytes 786440 | tf_op jit(solution)/shard_map/ppermute | solution.py:30
  12.3 3.0 %forward_yz.2 = (f32[8,64,128]{2,1,0:T(8,128)S(1)}, f32[8,64,128]{2,1,0:T(8,128)S(1)}, f32[8,64,128]{2,1,0:T(8,128)S(1)}, f32[8,64,128]{2,1,0:T(8,128)S(1)}) custom-call(f32[8,8,64,128]{3,2,1,0:T(8,128)} %x_any.3, f32[64,64]{1,0:T(8,128)} %by_any.3, f32[128,128]{1,0:T(8,128)} %bz_any.3), custom_call_target="tpu_custom_call" | custom-call | flops 301989888 | bytes 4194304 | tf_op jit(solution)/shard_map/forward_yz/pallas_call | solution.py:111
  15.3 0.1 collective-permute-start.4
  15.4 0.0 collective-permute-done.refs_1_
  15.4 2.9 %collective-permute-start.5 = (f32[8,64,128]{2,1,0:T(8,128)S(1)}, f32[8,64,128]{2,1,0:T(8,128)S(1)}, u32[]{:S(2)}, u32[]{:S(2)}) collective-permute-start(f32[8,64,128]{2,1,0:T(8,128)S(1)} %get-tuple-element.62), channel_id=1, source_target_pairs={{0,7},{1,6},{2,1},{3,0},{4,3},{5,2},{6,5},{7,4},{8,15},{9,14},{10,... | collective-permute-start | bytes 786440 | tf_op jit(solution)/shard_map/ppermute | solution.py:30
  18.3 3.1 %collective-permute-done.1.refs_2_ = f32[8,64,128]{2,1,0:T(8,128)S(1)} collective-permute-done((f32[8,64,128]{2,1,0:T(8,128)S(1)}, f32[8,64,128]{2,1,0:T(8,128)S(1)}, u32[]{:S(2)}, u32[]{:S(2)}) %collective-permute-start.1) | collective-permute-done | bytes 262176 | tf_op jit(solution)/shard_map/ppermute | solution.py:30
  21.4 0.0 collective-permute-start.6
  21.4 0.0 copy-done.3
  21.5 0.0 copy-done.5
  21.5 0.0 copy-done.6
  21.5 0.0 copy-done.4
  21.5 0.0 copy-done.2
  21.5 2.6 %prepare.1 = (f32[8,512,128]{2,1,0:T(8,128)S(1)}, f32[8,512,128]{2,1,0:T(8,128)S(1)}, f32[8,512,128]{2,1,0:T(8,128)S(1)}, f32[8,512,128]{2,1,0:T(8,128)S(1)}, f3...) custom-call(f32[256]{0:T(256)S(1)} %copy-done.3, ...), custom_call_target="tpu_custom_call" | custom-call | flops 15728640 | bytes 10485760 | tf_op jit(solution)/shard_map/prepare/pallas_call | solution.py:272
  24.1 2.7 %reduced_terms.1 = (f32[32,16,128]{2,1,0:T(8,128)S(1)}, f32[32,16,128]{2,1,0:T(8,128)S(1)}, f32[32,16,128]{2,1,0:T(8,128)S(1)}, f32[32,16,128]{2,1,0:T(8,128)S(1...) custom-call(f32[256]{0:T(256)S(1)} %copy-done.3, f32[1,64]{1,0:T(1,128)S(1)} %bitcast.3, f32[64]{0:T(128)S(1)} %copy-done.5, ...), custom_call_target="tpu_custom_call" | custom-call | flops 20971520 | bytes 1572864 | tf_op jit(solution)/shard_map/reduced_terms/pallas_call | solution.py:344
  26.9 0.0 collective-permute-done.2.refs_3_
  26.9 0.0 collective-permute-done.3.refs_4_
  26.9 3.8 %collective-permute-done.4.refs_5_ = f32[8,64,128]{2,1,0:T(8,128)S(1)} collective-permute-done((f32[8,64,128]{2,1,0:T(8,128)S(1)}, f32[8,64,128]{2,1,0:T(8,128)S(1)}, u32[]{:S(2)}, u32[]{:S(2)}) %collective-permute-start.4) | collective-permute-done | bytes 262176 | tf_op jit(solution)/shard_map/ppermute | solution.py:30
  30.7 0.1 collective-permute-done.5.refs_6_
  30.8 0.0 collective-permute-done.6.refs_7_
  30.8 0.9 eliminate.1
  31.7 25.1 %all_to_all.10.g_ref = f32[32,2,16,128]{3,2,1,0:T(8,128)S(1)} all-to-all(f32[32,2,16,128]{3,2,1,0:T(8,128)S(1)} %get-tuple-element.65), channel_id=1, replica_groups=mesh['ta'=32,'gx'=8] {'ta'}, dimensions={0} | all-to-all | bytes 1048576 | tf_op jit(solution)/shard_map/all_to_all | solution.py:495
  56.8 0.3 interface_solve.1
  57.1 22.0 %all_to_all.11.ends_ref = f32[32,2,16,128]{3,2,1,0:T(8,128)S(1)} all-to-all(f32[32,2,16,128]{3,2,1,0:T(8,128)S(1)} %interface_solve.1), channel_id=1, replica_groups=mesh['ta'=32,'gx'=8] {'ta'}, dimensions={0} | all-to-all | bytes 1048576 | tf_op jit(solution)/shard_map/all_to_all | solution.py:497
  79.1 0.8 return_x.3
  79.9 2.9 %collective-permute-start.7 = (f32[8,64,128]{2,1,0:T(8,128)S(1)}, f32[8,64,128]{2,1,0:T(8,128)S(1)}, u32[]{:S(2)}, u32[]{:S(2)}) collective-permute-start(f32[8,64,128]{2,1,0:T(8,128)S(1)} %get-tuple-element.74), channel_id=1, source_target_pairs={{0,4},{1,5},{2,6},{3,7},{4,0},{5,1},{6,2},{7,3},{8,12},{9,13},{10,... | collective-permute-start | bytes 786440 | tf_op jit(solution)/shard_map/ppermute | solution.py:30
  82.7 4.4 %collective-permute-start.8 = (f32[8,64,128]{2,1,0:T(8,128)S(1)}, f32[8,64,128]{2,1,0:T(8,128)S(1)}, u32[]{:S(2)}, u32[]{:S(2)}) collective-permute-start(f32[8,64,128]{2,1,0:T(8,128)S(1)} %get-tuple-element.75), channel_id=1, source_target_pairs={{0,5},{1,4},{2,7},{3,6},{4,1},{5,0},{6,3},{7,2},{8,13},{9,12},{10,... | collective-permute-start | bytes 786440 | tf_op jit(solution)/shard_map/ppermute | solution.py:30
  87.1 1.2 %collective-permute-start.9 = (f32[8,64,128]{2,1,0:T(8,128)S(1)}, f32[8,64,128]{2,1,0:T(8,128)S(1)}, u32[]{:S(2)}, u32[]{:S(2)}) collective-permute-start(f32[8,64,128]{2,1,0:T(8,128)S(1)} %get-tuple-element.76), channel_id=1, source_target_pairs={{0,2},{1,3},{2,4},{3,5},{4,6},{5,7},{6,0},{7,1},{8,10},{9,11},{10,... | collective-permute-start | bytes 786440 | tf_op jit(solution)/shard_map/ppermute | solution.py:30
  88.3 1.5 %collective-permute-start.10 = (f32[8,64,128]{2,1,0:T(8,128)S(1)}, f32[8,64,128]{2,1,0:T(8,128)S(1)}, u32[]{:S(2)}, u32[]{:S(2)}) collective-permute-start(f32[8,64,128]{2,1,0:T(8,128)S(1)} %get-tuple-element.77), channel_id=1, source_target_pairs={{0,6},{1,7},{2,0},{3,1},{4,2},{5,3},{6,4},{7,5},{8,14},{9,15},{10,... | collective-permute-start | bytes 786440 | tf_op jit(solution)/shard_map/ppermute | solution.py:30
  89.8 0.8 return_x.2
  90.5 0.1 collective-permute-start.11
  90.6 0.0 collective-permute-done.7.refs_1_
  90.6 5.6 %collective-permute-start.12 = (f32[8,64,128]{2,1,0:T(8,128)S(1)}, f32[8,64,128]{2,1,0:T(8,128)S(1)}, u32[]{:S(2)}, u32[]{:S(2)}) collective-permute-start(f32[8,64,128]{2,1,0:T(8,128)S(1)} %get-tuple-element.79), channel_id=1, source_target_pairs={{0,7},{1,6},{2,1},{3,0},{4,3},{5,2},{6,5},{7,4},{8,15},{9,14},{10,... | collective-permute-start | bytes 786440 | tf_op jit(solution)/shard_map/ppermute | solution.py:30
  96.2 0.8 collective-permute-done.8.refs_2_
  97.1 2.3 %collective-permute-start.13 = (f32[8,64,128]{2,1,0:T(8,128)S(1)}, f32[8,64,128]{2,1,0:T(8,128)S(1)}, u32[]{:S(2)}, u32[]{:S(2)}) collective-permute-start(f32[8,64,128]{2,1,0:T(8,128)S(1)} %get-tuple-element.80), channel_id=1, source_target_pairs={{0,1},{1,0},{2,3},{3,2},{4,5},{5,4},{6,7},{7,6},{8,9},{9,8},{10,11... | collective-permute-start | bytes 786440 | tf_op jit(solution)/shard_map/ppermute | solution.py:30
  99.4 3.3 %collective-permute-done.9.refs_3_ = f32[8,64,128]{2,1,0:T(8,128)S(1)} collective-permute-done((f32[8,64,128]{2,1,0:T(8,128)S(1)}, f32[8,64,128]{2,1,0:T(8,128)S(1)}, u32[]{:S(2)}, u32[]{:S(2)}) %collective-permute-start.9) | collective-permute-done | bytes 262176 | tf_op jit(solution)/shard_map/ppermute | solution.py:30
  102.6 1.5 %backward_yz.2.early_ref = f32[8,8,64,128]{3,2,1,0:T(8,128)S(1)} custom-call(bf16[64,96]{1,0:T(8,128)(2,1)S(1)} %get-tuple-element.45.by3_ref, bf16[384,128]{1,0:T(8,128)(2,1)S(1)} %get-tuple-element.44.bz3_ref, f32[8,64,128]{2,1,0:T(8,128)S(1)} %get-tuple-element.72.refs_0_, f32[8,64,128]{2,1,0:T(8,128)S(1)} %collective-permute-done.7.refs_1_, ...), custom_call_target="tpu_custom_call" | custom-call | flops 301989888 | bytes 4194304 | tf_op jit(solution)/shard_map/backward_yz/pallas_call | solution.py:184
  104.2 0.0 collective-permute-done.10.refs_0_
  104.2 4.1 %collective-permute-done.11.refs_1_ = f32[8,64,128]{2,1,0:T(8,128)S(1)} collective-permute-done((f32[8,64,128]{2,1,0:T(8,128)S(1)}, f32[8,64,128]{2,1,0:T(8,128)S(1)}, u32[]{:S(2)}, u32[]{:S(2)}) %collective-permute-start.11) | collective-permute-done | bytes 262176 | tf_op jit(solution)/shard_map/ppermute | solution.py:30
  108.3 0.0 collective-permute-done.12.refs_2_
  108.3 0.0 collective-permute-done.13.refs_3_
  108.3 2.4 %backward_yz.3 = f32[8,8,64,128]{3,2,1,0:T(8,128)} custom-call(bf16[64,96]{1,0:T(8,128)(2,1)S(1)} %get-tuple-element.43.by3_ref, bf16[384,128]{1,0:T(8,128)(2,1)S(1)} %get-tuple-element.44.bz3_ref, f32[8,8,64,128]{3,2,1,0:T(8,128)S(1)} %backward_yz.2.early_ref, f32[8,64,128]{2,1,0:T(8,128)S(1)} %collective-permute-done.10.refs_0_, ...), custom_call_target="tpu_custom_call" | custom-call | flops 301989888 | bytes 4194304 | tf_op jit(solution)/shard_map/backward_yz/pallas_call | solution.py:184
  (6 shorter events, 0.0 us)
Async XLA Ops:
  0.0 21.4 %copy-start = (f32[128,128]{1,0:T(8,128)S(1)}, f32[128,128]{1,0:T(8,128)}, u32[]{:S(2)}) copy-start(f32[128,128]{1,0:T(8,128)} %bz_any.3) | copy-start | bytes 196612
  0.0 21.4 %copy-start.1 = (f32[64,64]{1,0:T(8,128)S(1)}, f32[64,64]{1,0:T(8,128)}, u32[]{:S(2)}) copy-start(f32[64,64]{1,0:T(8,128)} %by_any.3) | copy-start | bytes 49156
  0.0 21.4 %copy-start.3 = (f32[256]{0:T(256)S(1)}, f32[256]{0:T(256)}, u32[]{:S(2)}) copy-start(f32[256]{0:T(256)} %steps_ref.3) | copy-start | bytes 3076
  0.0 21.4 %copy-start.5 = (f32[64]{0:T(128)S(1)}, f32[64]{0:T(128)}, u32[]{:S(2)}) copy-start(f32[64]{0:T(128)} %ey_ref.3) | copy-start | bytes 772
  0.0 21.4 %copy-start.6 = (f32[128]{0:T(128)S(1)}, f32[128]{0:T(128)}, u32[]{:S(2)}) copy-start(f32[128]{0:T(128)} %param.14) | copy-start | bytes 1540
  0.0 21.4 %copy-start.4 = (f32[64]{0:T(128)S(1)}, f32[64]{0:T(128)}, u32[]{:S(2)}) copy-start(f32[64]{0:T(128)} %param.12) | copy-start | bytes 772
  0.0 21.4 %copy-start.2 = (f32[64,64]{1,0:T(8,128)S(1)}, f32[64,64]{1,0:T(8,128)}, u32[]{:S(2)}) copy-start(f32[64,64]{1,0:T(8,128)} %bx_ref.1) | copy-start | bytes 49156
  3.1 12.2 %collective-permute-start = (f32[8,64,128]{2,1,0:T(8,128)S(1)}, f32[8,64,128]{2,1,0:T(8,128)S(1)}, u32[]{:S(2)}, u32[]{:S(2)}) collective-permute-start(f32[8,64,128]{2,1,0:T(8,128)S(1)} %get-tuple-element.57), channel_id=1, source_target_pairs={{0,4},{1,5},{2,6},{3,7},{4,0},{5,1},{6,2},{7,3},{8,12},{9,13},{10,... | collective-permute-start | bytes 786440 | tf_op jit(solution)/shard_map/ppermute | solution.py:30
  6.8 14.6 %collective-permute-start.1 = (f32[8,64,128]{2,1,0:T(8,128)S(1)}, f32[8,64,128]{2,1,0:T(8,128)S(1)}, u32[]{:S(2)}, u32[]{:S(2)}) collective-permute-start(f32[8,64,128]{2,1,0:T(8,128)S(1)} %get-tuple-element.58), channel_id=1, source_target_pairs={{0,5},{1,4},{2,7},{3,6},{4,1},{5,0},{6,3},{7,2},{8,13},{9,12},{10,... | collective-permute-start | bytes 786440 | tf_op jit(solution)/shard_map/ppermute | solution.py:30
  9.6 17.3 %collective-permute-start.2 = (f32[8,64,128]{2,1,0:T(8,128)S(1)}, f32[8,64,128]{2,1,0:T(8,128)S(1)}, u32[]{:S(2)}, u32[]{:S(2)}) collective-permute-start(f32[8,64,128]{2,1,0:T(8,128)S(1)} %get-tuple-element.59), channel_id=1, source_target_pairs={{0,2},{1,3},{2,4},{3,5},{4,6},{5,7},{6,0},{7,1},{8,10},{9,11},{10,... | collective-permute-start | bytes 786440 | tf_op jit(solution)/shard_map/ppermute | solution.py:30
  9.6 17.3 %collective-permute-start.3 = (f32[8,64,128]{2,1,0:T(8,128)S(1)}, f32[8,64,128]{2,1,0:T(8,128)S(1)}, u32[]{:S(2)}, u32[]{:S(2)}) collective-permute-start(f32[8,64,128]{2,1,0:T(8,128)S(1)} %get-tuple-element.60), channel_id=1, source_target_pairs={{0,6},{1,7},{2,0},{3,1},{4,2},{5,3},{6,4},{7,5},{8,14},{9,15},{10,... | collective-permute-start | bytes 786440 | tf_op jit(solution)/shard_map/ppermute | solution.py:30
  15.3 15.4 %collective-permute-start.4 = (f32[8,64,128]{2,1,0:T(8,128)S(1)}, f32[8,64,128]{2,1,0:T(8,128)S(1)}, u32[]{:S(2)}, u32[]{:S(2)}) collective-permute-start(f32[8,64,128]{2,1,0:T(8,128)S(1)} %get-tuple-element.61), channel_id=1, source_target_pairs={{0,3},{1,2},{2,5},{3,4},{4,7},{5,6},{6,1},{7,0},{8,11},{9,10},{10,... | collective-permute-start | bytes 786440 | tf_op jit(solution)/shard_map/ppermute | solution.py:30
  15.4 15.4 %collective-permute-start.5 = (f32[8,64,128]{2,1,0:T(8,128)S(1)}, f32[8,64,128]{2,1,0:T(8,128)S(1)}, u32[]{:S(2)}, u32[]{:S(2)}) collective-permute-start(f32[8,64,128]{2,1,0:T(8,128)S(1)} %get-tuple-element.62), channel_id=1, source_target_pairs={{0,7},{1,6},{2,1},{3,0},{4,3},{5,2},{6,5},{7,4},{8,15},{9,14},{10,... | collective-permute-start | bytes 786440 | tf_op jit(solution)/shard_map/ppermute | solution.py:30
  21.4 9.4 %collective-permute-start.6 = (f32[8,64,128]{2,1,0:T(8,128)S(1)}, f32[8,64,128]{2,1,0:T(8,128)S(1)}, u32[]{:S(2)}, u32[]{:S(2)}) collective-permute-start(f32[8,64,128]{2,1,0:T(8,128)S(1)} %get-tuple-element.63), channel_id=1, source_target_pairs={{0,1},{1,0},{2,3},{3,2},{4,5},{5,4},{6,7},{7,6},{8,9},{9,8},{10,11... | collective-permute-start | bytes 786440 | tf_op jit(solution)/shard_map/ppermute | solution.py:30
  79.9 10.8 %collective-permute-start.7 = (f32[8,64,128]{2,1,0:T(8,128)S(1)}, f32[8,64,128]{2,1,0:T(8,128)S(1)}, u32[]{:S(2)}, u32[]{:S(2)}) collective-permute-start(f32[8,64,128]{2,1,0:T(8,128)S(1)} %get-tuple-element.74), channel_id=1, source_target_pairs={{0,4},{1,5},{2,6},{3,7},{4,0},{5,1},{6,2},{7,3},{8,12},{9,13},{10,... | collective-permute-start | bytes 786440 | tf_op jit(solution)/shard_map/ppermute | solution.py:30
  82.7 14.4 %collective-permute-start.8 = (f32[8,64,128]{2,1,0:T(8,128)S(1)}, f32[8,64,128]{2,1,0:T(8,128)S(1)}, u32[]{:S(2)}, u32[]{:S(2)}) collective-permute-start(f32[8,64,128]{2,1,0:T(8,128)S(1)} %get-tuple-element.75), channel_id=1, source_target_pairs={{0,5},{1,4},{2,7},{3,6},{4,1},{5,0},{6,3},{7,2},{8,13},{9,12},{10,... | collective-permute-start | bytes 786440 | tf_op jit(solution)/shard_map/ppermute | solution.py:30
  87.1 15.5 %collective-permute-start.9 = (f32[8,64,128]{2,1,0:T(8,128)S(1)}, f32[8,64,128]{2,1,0:T(8,128)S(1)}, u32[]{:S(2)}, u32[]{:S(2)}) collective-permute-start(f32[8,64,128]{2,1,0:T(8,128)S(1)} %get-tuple-element.76), channel_id=1, source_target_pairs={{0,2},{1,3},{2,4},{3,5},{4,6},{5,7},{6,0},{7,1},{8,10},{9,11},{10,... | collective-permute-start | bytes 786440 | tf_op jit(solution)/shard_map/ppermute | solution.py:30
  88.3 15.8 %collective-permute-start.10 = (f32[8,64,128]{2,1,0:T(8,128)S(1)}, f32[8,64,128]{2,1,0:T(8,128)S(1)}, u32[]{:S(2)}, u32[]{:S(2)}) collective-permute-start(f32[8,64,128]{2,1,0:T(8,128)S(1)} %get-tuple-element.77), channel_id=1, source_target_pairs={{0,6},{1,7},{2,0},{3,1},{4,2},{5,3},{6,4},{7,5},{8,14},{9,15},{10,... | collective-permute-start | bytes 786440 | tf_op jit(solution)/shard_map/ppermute | solution.py:30
  90.5 17.7 %collective-permute-start.11 = (f32[8,64,128]{2,1,0:T(8,128)S(1)}, f32[8,64,128]{2,1,0:T(8,128)S(1)}, u32[]{:S(2)}, u32[]{:S(2)}) collective-permute-start(f32[8,64,128]{2,1,0:T(8,128)S(1)} %get-tuple-element.78), channel_id=1, source_target_pairs={{0,3},{1,2},{2,5},{3,4},{4,7},{5,6},{6,1},{7,0},{8,11},{9,10},{10,... | collective-permute-start | bytes 786440 | tf_op jit(solution)/shard_map/ppermute | solution.py:30
  90.6 17.6 %collective-permute-start.12 = (f32[8,64,128]{2,1,0:T(8,128)S(1)}, f32[8,64,128]{2,1,0:T(8,128)S(1)}, u32[]{:S(2)}, u32[]{:S(2)}) collective-permute-start(f32[8,64,128]{2,1,0:T(8,128)S(1)} %get-tuple-element.79), channel_id=1, source_target_pairs={{0,7},{1,6},{2,1},{3,0},{4,3},{5,2},{6,5},{7,4},{8,15},{9,14},{10,... | collective-permute-start | bytes 786440 | tf_op jit(solution)/shard_map/ppermute | solution.py:30
  97.1 11.2 %collective-permute-start.13 = (f32[8,64,128]{2,1,0:T(8,128)S(1)}, f32[8,64,128]{2,1,0:T(8,128)S(1)}, u32[]{:S(2)}, u32[]{:S(2)}) collective-permute-start(f32[8,64,128]{2,1,0:T(8,128)S(1)} %get-tuple-element.80), channel_id=1, source_target_pairs={{0,1},{1,0},{2,3},{3,2},{4,5},{5,4},{6,7},{7,6},{8,9},{9,8},{10,11... | collective-permute-start | bytes 786440 | tf_op jit(solution)/shard_map/ppermute | solution.py:30

commit v8 on v6

--- a/solution.py
+++ b/solution.py
@@ -355,7 +355,7 @@
         fh_ref[j] = a_ref[j] * first - k_ref[j] * before
         return (last + cl_ref[j] * first) - e_ref[j] * before
 
-    lax.fori_loop(0, count, down, zero, unroll=8)
+    lax.fori_loop(0, count, down, zero, unroll=32)
 
     def up(i, after):
         j = count - 1 - i
@@ -367,7 +367,7 @@
 
         return fh_ref[j] - b_ref[j] * after
 
-    lax.fori_loop(0, count, up, zero, unroll=8)
+    lax.fori_loop(0, count, up, zero, unroll=32)
 
 
 def interface_solve(g, terms):

time: 111 us -> 111 us (level)
  no operation moved by 1% of the time
where the time goes in v8:
time: 111 us
  blocking collectives  47 us (42%)
  starting transfers between devices  30.8 us (28%)
  Pallas kernels  17.1 us (15%)
  waiting for transfers between devices  15.3 us (14%)
    all_to_all x2, blocking collectives, local(): ends = lax.all_to_all(ends, 'ta', 0, 0, tiled=True)  47 us
    ppermute x14, starting transfers between devices, send(): return lax.ppermute(piece, 'gx', pairs)  30.8 us
    ppermute x14, waiting for transfers between devices, send(): return lax.ppermute(piece, 'gx', pairs)  15.3 us
    pallas_call x2, Pallas kernels, forward_yz(): pl.pallas_call(partial(forward_body, peers), in_specs=[ANY] * 3, out_spec...  6.06 us
    pallas_call x2, Pallas kernels, backward_yz(): pl.pallas_call(backward_late_body if early else backward_early_body, in_s...  3.87 us
    pallas_call x1, Pallas kernels, reduced_terms(): pl.pallas_call(partial(reduced_body, rows), in_specs=[SMEM, VMEM, SMEM, V...  2.75 us
    pallas_call x1, Pallas kernels, prepare(): pl.pallas_call(prepare_body, in_specs=[SMEM, VMEM, SMEM, VMEM, VMEM, VMEM...  2.59 us
  transfers between devices with their start and end apart: 14, of which 6 were waited for; matrix products, arithmetic and copies ran while one was open for 0% of the time, Pallas kernels for 9%

profile of v8, /device:TPU:1, one launch (start us, length us, event | category | flops | bytes accessed | tf_op | source)
XLA Modules:
  0.0 110.7 jit_solution(8977268058541749765)
XLA Ops:
  0.0 0.0 copy-start.5
  0.0 0.0 copy-start.6
  0.0 0.0 copy-start.4
  0.0 0.0 copy-start.2
  0.0 3.1 %forward_yz.3 = (f32[8,64,128]{2,1,0:T(8,128)S(1)}, f32[8,64,128]{2,1,0:T(8,128)S(1)}, f32[8,64,128]{2,1,0:T(8,128)S(1)}, f32[8,64,128]{2,1,0:T(8,128)S(1)}) custom-call(f32[8,8,64,128]{3,2,1,0:T(8,128)} %x_any.3, f32[64,64]{1,0:T(8,128)} %by_any.3, f32[128,128]{1,0:T(8,128)} %bz_any.3), custom_call_target="tpu_custom_call" | custom-call | flops 301989888 | bytes 4194304 | tf_op jit(solution)/shard_map/forward_yz/pallas_call | solution.py:108
  3.1 3.7 %collective-permute-start = (f32[8,64,128]{2,1,0:T(8,128)S(1)}, f32[8,64,128]{2,1,0:T(8,128)S(1)}, u32[]{:S(2)}, u32[]{:S(2)}) collective-permute-start(f32[8,64,128]{2,1,0:T(8,128)S(1)} %get-tuple-element.56), channel_id=1, source_target_pairs={{0,4},{1,5},{2,6},{3,7},{4,0},{5,1},{6,2},{7,3},{8,12},{9,13},{10,... | collective-permute-start | bytes 786440 | tf_op jit(solution)/shard_map/ppermute | solution.py:30
  6.8 2.8 %collective-permute-start.1 = (f32[8,64,128]{2,1,0:T(8,128)S(1)}, f32[8,64,128]{2,1,0:T(8,128)S(1)}, u32[]{:S(2)}, u32[]{:S(2)}) collective-permute-start(f32[8,64,128]{2,1,0:T(8,128)S(1)} %get-tuple-element.57), channel_id=1, source_target_pairs={{0,5},{1,4},{2,7},{3,6},{4,1},{5,0},{6,3},{7,2},{8,13},{9,12},{10,... | collective-permute-start | bytes 786440 | tf_op jit(solution)/shard_map/ppermute | solution.py:30
  9.6 0.0 collective-permute-start.2
  9.6 2.7 %collective-permute-start.3 = (f32[8,64,128]{2,1,0:T(8,128)S(1)}, f32[8,64,128]{2,1,0:T(8,128)S(1)}, u32[]{:S(2)}, u32[]{:S(2)}) collective-permute-start(f32[8,64,128]{2,1,0:T(8,128)S(1)} %get-tuple-element.59), channel_id=1, source_target_pairs={{0,6},{1,7},{2,0},{3,1},{4,2},{5,3},{6,4},{7,5},{8,14},{9,15},{10,... | collective-permute-start | bytes 786440 | tf_op jit(solution)/shard_map/ppermute | solution.py:30
  12.3 3.0 %forward_yz.2 = (f32[8,64,128]{2,1,0:T(8,128)S(1)}, f32[8,64,128]{2,1,0:T(8,128)S(1)}, f32[8,64,128]{2,1,0:T(8,128)S(1)}, f32[8,64,128]{2,1,0:T(8,128)S(1)}) custom-call(f32[8,8,64,128]{3,2,1,0:T(8,128)} %x_any.3, f32[64,64]{1,0:T(8,128)} %by_any.3, f32[128,128]{1,0:T(8,128)} %bz_any.3), custom_call_target="tpu_custom_call" | custom-call | flops 301989888 | bytes 4194304 | tf_op jit(solution)/shard_map/forward_yz/pallas_call | solution.py:108
  15.3 0.1 collective-permute-start.4
  15.4 0.0 collective-permute-done.refs_1_
  15.4 2.9 %collective-permute-start.5 = (f32[8,64,128]{2,1,0:T(8,128)S(1)}, f32[8,64,128]{2,1,0:T(8,128)S(1)}, u32[]{:S(2)}, u32[]{:S(2)}) collective-permute-start(f32[8,64,128]{2,1,0:T(8,128)S(1)} %get-tuple-element.61), channel_id=1, source_target_pairs={{0,7},{1,6},{2,1},{3,0},{4,3},{5,2},{6,5},{7,4},{8,15},{9,14},{10,... | collective-permute-start | bytes 786440 | tf_op jit(solution)/shard_map/ppermute | solution.py:30
  18.3 3.1 %collective-permute-done.1.refs_2_ = f32[8,64,128]{2,1,0:T(8,128)S(1)} collective-permute-done((f32[8,64,128]{2,1,0:T(8,128)S(1)}, f32[8,64,128]{2,1,0:T(8,128)S(1)}, u32[]{:S(2)}, u32[]{:S(2)}) %collective-permute-start.1) | collective-permute-done | bytes 262176 | tf_op jit(solution)/shard_map/ppermute | solution.py:30
  21.4 0.0 collective-permute-start.6
  21.4 0.0 copy-done
  21.4 0.0 copy-done.1
  21.4 0.0 copy-done.3
  21.5 0.0 copy-done.5
  21.5 0.0 copy-done.6
  21.5 2.6 %prepare.1 = (f32[8,512,128]{2,1,0:T(8,128)S(1)}, f32[8,512,128]{2,1,0:T(8,128)S(1)}, f32[8,512,128]{2,1,0:T(8,128)S(1)}, f32[8,512,128]{2,1,0:T(8,128)S(1)}, f3...) custom-call(f32[256]{0:T(256)S(1)} %copy-done.3, ...), custom_call_target="tpu_custom_call" | custom-call | flops 15728640 | bytes 10485760 | tf_op jit(solution)/shard_map/prepare/pallas_call | solution.py:265
  24.1 2.7 %reduced_terms.1 = (f32[32,16,128]{2,1,0:T(8,128)S(1)}, f32[32,16,128]{2,1,0:T(8,128)S(1)}, f32[32,16,128]{2,1,0:T(8,128)S(1)}, f32[32,16,128]{2,1,0:T(8,128)S(1...) custom-call(f32[256]{0:T(256)S(1)} %copy-done.3, f32[1,64]{1,0:T(1,128)S(1)} %bitcast.3, f32[64]{0:T(128)S(1)} %copy-done.5, ...), custom_call_target="tpu_custom_call" | custom-call | flops 20971520 | bytes 1572864 | tf_op jit(solution)/shard_map/reduced_terms/pallas_call | solution.py:336
  26.9 0.0 collective-permute-done.2.refs_3_
  26.9 0.0 collective-permute-done.3.refs_4_
  26.9 3.8 %collective-permute-done.4.refs_5_ = f32[8,64,128]{2,1,0:T(8,128)S(1)} collective-permute-done((f32[8,64,128]{2,1,0:T(8,128)S(1)}, f32[8,64,128]{2,1,0:T(8,128)S(1)}, u32[]{:S(2)}, u32[]{:S(2)}) %collective-permute-start.4) | collective-permute-done | bytes 262176 | tf_op jit(solution)/shard_map/ppermute | solution.py:30
  30.7 0.1 collective-permute-done.5.refs_6_
  30.8 0.0 collective-permute-done.6.refs_7_
  30.8 0.9 eliminate.1
  31.7 25.1 %all_to_all.10.g_ref = f32[32,2,16,128]{3,2,1,0:T(8,128)S(1)} all-to-all(f32[32,2,16,128]{3,2,1,0:T(8,128)S(1)} %get-tuple-element.64), channel_id=1, replica_groups=mesh['ta'=32,'gx'=8] {'ta'}, dimensions={0} | all-to-all | bytes 1048576 | tf_op jit(solution)/shard_map/all_to_all | solution.py:488
  56.8 0.1 interface_solve.1
  56.9 22.0 %all_to_all.11.ends_ref = f32[32,2,16,128]{3,2,1,0:T(8,128)S(1)} all-to-all(f32[32,2,16,128]{3,2,1,0:T(8,128)S(1)} %interface_solve.1), channel_id=1, replica_groups=mesh['ta'=32,'gx'=8] {'ta'}, dimensions={0} | all-to-all | bytes 1048576 | tf_op jit(solution)/shard_map/all_to_all | solution.py:490
  78.9 0.8 return_x.1
  79.7 2.9 %collective-permute-start.7 = (f32[8,64,128]{2,1,0:T(8,128)S(1)}, f32[8,64,128]{2,1,0:T(8,128)S(1)}, u32[]{:S(2)}, u32[]{:S(2)}) collective-permute-start(f32[8,64,128]{2,1,0:T(8,128)S(1)} %get-tuple-element.72), channel_id=1, source_target_pairs={{0,4},{1,5},{2,6},{3,7},{4,0},{5,1},{6,2},{7,3},{8,12},{9,13},{10,... | collective-permute-start | bytes 786440 | tf_op jit(solution)/shard_map/ppermute | solution.py:30
  82.6 4.4 %collective-permute-start.8 = (f32[8,64,128]{2,1,0:T(8,128)S(1)}, f32[8,64,128]{2,1,0:T(8,128)S(1)}, u32[]{:S(2)}, u32[]{:S(2)}) collective-permute-start(f32[8,64,128]{2,1,0:T(8,128)S(1)} %get-tuple-element.73), channel_id=1, source_target_pairs={{0,5},{1,4},{2,7},{3,6},{4,1},{5,0},{6,3},{7,2},{8,13},{9,12},{10,... | collective-permute-start | bytes 786440 | tf_op jit(solution)/shard_map/ppermute | solution.py:30
  87.0 1.2 %collective-permute-start.9 = (f32[8,64,128]{2,1,0:T(8,128)S(1)}, f32[8,64,128]{2,1,0:T(8,128)S(1)}, u32[]{:S(2)}, u32[]{:S(2)}) collective-permute-start(f32[8,64,128]{2,1,0:T(8,128)S(1)} %get-tuple-element.74), channel_id=1, source_target_pairs={{0,2},{1,3},{2,4},{3,5},{4,6},{5,7},{6,0},{7,1},{8,10},{9,11},{10,... | collective-permute-start | bytes 786440 | tf_op jit(solution)/shard_map/ppermute | solution.py:30
  88.2 1.5 %collective-permute-start.10 = (f32[8,64,128]{2,1,0:T(8,128)S(1)}, f32[8,64,128]{2,1,0:T(8,128)S(1)}, u32[]{:S(2)}, u32[]{:S(2)}) collective-permute-start(f32[8,64,128]{2,1,0:T(8,128)S(1)} %get-tuple-element.75), channel_id=1, source_target_pairs={{0,6},{1,7},{2,0},{3,1},{4,2},{5,3},{6,4},{7,5},{8,14},{9,15},{10,... | collective-permute-start | bytes 786440 | tf_op jit(solution)/shard_map/ppermute | solution.py:30
  89.6 0.0 collective-permute-start.11
  89.6 0.0 collective-permute-done.7.refs_1_
  89.6 6.4 %collective-permute-start.12 = (f32[8,64,128]{2,1,0:T(8,128)S(1)}, f32[8,64,128]{2,1,0:T(8,128)S(1)}, u32[]{:S(2)}, u32[]{:S(2)}) collective-permute-start(f32[8,64,128]{2,1,0:T(8,128)S(1)} %get-tuple-element.77), channel_id=1, source_target_pairs={{0,7},{1,6},{2,1},{3,0},{4,3},{5,2},{6,5},{7,4},{8,15},{9,14},{10,... | collective-permute-start | bytes 786440 | tf_op jit(solution)/shard_map/ppermute | solution.py:30
  96.1 0.8 collective-permute-done.8.refs_2_
  96.9 2.3 %collective-permute-start.13 = (f32[8,64,128]{2,1,0:T(8,128)S(1)}, f32[8,64,128]{2,1,0:T(8,128)S(1)}, u32[]{:S(2)}, u32[]{:S(2)}) collective-permute-start(f32[8,64,128]{2,1,0:T(8,128)S(1)} %get-tuple-element.78), channel_id=1, source_target_pairs={{0,1},{1,0},{2,3},{3,2},{4,5},{5,4},{6,7},{7,6},{8,9},{9,8},{10,11... | collective-permute-start | bytes 786440 | tf_op jit(solution)/shard_map/ppermute | solution.py:30
  99.2 3.3 %collective-permute-done.9.refs_3_ = f32[8,64,128]{2,1,0:T(8,128)S(1)} collective-permute-done((f32[8,64,128]{2,1,0:T(8,128)S(1)}, f32[8,64,128]{2,1,0:T(8,128)S(1)}, u32[]{:S(2)}, u32[]{:S(2)}) %collective-permute-start.9) | collective-permute-done | bytes 262176 | tf_op jit(solution)/shard_map/ppermute | solution.py:30
  102.5 1.5 %backward_yz.2.early_ref = f32[8,8,64,128]{3,2,1,0:T(8,128)S(1)} custom-call(bf16[64,96]{1,0:T(8,128)(2,1)S(1)} %get-tuple-element.44.by3_ref, bf16[384,128]{1,0:T(8,128)(2,1)S(1)} %get-tuple-element.43.bz3_ref, f32[8,64,128]{2,1,0:T(8,128)S(1)} %get-tuple-element.71.refs_0_, f32[8,64,128]{2,1,0:T(8,128)S(1)} %collective-permute-done.7.refs_1_, ...), custom_call_target="tpu_custom_call" | custom-call | flops 301989888 | bytes 4194304 | tf_op jit(solution)/shard_map/backward_yz/pallas_call | solution.py:179
  104.0 0.0 collective-permute-done.10.refs_0_
  104.0 4.1 %collective-permute-done.11.refs_1_ = f32[8,64,128]{2,1,0:T(8,128)S(1)} collective-permute-done((f32[8,64,128]{2,1,0:T(8,128)S(1)}, f32[8,64,128]{2,1,0:T(8,128)S(1)}, u32[]{:S(2)}, u32[]{:S(2)}) %collective-permute-start.11) | collective-permute-done | bytes 262176 | tf_op jit(solution)/shard_map/ppermute | solution.py:30
  108.1 0.0 collective-permute-done.12.refs_2_
  108.1 0.0 collective-permute-done.13.refs_3_
  108.1 2.4 %backward_yz.3 = f32[8,8,64,128]{3,2,1,0:T(8,128)} custom-call(bf16[64,96]{1,0:T(8,128)(2,1)S(1)} %get-tuple-element.42.by3_ref, bf16[384,128]{1,0:T(8,128)(2,1)S(1)} %get-tuple-element.43.bz3_ref, f32[8,8,64,128]{3,2,1,0:T(8,128)S(1)} %backward_yz.2.early_ref, f32[8,64,128]{2,1,0:T(8,128)S(1)} %collective-permute-done.10.refs_0_, ...), custom_call_target="tpu_custom_call" | custom-call | flops 301989888 | bytes 4194304 | tf_op jit(solution)/shard_map/backward_yz/pallas_call | solution.py:179
  (5 shorter events, 0.0 us)
Async XLA Ops:
  0.0 21.4 %copy-start = (f32[128,128]{1,0:T(8,128)S(1)}, f32[128,128]{1,0:T(8,128)}, u32[]{:S(2)}) copy-start(f32[128,128]{1,0:T(8,128)} %bz_any.3) | copy-start | bytes 196612
  0.0 21.4 %copy-start.1 = (f32[64,64]{1,0:T(8,128)S(1)}, f32[64,64]{1,0:T(8,128)}, u32[]{:S(2)}) copy-start(f32[64,64]{1,0:T(8,128)} %by_any.3) | copy-start | bytes 49156
  0.0 21.4 %copy-start.3 = (f32[256]{0:T(256)S(1)}, f32[256]{0:T(256)}, u32[]{:S(2)}) copy-start(f32[256]{0:T(256)} %steps_ref.3) | copy-start | bytes 3076
  0.0 21.4 %copy-start.5 = (f32[64]{0:T(128)S(1)}, f32[64]{0:T(128)}, u32[]{:S(2)}) copy-start(f32[64]{0:T(128)} %ey_ref.3) | copy-start | bytes 772
  0.0 21.4 %copy-start.6 = (f32[128]{0:T(128)S(1)}, f32[128]{0:T(128)}, u32[]{:S(2)}) copy-start(f32[128]{0:T(128)} %param.14) | copy-start | bytes 1540
  0.0 21.4 %copy-start.4 = (f32[64]{0:T(128)S(1)}, f32[64]{0:T(128)}, u32[]{:S(2)}) copy-start(f32[64]{0:T(128)} %param.12) | copy-start | bytes 772
  0.0 21.4 %copy-start.2 = (f32[64,64]{1,0:T(8,128)S(1)}, f32[64,64]{1,0:T(8,128)}, u32[]{:S(2)}) copy-start(f32[64,64]{1,0:T(8,128)} %bx_ref.1) | copy-start | bytes 49156
  3.1 12.2 %collective-permute-start = (f32[8,64,128]{2,1,0:T(8,128)S(1)}, f32[8,64,128]{2,1,0:T(8,128)S(1)}, u32[]{:S(2)}, u32[]{:S(2)}) collective-permute-start(f32[8,64,128]{2,1,0:T(8,128)S(1)} %get-tuple-element.56), channel_id=1, source_target_pairs={{0,4},{1,5},{2,6},{3,7},{4,0},{5,1},{6,2},{7,3},{8,12},{9,13},{10,... | collective-permute-start | bytes 786440 | tf_op jit(solution)/shard_map/ppermute | solution.py:30
  6.8 14.6 %collective-permute-start.1 = (f32[8,64,128]{2,1,0:T(8,128)S(1)}, f32[8,64,128]{2,1,0:T(8,128)S(1)}, u32[]{:S(2)}, u32[]{:S(2)}) collective-permute-start(f32[8,64,128]{2,1,0:T(8,128)S(1)} %get-tuple-element.57), channel_id=1, source_target_pairs={{0,5},{1,4},{2,7},{3,6},{4,1},{5,0},{6,3},{7,2},{8,13},{9,12},{10,... | collective-permute-start | bytes 786440 | tf_op jit(solution)/shard_map/ppermute | solution.py:30
  9.6 17.3 %collective-permute-start.2 = (f32[8,64,128]{2,1,0:T(8,128)S(1)}, f32[8,64,128]{2,1,0:T(8,128)S(1)}, u32[]{:S(2)}, u32[]{:S(2)}) collective-permute-start(f32[8,64,128]{2,1,0:T(8,128)S(1)} %get-tuple-element.58), channel_id=1, source_target_pairs={{0,2},{1,3},{2,4},{3,5},{4,6},{5,7},{6,0},{7,1},{8,10},{9,11},{10,... | collective-permute-start | bytes 786440 | tf_op jit(solution)/shard_map/ppermute | solution.py:30
  9.6 17.3 %collective-permute-start.3 = (f32[8,64,128]{2,1,0:T(8,128)S(1)}, f32[8,64,128]{2,1,0:T(8,128)S(1)}, u32[]{:S(2)}, u32[]{:S(2)}) collective-permute-start(f32[8,64,128]{2,1,0:T(8,128)S(1)} %get-tuple-element.59), channel_id=1, source_target_pairs={{0,6},{1,7},{2,0},{3,1},{4,2},{5,3},{6,4},{7,5},{8,14},{9,15},{10,... | collective-permute-start | bytes 786440 | tf_op jit(solution)/shard_map/ppermute | solution.py:30
  15.3 15.4 %collective-permute-start.4 = (f32[8,64,128]{2,1,0:T(8,128)S(1)}, f32[8,64,128]{2,1,0:T(8,128)S(1)}, u32[]{:S(2)}, u32[]{:S(2)}) collective-permute-start(f32[8,64,128]{2,1,0:T(8,128)S(1)} %get-tuple-element.60), channel_id=1, source_target_pairs={{0,3},{1,2},{2,5},{3,4},{4,7},{5,6},{6,1},{7,0},{8,11},{9,10},{10,... | collective-permute-start | bytes 786440 | tf_op jit(solution)/shard_map/ppermute | solution.py:30
  15.4 15.4 %collective-permute-start.5 = (f32[8,64,128]{2,1,0:T(8,128)S(1)}, f32[8,64,128]{2,1,0:T(8,128)S(1)}, u32[]{:S(2)}, u32[]{:S(2)}) collective-permute-start(f32[8,64,128]{2,1,0:T(8,128)S(1)} %get-tuple-element.61), channel_id=1, source_target_pairs={{0,7},{1,6},{2,1},{3,0},{4,3},{5,2},{6,5},{7,4},{8,15},{9,14},{10,... | collective-permute-start | bytes 786440 | tf_op jit(solution)/shard_map/ppermute | solution.py:30
  21.4 9.4 %collective-permute-start.6 = (f32[8,64,128]{2,1,0:T(8,128)S(1)}, f32[8,64,128]{2,1,0:T(8,128)S(1)}, u32[]{:S(2)}, u32[]{:S(2)}) collective-permute-start(f32[8,64,128]{2,1,0:T(8,128)S(1)} %get-tuple-element.62), channel_id=1, source_target_pairs={{0,1},{1,0},{2,3},{3,2},{4,5},{5,4},{6,7},{7,6},{8,9},{9,8},{10,11... | collective-permute-start | bytes 786440 | tf_op jit(solution)/shard_map/ppermute | solution.py:30
  79.7 9.9 %collective-permute-start.7 = (f32[8,64,128]{2,1,0:T(8,128)S(1)}, f32[8,64,128]{2,1,0:T(8,128)S(1)}, u32[]{:S(2)}, u32[]{:S(2)}) collective-permute-start(f32[8,64,128]{2,1,0:T(8,128)S(1)} %get-tuple-element.72), channel_id=1, source_target_pairs={{0,4},{1,5},{2,6},{3,7},{4,0},{5,1},{6,2},{7,3},{8,12},{9,13},{10,... | collective-permute-start | bytes 786440 | tf_op jit(solution)/shard_map/ppermute | solution.py:30
  82.6 14.4 %collective-permute-start.8 = (f32[8,64,128]{2,1,0:T(8,128)S(1)}, f32[8,64,128]{2,1,0:T(8,128)S(1)}, u32[]{:S(2)}, u32[]{:S(2)}) collective-permute-start(f32[8,64,128]{2,1,0:T(8,128)S(1)} %get-tuple-element.73), channel_id=1, source_target_pairs={{0,5},{1,4},{2,7},{3,6},{4,1},{5,0},{6,3},{7,2},{8,13},{9,12},{10,... | collective-permute-start | bytes 786440 | tf_op jit(solution)/shard_map/ppermute | solution.py:30
  87.0 15.5 %collective-permute-start.9 = (f32[8,64,128]{2,1,0:T(8,128)S(1)}, f32[8,64,128]{2,1,0:T(8,128)S(1)}, u32[]{:S(2)}, u32[]{:S(2)}) collective-permute-start(f32[8,64,128]{2,1,0:T(8,128)S(1)} %get-tuple-element.74), channel_id=1, source_target_pairs={{0,2},{1,3},{2,4},{3,5},{4,6},{5,7},{6,0},{7,1},{8,10},{9,11},{10,... | collective-permute-start | bytes 786440 | tf_op jit(solution)/shard_map/ppermute | solution.py:30
  88.2 15.8 %collective-permute-start.10 = (f32[8,64,128]{2,1,0:T(8,128)S(1)}, f32[8,64,128]{2,1,0:T(8,128)S(1)}, u32[]{:S(2)}, u32[]{:S(2)}) collective-permute-start(f32[8,64,128]{2,1,0:T(8,128)S(1)} %get-tuple-element.75), channel_id=1, source_target_pairs={{0,6},{1,7},{2,0},{3,1},{4,2},{5,3},{6,4},{7,5},{8,14},{9,15},{10,... | collective-permute-start | bytes 786440 | tf_op jit(solution)/shard_map/ppermute | solution.py:30
  89.6 18.5 %collective-permute-start.11 = (f32[8,64,128]{2,1,0:T(8,128)S(1)}, f32[8,64,128]{2,1,0:T(8,128)S(1)}, u32[]{:S(2)}, u32[]{:S(2)}) collective-permute-start(f32[8,64,128]{2,1,0:T(8,128)S(1)} %get-tuple-element.76), channel_id=1, source_target_pairs={{0,3},{1,2},{2,5},{3,4},{4,7},{5,6},{6,1},{7,0},{8,11},{9,10},{10,... | collective-permute-start | bytes 786440 | tf_op jit(solution)/shard_map/ppermute | solution.py:30
  89.6 18.5 %collective-permute-start.12 = (f32[8,64,128]{2,1,0:T(8,128)S(1)}, f32[8,64,128]{2,1,0:T(8,128)S(1)}, u32[]{:S(2)}, u32[]{:S(2)}) collective-permute-start(f32[8,64,128]{2,1,0:T(8,128)S(1)} %get-tuple-element.77), channel_id=1, source_target_pairs={{0,7},{1,6},{2,1},{3,0},{4,3},{5,2},{6,5},{7,4},{8,15},{9,14},{10,... | collective-permute-start | bytes 786440 | tf_op jit(solution)/shard_map/ppermute | solution.py:30
  96.9 11.2 %collective-permute-start.13 = (f32[8,64,128]{2,1,0:T(8,128)S(1)}, f32[8,64,128]{2,1,0:T(8,128)S(1)}, u32[]{:S(2)}, u32[]{:S(2)}) collective-permute-start(f32[8,64,128]{2,1,0:T(8,128)S(1)} %get-tuple-element.78), channel_id=1, source_target_pairs={{0,1},{1,0},{2,3},{3,2},{4,5},{5,4},{6,7},{7,6},{8,9},{9,8},{10,11... | collective-permute-start | bytes 786440 | tf_op jit(solution)/shard_map/ppermute | solution.py:30
